TPU v7x, 128 devices: a whole 4x4x4 slice. The times are simulated.
128 devices in a mesh: gx: 32 (over y_lo, x, z), gy: 4 (over y_hi, core).
Axes of the slice: x: 4, y: 4 (y_hi: 2, y_lo: 2; y = y_hi * 2 + y_lo), z: 4, core: 2. Of those that a mesh axis runs over, the one named last changes fastest.
Arguments:
- orbitals: float32 [32, 256, 32, 128], P(None, 'gx', 'gy'), may hold values from -340 to 340
- potential: float32 [256, 32, 128], P('gx', 'gy'), may hold values from -3 to 1
Outputs:
- orthonormal: float32 [32, 256, 32, 128], P(None, 'gx', 'gy')
- rfactor: float32 [32, 32], replicated
All inputs are finite; a program needn't handle non-finite values.
Results may differ from a plain program's by a relative error of at most 0.0003.
Values sent between devices are 32-bit elements; how exact they have to be, the bound alone decides.
No kernel may reach another device: no remote copies, remote signals or barrier semaphores. Data moves between devices by JAX's collectives and lax.ppermute only.
A program may use at most 128 MiB of HBM per device.

v0:
```python
import jax
import jax.numpy as jnp
from jax import lax
from jax.sharding import PartitionSpec as P

DEGREE = 3


stencil_weights = (
    -5369.0 / 1800.0,
    12.0 / 7.0,
    -15.0 / 56.0,
    10.0 / 189.0,
    -1.0 / 112.0,
    2.0 / 1925.0,
    -1.0 / 16632.0,
)
grid_spacing = 0.5
filter_low = 4.0
filter_high = 46.0
highest = lax.Precision.HIGHEST


def extended(block, sides, width):
    for axis, dim in sides:
        count = lax.axis_size(axis)
        forward = [(i, i + 1) for i in range(count - 1)]
        forward.append((count - 1, 0))
        backward = [(target, source) for source, target in forward]
        low = lax.ppermute(
            lax.slice_in_dim(block, block.shape[dim] - width, None, axis=dim), axis, forward
        )
        high = lax.ppermute(lax.slice_in_dim(block, 0, width, axis=dim), axis, backward)
        block = jnp.concatenate([low, block, high], axis=dim)
    return block


def from_partner(block, axis, stride):
    count = lax.axis_size(axis)
    route = []
    for low in range(count):
        high = low | 1 << stride
        if high != low and high < count:
            route += [(low, high), (high, low)]
    return lax.ppermute(block, axis, route)


def line_sum(padded, axis_pos, extent):
    running = None
    for offset in range(1, 7):
        forward = lax.slice_in_dim(padded, 6 + offset, 6 + offset + extent, axis=axis_pos)
        behind = lax.slice_in_dim(padded, 6 - offset, 6 - offset + extent, axis=axis_pos)
        weighted = stencil_weights[offset] * (forward + behind)
        running = weighted if running is None else running + weighted
    return running


def rolled_sum(centre, axis_pos):
    running = None
    for offset in range(1, 7):
        weighted = stencil_weights[offset] * (
            jnp.roll(centre, offset, axis_pos) + jnp.roll(centre, -offset, axis_pos)
        )
        running = weighted if running is None else running + weighted
    return running


def finish_apply(current, laplace, potential):
    applied = -0.5 / grid_spacing**2 * laplace + potential[None] * current
    centre_shift = 0.5 * (filter_high + filter_low)
    half_width = 0.5 * (filter_high - filter_low)
    return (applied - centre_shift * current) / half_width


def scaled_apply(current, potential):
    extent_x = current.shape[1]
    extent_y = current.shape[2]
    padded = extended(current, (("gx", 1), ("gy", 2)), 6)
    across_x = line_sum(padded[:, :, 6 : 6 + extent_y], 1, extent_x)
    across_y = line_sum(padded[:, 6 : 6 + extent_x, :], 2, extent_y)
    laplace = 3.0 * stencil_weights[0] * current + across_x + across_y + rolled_sum(current, 3)
    return finish_apply(current, laplace, potential)


def run_filter(start, potential, apply_fn):
    previous = start
    current = apply_fn(start, potential)
    for degree_step in range(DEGREE - 1):
        following = 2.0 * apply_fn(current, potential) - previous
        previous, current = (current, following)
    return current


def local_pass(matrix_rows, total_cells):
    gram_local = jnp.dot(matrix_rows, matrix_rows.T, precision=highest) / total_cells
    lower_factor = jnp.linalg.cholesky(gram_local)
    return (jax.scipy.linalg.solve_triangular(lower_factor, matrix_rows, lower=True), lower_factor)


def combine_level(triangle, partner):
    joined = jnp.dot(triangle.T, triangle, precision=highest) + jnp.dot(
        partner.T, partner, precision=highest
    )
    return jnp.triu(jnp.linalg.cholesky(joined).T)


def per_device(orbitals, potential):
    current = run_filter(orbitals, potential, scaled_apply)
    orbital_count = current.shape[0]
    matrix_rows = current.reshape(orbital_count, -1)
    total_cells = float(matrix_rows.shape[1] * lax.axis_size("gx") * lax.axis_size("gy"))
    first_rows, first_lower = local_pass(matrix_rows, total_cells)
    local_rows, second_lower = local_pass(first_rows, total_cells)
    lower_local = jnp.dot(first_lower, second_lower, precision=highest)
    triangle = lower_local.T
    for bit_place in range(lax.axis_size("gx").bit_length() - 1):
        partner = from_partner(triangle, "gx", bit_place)
        triangle = combine_level(triangle, partner)
    for bit_place in range(lax.axis_size("gy").bit_length() - 1):
        partner = from_partner(triangle, "gy", bit_place)
        triangle = combine_level(triangle, partner)
    mixer = jax.scipy.linalg.solve_triangular(triangle.T, lower_local, lower=True)
    final_rows = jnp.dot(mixer, local_rows, precision=highest)
    return (final_rows.reshape(current.shape), triangle)


def solution(mesh):
    return jax.shard_map(
        per_device,
        mesh=mesh,
        in_specs=(P(None, "gx", "gy", None), P("gx", "gy", None)),
        out_specs=(P(None, "gx", "gy", None), P()),
        check_vma=False,
    )
```

profile of v0, /device:TPU:1, one launch (start us, length us, event | category | flops | bytes accessed | tf_op | source)
XLA Modules:
  0.0 380.4 jit_solution(13855069605671639176)
XLA Ops:
  2.5 2.5 collective-permute-start.1
  5.3 5.4 %collective-permute-start = (f32[32,6,8,128]{3,0,2,1:T(8,128)S(1)}, f32[32,6,8,128]{3,0,2,1:T(8,128)S(1)}, u32[]{:S(2)}, u32[]{:S(2)}) collective-permute-start(f32[32,6,8,128]{3,0,2,1:T(8,128)S(1)} %copy.234), channel_id=1, source_target_pairs={{4,0},{8,4},{12,8},{16,12},{20,16},{24,20},{28,24},{32,28},{36,32}... | collective-permute-start | bytes 2359304 | tf_op jit(solution)/shard_map/ppermute | solution.py:33
  12.9 14.7 %collective-permute-done.1 = f32[32,6,8,128]{3,0,2,1:T(8,128)S(1)} collective-permute-done((f32[32,6,8,128]{3,0,2,1:T(8,128)S(1)}, f32[32,6,8,128]{3,0,2,1:T(8,128)S(1)}, u32[]{:S(2)}, u32[]{:S(2)}) %collective-permute-start.1) | collective-permute-done | bytes 786464 | tf_op jit(solution)/shard_map/ppermute | solution.py:30
  28.7 2.0 constant_dynamic-update-slice_fusion.1
  34.6 2.7 collective-permute-start.3
  80.6 20.8 %broadcast_multiply_fusion = (f32[32,8,8,128]{3,0,2,1:T(8,128)S(1)}, f32[32,8,8,128]{3,0,2,1:T(8,128)}) fusion(f32[8,8,128]{2,1,0:T(8,128)S(1)} %copy-done.9, f32[32,8,8,6]{3,0,2,1:T(8,128)} %copy.257, f32[32,8,8,122]{3,0,2,1:T(8,128)} %copy.258, f32[32,8,8,122]{3,0,2,1:T(8,128)} %copy.255, f32[32,8,8,6]{3,0,2,1:T(8,128)} %copy.256, ...), kind=kLoop, calls=%fused_computation.291 | loop fusion | flops 22282240 | bytes 34897920 | tf_op jit(solution)/shard_map/div | solution.py:72
  104.9 2.7 collective-permute-start.4
  109.4 1.8 fusion.233
  111.2 1.7 fusion.234
  113.0 9.9 %collective-permute-done.4 = f32[32,6,8,128]{3,0,2,1:T(8,128)S(1)} collective-permute-done((f32[32,6,8,128]{3,0,2,1:T(8,128)S(1)}, f32[32,6,8,128]{3,0,2,1:T(8,128)S(1)}, u32[]{:S(2)}, u32[]{:S(2)}) %collective-permute-start.4) | collective-permute-done | bytes 786464 | tf_op jit(solution)/shard_map/ppermute | solution.py:33
  122.9 6.3 %collective-permute-done.5 = f32[32,6,8,128]{3,0,2,1:T(8,128)S(1)} collective-permute-done((f32[32,6,8,128]{3,0,2,1:T(8,128)S(1)}, f32[32,6,8,128]{3,0,2,1:T(8,128)S(1)}, u32[]{:S(2)}, u32[]{:S(2)}) %collective-permute-start.5) | collective-permute-done | bytes 786464 | tf_op jit(solution)/shard_map/ppermute | solution.py:30
  130.0 2.9 collective-permute-start.6
  132.9 3.1 collective-permute-start.7
  136.1 1.8 fusion.235
  137.8 1.7 fusion.236
  146.3 1.8 fusion.241
  148.1 30.7 %collective-permute-done.6 = f32[32,20,6,128]{3,0,2,1:T(8,128)S(1)} collective-permute-done((f32[32,20,6,128]{3,0,2,1:T(8,128)S(1)}, f32[32,20,6,128]{3,0,2,1:T(8,128)S(1)}, u32[]{:S(2)}, u32[]{:S(2)}) %collective-permute-start.6) | collective-permute-done | bytes 1966112 | tf_op jit(solution)/shard_map/ppermute | solution.py:33
  178.8 4.3 %pad_maximum_fusion = (f32[32,20,14,128]{3,0,2,1:T(8,128)}, f32[32,20,14,128]{3,0,2,1:T(8,128)}) fusion(f32[32,20,6,128]{3,0,2,1:T(8,128)S(1)} %collective-permute-done.6, f32[32,6,8,128]{3,0,2,1:T(8,128)S(1)} %collective-permute-done.4, f32[32,8,8,128]{3,0,2,1:T(8,128)S(1)} %get-tuple-element.4, f32[32,6,8,128]{3,0,2,1:T(8,128)S(1)} %collective-permute-done.5, ...), kind=kLoop, calls=%fused_computation.20 | loop fusion | flops 6881280 | bytes 15728640 | tf_op jit(solution)/shard_map/concatenate | solution.py:34
  183.0 17.8 %fusion.46 = f32[32,8,8,128]{3,0,2,1:T(8,128)S(1)} fusion(f32[32,8,8,128]{3,0,2,1:T(8,128)S(1)} %get-tuple-element.4, f32[32,6,8,128]{3,0,2,1:T(8,128)} %copy-done.5, f32[32,6,8,128]{3,0,2,1:T(8,128)} %copy-done.3, f32[32,20,14,128]{3,0,2,1:T(8,128)} %get-tuple-element.11, f32[32,20,14,128]{3,0,2,1:T(8,128)} %get-tuple-element.10, ...), kind=kLoop, calls=%fused_computation.122 | loop fusion | flops 22544384 | bytes 30965760 | tf_op jit(solution)/shard_map/sub | solution.py:89
  207.5 1.8 fusion.220
  211.0 11.1 %collective-permute-done.8 = f32[32,6,8,128]{3,0,2,1:T(8,128)S(1)} collective-permute-done((f32[32,6,8,128]{3,0,2,1:T(8,128)S(1)}, f32[32,6,8,128]{3,0,2,1:T(8,128)S(1)}, u32[]{:S(2)}, u32[]{:S(2)}) %collective-permute-start.8) | collective-permute-done | bytes 786464 | tf_op jit(solution)/shard_map/ppermute | solution.py:33
  222.1 4.2 %collective-permute-done.9 = f32[32,6,8,128]{3,0,2,1:T(8,128)S(1)} collective-permute-done((f32[32,6,8,128]{3,0,2,1:T(8,128)S(1)}, f32[32,6,8,128]{3,0,2,1:T(8,128)S(1)}, u32[]{:S(2)}, u32[]{:S(2)}) %collective-permute-start.9) | collective-permute-done | bytes 786464 | tf_op jit(solution)/shard_map/ppermute | solution.py:30
  227.2 2.4 collective-permute-start.10
  230.6 1.8 fusion.222
  232.3 1.7 fusion.223
  240.8 1.8 fusion.228
  242.6 29.8 %collective-permute-done.10 = f32[32,20,6,128]{3,0,2,1:T(8,128)S(1)} collective-permute-done((f32[32,20,6,128]{3,0,2,1:T(8,128)S(1)}, f32[32,20,6,128]{3,0,2,1:T(8,128)S(1)}, u32[]{:S(2)}, u32[]{:S(2)}) %collective-permute-start.10) | collective-permute-done | bytes 1966112 | tf_op jit(solution)/shard_map/ppermute | solution.py:33
  272.4 4.5 %pad_maximum_fusion.1 = (f32[32,20,14,128]{3,0,2,1:T(8,128)}, f32[32,20,14,128]{3,0,2,1:T(8,128)}) fusion(f32[32,20,6,128]{3,0,2,1:T(8,128)S(1)} %collective-permute-done.10, f32[32,6,8,128]{3,0,2,1:T(8,128)S(1)} %collective-permute-done.8, f32[32,8,8,128]{3,0,2,1:T(8,128)S(1)} %fusion.46, f32[32,6,8,128]{3,0,2,1:T(8,128)S(1)} %collective-permute-done.9, ...), kind=kLoop, calls=%fused_computation.22 | loop fusion | flops 6881280 | bytes 15728640 | tf_op jit(solution)/shard_map/concatenate | solution.py:34
  276.9 17.4 %fusion.13 = f32[32,8,8,128]{3,0,2,1:T(8,128)S(1)} fusion(f32[32,8,8,128]{3,0,2,1:T(8,128)S(1)} %fusion.46, f32[32,6,8,128]{3,0,2,1:T(8,128)} %copy-done.6, f32[32,6,8,128]{3,0,2,1:T(8,128)} %copy-done.4, f32[32,20,14,128]{3,0,2,1:T(8,128)} %get-tuple-element.7, f32[32,20,14,128]{3,0,2,1:T(8,128)} %get-tuple-element.6, ...), kind=kLoop, calls=%fused_computation.89 | loop fusion | flops 22806528 | bytes 29917184 | tf_op jit(solution)/shard_map/sub | solution.py:89
  296.0 2.9 cholesky.149
  300.3 2.4 custom-call.11
  305.4 2.9 cholesky.160
  311.1 2.4 custom-call.12
  315.0 2.9 cholesky.171
  320.0 3.9 %collective-permute-done.13 = f32[32,32]{1,0:T(8,128)S(1)} collective-permute-done((f32[32,32]{1,0:T(8,128)S(1)}, f32[32,32]{1,0:T(8,128)S(1)}, u32[]{:S(2)}, u32[]{:S(2)}) %collective-permute-start.13) | collective-permute-done | bytes 4128 | tf_op jit(solution)/shard_map/ppermute | solution.py:45
  324.2 2.9 cholesky.182
  328.9 2.4 collective-permute-done.14
  331.6 2.9 cholesky.193
  336.3 3.9 %collective-permute-done.15 = f32[32,32]{1,0:T(8,128)S(1)} collective-permute-done((f32[32,32]{1,0:T(8,128)S(1)}, f32[32,32]{1,0:T(8,128)S(1)}, u32[]{:S(2)}, u32[]{:S(2)}) %collective-permute-start.15) | collective-permute-done | bytes 4128 | tf_op jit(solution)/shard_map/ppermute | solution.py:45
  340.5 2.9 cholesky.204
  345.2 2.4 collective-permute-done.16
  347.9 2.9 cholesky.215
  352.4 6.8 %collective-permute-start.17 = (f32[32,32]{1,0:T(8,128)S(1)}, f32[32,32]{1,0:T(8,128)S(1)}, u32[]{:S(2)}, u32[]{:S(2)}) collective-permute-start(f32[32,32]{1,0:T(8,128)S(1)} %bitcast_select_fusion.2), channel_id=1, source_target_pairs={{0,1},{1,0},{2,3},{3,2},{4,5},{5,4},{6,7},{7,6},{8,9},{9,8},{10,11... | collective-permute-start | bytes 12296 | tf_op jit(solution)/shard_map/ppermute | solution.py:45
  360.3 2.9 cholesky.226
  364.8 1.9 collective-permute-start.18
  367.0 2.0 collective-permute-done.18
  369.2 2.9 cholesky.237
  375.1 2.4 custom-call.9
  (180 shorter events, 111.0 us)
Async XLA Ops:
  0.6 10.1 %copy-start = (f32[32,8,8,128]{3,2,1,0:T(8,128)S(1)}, f32[32,8,8,128]{3,2,1,0:T(8,128)}, u32[]{:S(2)}) copy-start(f32[32,8,8,128]{3,2,1,0:T(8,128)} %param.5) | copy-start | bytes 3145732
  2.5 25.1 %collective-permute-start.1 = (f32[32,6,8,128]{3,0,2,1:T(8,128)S(1)}, f32[32,6,8,128]{3,0,2,1:T(8,128)S(1)}, u32[]{:S(2)}, u32[]{:S(2)}) collective-permute-start(f32[32,6,8,128]{3,0,2,1:T(8,128)S(1)} %copy.233), channel_id=1, source_target_pairs={{0,4},{4,8},{8,12},{12,16},{16,20},{20,24},{24,28},{28,32},{32,36}... | collective-permute-start | bytes 2359304 | tf_op jit(solution)/shard_map/ppermute | solution.py:30
  5.3 25.4 %collective-permute-start = (f32[32,6,8,128]{3,0,2,1:T(8,128)S(1)}, f32[32,6,8,128]{3,0,2,1:T(8,128)S(1)}, u32[]{:S(2)}, u32[]{:S(2)}) collective-permute-start(f32[32,6,8,128]{3,0,2,1:T(8,128)S(1)} %copy.234), channel_id=1, source_target_pairs={{4,0},{8,4},{12,8},{16,12},{20,16},{24,20},{28,24},{32,28},{36,32}... | collective-permute-start | bytes 2359304 | tf_op jit(solution)/shard_map/ppermute | solution.py:33
  31.7 1.6 copy-start.1
  33.4 45.3 %collective-permute-start.2 = (f32[32,20,6,128]{3,0,2,1:T(8,128)S(1)}, f32[32,20,6,128]{3,0,2,1:T(8,128)S(1)}, u32[]{:S(2)}, u32[]{:S(2)}) collective-permute-start(f32[32,20,6,128]{3,0,2,1:T(8,128)S(1)} %get-tuple-element.14), channel_id=1, source_target_pairs={{1,0},{2,1},{3,2},{0,3},{5,4},{6,5},{7,6},{4,7},{9,8},{10,9},{11,1... | collective-permute-start | bytes 5898248 | tf_op jit(solution)/shard_map/ppermute | solution.py:33
  34.6 44.6 %collective-permute-start.3 = (f32[32,20,6,128]{3,0,2,1:T(8,128)S(1)}, f32[32,20,6,128]{3,0,2,1:T(8,128)S(1)}, u32[]{:S(2)}, u32[]{:S(2)}) collective-permute-start(f32[32,20,6,128]{3,0,2,1:T(8,128)S(1)} %get-tuple-element.15), channel_id=1, source_target_pairs={{0,1},{1,2},{2,3},{3,0},{4,5},{5,6},{6,7},{7,4},{8,9},{9,10},{10,1... | collective-permute-start | bytes 5898248 | tf_op jit(solution)/shard_map/ppermute | solution.py:30
  74.3 3.2 copy-start.9
  78.7 1.3 copy-start.7
  79.2 1.4 copy-start.8
  104.9 18.0 %collective-permute-start.4 = (f32[32,6,8,128]{3,0,2,1:T(8,128)S(1)}, f32[32,6,8,128]{3,0,2,1:T(8,128)S(1)}, u32[]{:S(2)}, u32[]{:S(2)}) collective-permute-start(f32[32,6,8,128]{3,0,2,1:T(8,128)S(1)} %get-tuple-element.66), channel_id=1, source_target_pairs={{4,0},{8,4},{12,8},{16,12},{20,16},{24,20},{28,24},{32,28},{36,32}... | collective-permute-start | bytes 2359304 | tf_op jit(solution)/shard_map/ppermute | solution.py:33
  107.6 21.6 %collective-permute-start.5 = (f32[32,6,8,128]{3,0,2,1:T(8,128)S(1)}, f32[32,6,8,128]{3,0,2,1:T(8,128)S(1)}, u32[]{:S(2)}, u32[]{:S(2)}) collective-permute-start(f32[32,6,8,128]{3,0,2,1:T(8,128)S(1)} %get-tuple-element.67), channel_id=1, source_target_pairs={{0,4},{4,8},{8,12},{12,16},{16,20},{20,24},{24,28},{28,32},{32,36}... | collective-permute-start | bytes 2359304 | tf_op jit(solution)/shard_map/ppermute | solution.py:30
  122.9 55.9 %copy-start.3 = (f32[32,6,8,128]{3,0,2,1:T(8,128)}, f32[32,6,8,128]{3,0,2,1:T(8,128)S(1)}, u32[]{:S(2)}) copy-start(f32[32,6,8,128]{3,0,2,1:T(8,128)S(1)} %collective-permute-done.4) | copy-start | bytes 2359300
  129.1 49.6 %copy-start.5 = (f32[32,6,8,128]{3,0,2,1:T(8,128)}, f32[32,6,8,128]{3,0,2,1:T(8,128)S(1)}, u32[]{:S(2)}) copy-start(f32[32,6,8,128]{3,0,2,1:T(8,128)S(1)} %collective-permute-done.5) | copy-start | bytes 2359300
  130.0 48.7 %collective-permute-start.6 = (f32[32,20,6,128]{3,0,2,1:T(8,128)S(1)}, f32[32,20,6,128]{3,0,2,1:T(8,128)S(1)}, u32[]{:S(2)}, u32[]{:S(2)}) collective-permute-start(f32[32,20,6,128]{3,0,2,1:T(8,128)S(1)} %get-tuple-element.12), channel_id=1, source_target_pairs={{1,0},{2,1},{3,2},{0,3},{5,4},{6,5},{7,6},{4,7},{9,8},{10,9},{11,1... | collective-permute-start | bytes 5898248 | tf_op jit(solution)/shard_map/ppermute | solution.py:33
  132.9 45.8 %collective-permute-start.7 = (f32[32,20,6,128]{3,0,2,1:T(8,128)S(1)}, f32[32,20,6,128]{3,0,2,1:T(8,128)S(1)}, u32[]{:S(2)}, u32[]{:S(2)}) collective-permute-start(f32[32,20,6,128]{3,0,2,1:T(8,128)S(1)} %get-tuple-element.13), channel_id=1, source_target_pairs={{0,1},{1,2},{2,3},{3,0},{4,5},{5,6},{6,7},{7,4},{8,9},{9,10},{10,1... | collective-permute-start | bytes 5898248 | tf_op jit(solution)/shard_map/ppermute | solution.py:30
  204.4 17.8 %collective-permute-start.8 = (f32[32,6,8,128]{3,0,2,1:T(8,128)S(1)}, f32[32,6,8,128]{3,0,2,1:T(8,128)S(1)}, u32[]{:S(2)}, u32[]{:S(2)}) collective-permute-start(f32[32,6,8,128]{3,0,2,1:T(8,128)S(1)} %get-tuple-element.40), channel_id=1, source_target_pairs={{4,0},{8,4},{12,8},{16,12},{20,16},{24,20},{28,24},{32,28},{36,32}... | collective-permute-start | bytes 2359304 | tf_op jit(solution)/shard_map/ppermute | solution.py:33
  204.4 22.0 %collective-permute-start.9 = (f32[32,6,8,128]{3,0,2,1:T(8,128)S(1)}, f32[32,6,8,128]{3,0,2,1:T(8,128)S(1)}, u32[]{:S(2)}, u32[]{:S(2)}) collective-permute-start(f32[32,6,8,128]{3,0,2,1:T(8,128)S(1)} %get-tuple-element.41), channel_id=1, source_target_pairs={{0,4},{4,8},{8,12},{12,16},{16,20},{20,24},{24,28},{28,32},{32,36}... | collective-permute-start | bytes 2359304 | tf_op jit(solution)/shard_map/ppermute | solution.py:30
  222.1 50.3 %copy-start.4 = (f32[32,6,8,128]{3,0,2,1:T(8,128)}, f32[32,6,8,128]{3,0,2,1:T(8,128)S(1)}, u32[]{:S(2)}) copy-start(f32[32,6,8,128]{3,0,2,1:T(8,128)S(1)} %collective-permute-done.8) | copy-start | bytes 2359300
  226.3 46.1 %copy-start.6 = (f32[32,6,8,128]{3,0,2,1:T(8,128)}, f32[32,6,8,128]{3,0,2,1:T(8,128)S(1)}, u32[]{:S(2)}) copy-start(f32[32,6,8,128]{3,0,2,1:T(8,128)S(1)} %collective-permute-done.9) | copy-start | bytes 2359300
  227.2 45.2 %collective-permute-start.10 = (f32[32,20,6,128]{3,0,2,1:T(8,128)S(1)}, f32[32,20,6,128]{3,0,2,1:T(8,128)S(1)}, u32[]{:S(2)}, u32[]{:S(2)}) collective-permute-start(f32[32,20,6,128]{3,0,2,1:T(8,128)S(1)} %get-tuple-element.8), channel_id=1, source_target_pairs={{1,0},{2,1},{3,2},{0,3},{5,4},{6,5},{7,6},{4,7},{9,8},{10,9},{11,1... | collective-permute-start | bytes 5898248 | tf_op jit(solution)/shard_map/ppermute | solution.py:33
  229.6 42.9 %collective-permute-start.11 = (f32[32,20,6,128]{3,0,2,1:T(8,128)S(1)}, f32[32,20,6,128]{3,0,2,1:T(8,128)S(1)}, u32[]{:S(2)}, u32[]{:S(2)}) collective-permute-start(f32[32,20,6,128]{3,0,2,1:T(8,128)S(1)} %get-tuple-element.9), channel_id=1, source_target_pairs={{0,1},{1,2},{2,3},{3,0},{4,5},{5,6},{6,7},{7,4},{8,9},{9,10},{10,1... | collective-permute-start | bytes 5898248 | tf_op jit(solution)/shard_map/ppermute | solution.py:30
  242.6 34.3 %copy-start.2 = (f32[32,8,8,128]{3,0,2,1:T(8,128)S(1)}, f32[32,8,8,128]{3,0,2,1:T(8,128)}, u32[]{:S(2)}) copy-start(f32[32,8,8,128]{3,0,2,1:T(8,128)} %get-tuple-element.5) | copy-start | bytes 3145732
  311.1 3.8 collective-permute-start.12
  319.5 4.4 %collective-permute-start.13 = (f32[32,32]{1,0:T(8,128)S(1)}, f32[32,32]{1,0:T(8,128)S(1)}, u32[]{:S(2)}, u32[]{:S(2)}) collective-permute-start(f32[32,32]{1,0:T(8,128)S(1)} %bitcast_select_fusion.6), channel_id=1, source_target_pairs={{0,8},{8,0},{4,12},{12,4},{16,24},{24,16},{20,28},{28,20},{32,40},... | collective-permute-start | bytes 12296 | tf_op jit(solution)/shard_map/ppermute | solution.py:45
  328.7 2.6 collective-permute-start.14
  336.1 4.1 %collective-permute-start.15 = (f32[32,32]{1,0:T(8,128)S(1)}, f32[32,32]{1,0:T(8,128)S(1)}, u32[]{:S(2)}, u32[]{:S(2)}) collective-permute-start(f32[32,32]{1,0:T(8,128)S(1)} %bitcast_select_fusion.4), channel_id=1, source_target_pairs={{0,32},{32,0},{4,36},{36,4},{8,40},{40,8},{12,44},{44,12},{16,48},... | collective-permute-start | bytes 12296 | tf_op jit(solution)/shard_map/ppermute | solution.py:45
  345.0 2.6 collective-permute-start.16
  352.4 7.7 %collective-permute-start.17 = (f32[32,32]{1,0:T(8,128)S(1)}, f32[32,32]{1,0:T(8,128)S(1)}, u32[]{:S(2)}, u32[]{:S(2)}) collective-permute-start(f32[32,32]{1,0:T(8,128)S(1)} %bitcast_select_fusion.2), channel_id=1, source_target_pairs={{0,1},{1,0},{2,3},{3,2},{4,5},{5,4},{6,7},{7,6},{8,9},{9,8},{10,11... | collective-permute-start | bytes 12296 | tf_op jit(solution)/shard_map/ppermute | solution.py:45
  364.8 4.1 %collective-permute-start.18 = (f32[32,32]{1,0:T(8,128)S(1)}, f32[32,32]{1,0:T(8,128)S(1)}, u32[]{:S(2)}, u32[]{:S(2)}) collective-permute-start(f32[32,32]{1,0:T(8,128)S(1)} %bitcast_select_fusion.1), channel_id=1, source_target_pairs={{0,2},{2,0},{1,3},{3,1},{4,6},{6,4},{5,7},{7,5},{8,10},{10,8},{9,1... | collective-permute-start | bytes 12296 | tf_op jit(solution)/shard_map/ppermute | solution.py:45
where the time goes:
time: 385 us; the launch traced here: 380 us
  waiting for transfers between devices  123 us (32%)
  other arithmetic  113 us (29%)
  local copies, waits for them, and re-layouts  97.2 us (25%)
  starting transfers between devices  34.9 us (9%)
  matrix products  10 us (3%)
    ppermute x6, waiting for transfers between devices, extended(): lax.ppermute(lax.slice_in_dim(block, 0, width, axis=dim), axis, backward)  82.6 us
    unnamed x49, local copies, waits for them, and re-layouts  44.7 us
    slice x24, local copies, waits for them, and re-layouts, rolled_sum(): jnp.roll(centre, -offset, axis_pos)  41.1 us
    sub x2, other arithmetic, run_filter(): following = 2.0 * apply_fn(current, potential) - previous  35.2 us
    another operation x21, other arithmetic, combine_level(): return jnp.triu(jnp.linalg.cholesky(joined).T)  25.8 us
    ppermute x6, waiting for transfers between devices, extended(): lax.ppermute(lax.slice_in_dim(block, block.shape[dim] - width, None, axis...  25.7 us
    div x1, other arithmetic, finish_apply(): return (applied - centre_shift * current) / half_width  20.8 us
    ppermute x7, waiting for transfers between devices, from_partner(): return lax.ppermute(block, axis, route)  15.1 us
  transfers between devices with their start and end apart: 19, of which 15 were waited for; matrix products, arithmetic and copies ran while one was open for 22% of the time, Pallas kernels for 0%

commit v1 on v0

v1 whole, which is shorter than its diff:
```python
import functools

import jax
import jax.numpy as jnp
from jax import lax
from jax.experimental import pallas as pl
from jax.experimental.pallas import tpu as pltpu
from jax.sharding import Mesh
from jax.sharding import PartitionSpec as P

stencil_weights = (
    -5369.0 / 1800.0,
    12.0 / 7.0,
    -15.0 / 56.0,
    10.0 / 189.0,
    -1.0 / 112.0,
    2.0 / 1925.0,
    -1.0 / 16632.0,
)
grid_spacing = 0.5
filter_low = 4.0
filter_high = 46.0
centre_shift = 0.5 * (filter_high + filter_low)
half_width = 0.5 * (filter_high - filter_low)
kinetic = -0.5 / grid_spacing**2
diagonal = (kinetic * 3.0 * stencil_weights[0] - centre_shift) / half_width
coupling = tuple(kinetic * w / half_width for w in stencil_weights)
highest = lax.Precision.HIGHEST

REACH = 6
DEEP = 3 * REACH
FLAT = 2 * REACH
PAIR = 2
BX = 8
SLAB = 4 * BX
VMEM = pl.BlockSpec(memory_space=pltpu.VMEM)
SMEM = pl.BlockSpec(memory_space=pltpu.SMEM)


def pack_kernel(got, up, down):
    for dest, first, first_flat in ((up, SLAB - DEEP, SLAB - FLAT), (down, 0, 0)):
        for o in range(PAIR):
            for i in range(DEEP):
                z, xi = divmod(first + i, BX)
                for gy in range(4):
                    dest[o * DEEP + i, gy] = got[z * 4 + gy, o * BX + xi]
        for i in range(FLAT // 2):
            z, xi = divmod(first_flat // 2 + i, BX // 2)
            for gy in range(4):
                dest[PAIR * DEEP + i, gy] = got[z * 4 + gy, PAIR * BX + xi]


def filter_kernel(core, got, low, high, far, far_low, far_high, out, field0, field1, field2, pot):
    mine = core[0]

    def put(field, o, row, tiles):
        for t in range(4):
            field[o, row, 8 + 8 * t : 16 + 8 * t] = tiles[t]
        field[o, row, 0:8] = tiles[3]
        field[o, row, 40:48] = tiles[0]

    for o in range(PAIR):
        def edge(i, carry, o=o):
            put(field0, o, i, [low[o * DEEP + i, gy] for gy in range(4)])
            put(field0, o, DEEP + SLAB + i, [high[o * DEEP + i, gy] for gy in range(4)])
            return carry

        lax.fori_loop(0, DEEP, edge, 0)
        for z in range(4):
            def inner(xi, carry, o=o, z=z):
                put(field0, o, DEEP + z * BX + xi, [got[z * 4 + gy, o * BX + xi] for gy in range(4)])
                return carry

            lax.fori_loop(0, BX, inner, 0)

    def put_pot(row, own, other):
        for gy in range(4):
            pot[row + mine, 8 * gy : 8 * gy + 8] = diagonal + own[gy] * (1.0 / half_width)
            pot[row + 1 - mine, 8 * gy : 8 * gy + 8] = diagonal + other[gy] * (1.0 / half_width)

    for i in range(FLAT // 2):
        r = PAIR * DEEP + i
        put_pot(2 * i, [low[r, g] for g in range(4)], [far_low[i, g] for g in range(4)])
        put_pot(
            FLAT + SLAB + 2 * i, [high[r, g] for g in range(4)], [far_high[i, g] for g in range(4)]
        )
    for z in range(4):
        for i in range(BX // 2):
            put_pot(
                FLAT + z * BX + 2 * i,
                [got[z * 4 + g, PAIR * BX + i] for g in range(4)],
                [far[z * 4 + g, i] for g in range(4)],
            )

    def apply(field, o, row, pot_row):
        v = field[o, row, 8:40]
        total = pot[pot_row] * v
        for j in range(1, REACH + 1):
            near = (field[o, row + j, 8:40] + field[o, row - j, 8:40]) + (
                field[o, row, 8 + j : 40 + j] + field[o, row, 8 - j : 40 - j]
            )
            near = near + (pltpu.roll(v, j, 1) + pltpu.roll(v, 128 - j, 1))
            total = total + coupling[j] * near
        return total

    def tiles_of(t):
        return [t[8 * k : 8 * k + 8] for k in range(4)]

    def first(i, carry):
        for o in range(PAIR):
            put(field1, o, i, tiles_of(apply(field0, o, i + REACH, i)))
        return carry

    lax.fori_loop(0, SLAB + 2 * FLAT, first, 0)

    def second(i, carry):
        for o in range(PAIR):
            t = apply(field1, o, i + REACH, i + REACH)
            put(field2, o, i, tiles_of(t + t - field0[o, i + FLAT, 8:40]))
        return carry

    lax.fori_loop(0, SLAB + FLAT, second, 0)

    for z in range(4):
        def third(xi, carry, z=z):
            i = z * BX + xi
            for o in range(PAIR):
                t = apply(field2, o, i + REACH, i + FLAT)
                t = t + t - field1[o, i + FLAT, 8:40]
                for gy in range(4):
                    out[z * 4 + gy, o, xi] = t[8 * gy : 8 * gy + 8]
            return carry

        lax.fori_loop(0, BX, third, 0)


def iota(shape, dim):
    return lax.broadcasted_iota(jnp.int32, shape, dim)


def spread(orbital_count):
    shape = (orbital_count * BX, orbital_count)
    return (iota(shape, 0) // BX == iota(shape, 1)).astype(jnp.float32)


def same_y(orbital_count):
    shape = (orbital_count * BX, orbital_count * BX)
    return iota(shape, 0) % BX == iota(shape, 1) % BX


def dot(a, b, dims=((1,), (0,))):
    return lax.dot_general(
        a, b, (dims, ((), ())), precision=highest, preferred_element_type=jnp.float32
    )


def gram_kernel(scale, y, out):
    n = y.shape[0]
    total = None
    for x in range(BX):
        block = y[:, x].reshape(n * BX, 128)
        part = dot(block, block, ((1,), (1,)))
        total = part if total is None else total + part
    total = jnp.where(same_y(n), total, 0.0) * scale
    ones = spread(n)
    gram = dot(dot(ones, total, ((0,), (0,))), ones)
    wide = jnp.concatenate([gram[8 * k : 8 * k + 8] for k in range(n // 8)], axis=1)
    for d in range(out.shape[0]):
        out[d] = wide


def finish_kernel(parts, y, out, factor):
    n = y.shape[0]
    wide = jnp.sum(parts[...], axis=0)
    gram = jnp.concatenate([wide[:, n * k : n * k + n] for k in range(n // 8)], axis=0)
    unit = (iota((n, n), 0) == iota((n, n), 1)).astype(jnp.float32)
    left = jnp.concatenate([gram, unit, jnp.zeros((n, 128 - 2 * n), jnp.float32)], axis=1)
    row_of = iota((n, 128), 0)
    done = jnp.zeros((n, 128), jnp.float32)
    for k in range(n):
        inverse = lax.rsqrt(left[k : k + 1, k : k + 1])
        row = left[k : k + 1] * inverse
        column = left[:, k : k + 1] * inverse
        done = jnp.where(row_of == k, row, done)
        left = left - jnp.where(row_of > k, column, 0.0) * row
    factor[...] = jnp.where(iota((n, n), 0) <= iota((n, n), 1), done[:, :n], 0.0)
    mixer = done[:, n : 2 * n]
    ones = spread(n)
    wide_mixer = jnp.where(same_y(n), dot(dot(ones, mixer), ones, ((1,), (1,))), 0.0)
    for x in range(BX):
        block = y[:, x].reshape(n * BX, 128)
        out[:, x] = dot(wide_mixer, block).reshape(n, BX, 128)


def call(kernel, out_shape, in_specs, scratch=(), flops=0, moved=0):
    return pl.pallas_call(
        kernel,
        out_shape=out_shape,
        in_specs=in_specs,
        out_specs=jax.tree.map(lambda _: VMEM, out_shape),
        scratch_shapes=list(scratch),
        cost_estimate=pl.CostEstimate(flops=flops, bytes_accessed=moved, transcendentals=0),
    )


def f32(*shape):
    return jax.ShapeDtypeStruct(shape, jnp.float32)


def per_device(orbitals, potential):
    n = orbitals.shape[0]
    slabs = lax.axis_size("s")
    group = lax.axis_size("z") * lax.axis_size("gy")
    core = lax.axis_index("gy") % 2
    halves = potential.reshape(BX // 2, 2, BX, 128).swapaxes(0, 1)
    halves = jnp.broadcast_to(halves[None], (group // 2, 2, BX // 2, BX, 128))
    sent = jnp.concatenate(
        [orbitals.reshape(group, PAIR * BX, BX, 128), halves.reshape(group, BX // 2, BX, 128)],
        axis=1,
    )
    got = lax.all_to_all(sent, ("z", "gy"), 0, 0, tiled=True)
    rows = PAIR * DEEP + FLAT // 2
    up, down = call(pack_kernel, (f32(rows, 4, 8, 128),) * 2, [VMEM])(got)
    ring = [(i, (i + 1) % slabs) for i in range(slabs)]
    low = lax.ppermute(up, "s", ring)
    high = lax.ppermute(down, "s", [(j, i) for i, j in ring])
    twin = [(i, i ^ 1) for i in range(lax.axis_size("gy"))]
    far = lax.ppermute(got[:, PAIR * BX :], "gy", twin)
    far_low = lax.ppermute(low[PAIR * DEEP :], "gy", twin)
    far_high = lax.ppermute(high[PAIR * DEEP :], "gy", twin)
    filtered = call(
        filter_kernel,
        f32(group, PAIR, BX, BX, 128),
        [SMEM] + [VMEM] * 6,
        [
            pltpu.VMEM((PAIR, SLAB + 2 * DEEP, 48, 128), jnp.float32),
            pltpu.VMEM((PAIR, SLAB + 2 * FLAT, 48, 128), jnp.float32),
            pltpu.VMEM((PAIR, SLAB + FLAT, 48, 128), jnp.float32),
            pltpu.VMEM((SLAB + 2 * FLAT, 32, 128), jnp.float32),
        ],
    )(core.reshape(1), got, low, high, far, far_low, far_high)
    back = lax.all_to_all(filtered, ("z", "gy"), 0, 0, tiled=True).reshape(n, BX, BX, 128)
    devices = slabs * group
    cells = float(devices * BX * BX * 128)
    parts = call(
        functools.partial(gram_kernel, 1.0 / cells), f32(devices, 8, 128), [VMEM]
    )(back)
    parts = lax.all_to_all(parts, ("s", "z", "gy"), 0, 0, tiled=True)
    return call(finish_kernel, (f32(n, BX, BX, 128), f32(n, n)), [VMEM, VMEM])(parts, back)


def solution(mesh):
    shape = mesh.devices.shape
    fine = Mesh(mesh.devices.reshape(shape[0] // 4, 4, shape[1]), ("s", "z", "gy"))
    return jax.shard_map(
        per_device,
        mesh=fine,
        in_specs=(P(None, ("s", "z"), "gy", None), P(("s", "z"), "gy", None)),
        out_specs=(P(None, ("s", "z"), "gy", None), P()),
        check_vma=False,
    )
```

time: 385 us -> 138 us (0.36)
  other arithmetic: 113 us -> 1.32 us
  waiting for transfers between devices: 123 us -> 13.4 us
  local copies, waits for them, and re-layouts: 97.2 us -> 2.4 us
  blocking collectives: 0 us -> 70.3 us
  Pallas kernels: 0 us -> 41.7 us
  starting transfers between devices: 34.9 us -> 7.28 us
  matrix products: 10 us -> 0 us
    ppermute x19 -> x5, waiting for transfers between devices: 123 us -> 13.4 us  [the longest x1 12.1 us: per_device(): low = lax.ppermute(up, 's', ring)]
    all_to_all x0 -> x3, blocking collectives: none -> 70.3 us  [the longest x1 29.3 us: per_device(): got = lax.all_to_all(sent, ('z', 'gy'), 0, 0, tiled=True)]
    slice x42 -> x3, local copies, waits for them, and re-layouts: 49.5 us -> 0.98 us  [the longest x1 0.97 us: per_device(): far = lax.ppermute(got[:, PAIR * BX:], 'gy', twin)]
    unnamed x49 -> x10, local copies, waits for them, and re-layouts: 44.7 us -> 0.64 us
    pallas_call x0 -> x4, Pallas kernels: none -> 41.7 us  [the longest x1 27 us: per_device(): call(filter_kernel, f32(group, PAIR, BX, BX, 128), [SMEM] + [VMEM] * 6, [...]
    another operation x33 -> x0, other arithmetic: 41.6 us -> none  [the longest x21 25.8 us: combine_level(): return jnp.triu(jnp.linalg.cholesky(joined).T)]
    sub x2 -> x0, other arithmetic: 35.2 us -> none  [run_filter(): following = 2.0 * apply_fn(current, potential) - previous]
    ppermute x19 -> x5, starting transfers between devices: 34.9 us -> 7.28 us  [the longest x1 2.36 us: per_device(): high = lax.ppermute(down, 's', [(j, i) for i, j in ring])]
  transfers between devices with their start and end apart: 19 -> 5, of which waited for: 15 -> 3; matrix products, arithmetic and copies ran while one was open for 22% -> 1% of each run, Pallas kernels for 0% -> 0%
where the time goes in v1:
time: 138 us; the launch traced here: 137 us
  blocking collectives  70.3 us (51%)
  Pallas kernels  41.7 us (30%)
  waiting for transfers between devices  13.4 us (10%)
  starting transfers between devices  7.28 us (5%)
  local copies, waits for them, and re-layouts  2.4 us (2%)
    all_to_all x1, blocking collectives, per_device(): got = lax.all_to_all(sent, ('z', 'gy'), 0, 0, tiled=True)  29.3 us
    pallas_call x1, Pallas kernels, per_device(): call(filter_kernel, f32(group, PAIR, BX, BX, 128), [SMEM] + [VMEM] * 6, [...  27 us
    all_to_all x1, blocking collectives, per_device(): lax.all_to_all(filtered, ('z', 'gy'), 0, 0, tiled=True)  21.3 us
    all_to_all x1, blocking collectives, per_device(): parts = lax.all_to_all(parts, ('s', 'z', 'gy'), 0, 0, tiled=True)  19.7 us
    ppermute x1, waiting for transfers between devices, per_device(): low = lax.ppermute(up, 's', ring)  12.1 us
    pallas_call x1, Pallas kernels, per_device(): call(finish_kernel, (f32(n, BX, BX, 128), f32(n, n)), [VMEM, VMEM])  7.7 us
    pallas_call x1, Pallas kernels, per_device(): call(functools.partial(gram_kernel, 1.0 / cells), f32(devices, 8, 128), [...  4.58 us
  transfers between devices with their start and end apart: 5, of which 3 were waited for; matrix products, arithmetic and copies ran while one was open for 1% of the time, Pallas kernels for 0%

profile of v1, /device:TPU:1, one launch (start us, length us, event | category | flops | bytes accessed | tf_op | source)
XLA Modules:
  0.0 137.0 jit_solution(5335295000045996615)
XLA Ops:
  0.6 0.8 copy.4
  1.4 1.3 pad_maximum_fusion
  2.8 29.3 %all_to_all.15.got = f32[16,20,8,128]{3,2,1,0:T(8,128)} all-to-all(f32[16,20,8,128]{3,2,1,0:T(8,128)S(1)} %pad_maximum_fusion), channel_id=1, replica_groups=mesh['s'=8,'z'=4,'gy'=4] {'z','gy'}, dimensions={0} | all-to-all | bytes 2621440 | tf_op jit(solution)/shard_map/all_to_all | solution.py:221
  32.0 2.5 %shard_map.41 = (f32[42,4,8,128]{3,2,1,0:T(8,128)}, f32[42,4,8,128]{3,2,1,0:T(8,128)}) custom-call(f32[16,20,8,128]{3,2,1,0:T(8,128)} %all_to_all.15.got), custom_call_target="tpu_custom_call" | custom-call | tf_op jit(solution)/shard_map/pallas_call | solution.py:223
  34.5 1.2 collective-permute-start
  35.7 2.4 %collective-permute-start.1 = (f32[42,4,8,128]{3,2,1,0:T(8,128)}, f32[42,4,8,128]{3,2,1,0:T(8,128)S(1)}, u32[]{:S(2)}, u32[]{:S(2)}) collective-permute-start(f32[42,4,8,128]{3,2,1,0:T(8,128)} %get-tuple-element.5), channel_id=1, source_target_pairs={{16,0},{32,16},{48,32},{64,48},{80,64},{96,80},{112,96},{0,112},{1... | collective-permute-start | bytes 2064392 | tf_op jit(solution)/shard_map/ppermute | solution.py:226
  38.1 1.0 slice.12
  39.0 1.6 %collective-permute-start.2 = (f32[16,4,8,128]{3,2,1,0:T(8,128)S(1)}, f32[16,4,8,128]{3,2,1,0:T(8,128)S(1)}, u32[]{:S(2)}, u32[]{:S(2)}) collective-permute-start(f32[16,4,8,128]{3,2,1,0:T(8,128)S(1)} %slice.12), channel_id=1, source_target_pairs={{0,1},{1,0},{2,3},{3,2},{4,5},{5,4},{6,7},{7,6},{8,9},{9,8},{10,11... | collective-permute-start | bytes 786440 | tf_op jit(solution)/shard_map/ppermute | solution.py:228
  40.6 12.1 %collective-permute-done.low = f32[42,4,8,128]{3,2,1,0:T(8,128)S(1)} collective-permute-done((f32[42,4,8,128]{3,2,1,0:T(8,128)}, f32[42,4,8,128]{3,2,1,0:T(8,128)S(1)}, u32[]{:S(2)}, u32[]{:S(2)}) %collective-permute-start) | collective-permute-done | bytes 688160 | tf_op jit(solution)/shard_map/ppermute | solution.py:225
  52.7 0.0 copy-start
  52.8 2.0 %collective-permute-start.3 = (f32[6,4,8,128]{3,2,1,0:T(8,128)S(1)}, f32[6,4,8,128]{3,2,1,0:T(8,128)S(1)}, u32[]{:S(2)}, u32[]{:S(2)}) collective-permute-start(f32[6,4,8,128]{3,2,1,0:T(8,128)S(1)} %slice.13), channel_id=1, source_target_pairs={{0,1},{1,0},{2,3},{3,2},{4,5},{5,4},{6,7},{7,6},{8,9},{9,8},{10,11... | collective-permute-start | bytes 294920 | tf_op jit(solution)/shard_map/ppermute | solution.py:229
  54.7 0.0 collective-permute-done.1.high
  54.7 0.0 copy-start.1
  54.8 0.1 collective-permute-start.4
  54.9 0.0 collective-permute-done.2.far
  54.9 0.0 copy-start.2
  54.9 0.8 collective-permute-done.3.far_low
  55.7 0.0 copy-start.3
  55.7 0.5 collective-permute-done.4.far_high
  56.1 0.0 copy-start.4
  56.1 0.0 copy-done
  56.1 0.0 copy-done.1
  56.1 0.0 copy-done.2
  56.2 0.2 copy-done.3
  56.3 0.4 copy-done.4
  56.8 27.0 %shard_map.42 = f32[16,2,8,8,128]{4,3,2,1,0:T(8,128)} custom-call(s32[1]{0:T(128)} %bitcast.core, f32[16,20,8,128]{3,2,1,0:T(8,128)} %all_to_all.15.got, f32[42,4,8,128]{3,2,1,0:T(8,128)} %copy-done, f32[42,4,8,128]{3,2,1,0:T(8,128)} %copy-done.1, f32[16,4,8,128]{3,2,1,0:T(8,128)} %copy-done.2, f32[6,4,8,128]{3,2,1,0:T(8,128)} %copy-done.3, ...), custom_call_target="tpu_custom_call" | custom-call | tf_op jit(solution)/shard_map/pallas_call | solution.py:231
  83.7 21.3 %all_to_all.16 = f32[16,2,8,8,128]{4,3,2,1,0:T(8,128)} all-to-all(f32[16,2,8,8,128]{4,3,2,1,0:T(8,128)} %shard_map.42), channel_id=1, replica_groups=mesh['s'=8,'z'=4,'gy'=4] {'z','gy'}, dimensions={0} | all-to-all | bytes 2097152 | tf_op jit(solution)/shard_map/all_to_all | solution.py:242
  105.1 4.6 %shard_map.43 = f32[128,8,128]{2,1,0:T(8,128)} custom-call(f32[32,8,8,128]{3,2,1,0:T(8,128)} %bitcast.7), custom_call_target="tpu_custom_call" | custom-call | tf_op jit(solution)/shard_map/pallas_call | solution.py:245
  109.6 19.7 %all_to_all.17.parts = f32[128,8,128]{2,1,0:T(8,128)} all-to-all(f32[128,8,128]{2,1,0:T(8,128)} %shard_map.43), channel_id=1, replica_groups=mesh['s'=8,'z'=4,'gy'=4] {'s','z','gy'}, dimensions={0} | all-to-all | bytes 1048576 | tf_op jit(solution)/shard_map/all_to_all | solution.py:248
  129.3 7.7 %shard_map.44 = (f32[32,8,8,128]{3,2,1,0:T(8,128)}, f32[32,32]{1,0:T(8,128)}) custom-call(f32[128,8,128]{2,1,0:T(8,128)} %all_to_all.17.parts, f32[32,8,8,128]{3,2,1,0:T(8,128)} %bitcast.8), custom_call_target="tpu_custom_call" | custom-call | tf_op jit(solution)/shard_map/pallas_call | solution.py:249
  (3 shorter events, 0.0 us)
Async XLA Ops:
  34.5 18.3 %collective-permute-start = (f32[42,4,8,128]{3,2,1,0:T(8,128)}, f32[42,4,8,128]{3,2,1,0:T(8,128)S(1)}, u32[]{:S(2)}, u32[]{:S(2)}) collective-permute-start(f32[42,4,8,128]{3,2,1,0:T(8,128)} %get-tuple-element.4), channel_id=1, source_target_pairs={{0,16},{16,32},{32,48},{48,64},{64,80},{80,96},{96,112},{112,0},{1... | collective-permute-start | bytes 2064392 | tf_op jit(solution)/shard_map/ppermute | solution.py:225
  35.7 19.1 %collective-permute-start.1 = (f32[42,4,8,128]{3,2,1,0:T(8,128)}, f32[42,4,8,128]{3,2,1,0:T(8,128)S(1)}, u32[]{:S(2)}, u32[]{:S(2)}) collective-permute-start(f32[42,4,8,128]{3,2,1,0:T(8,128)} %get-tuple-element.5), channel_id=1, source_target_pairs={{16,0},{32,16},{48,32},{64,48},{80,64},{96,80},{112,96},{0,112},{1... | collective-permute-start | bytes 2064392 | tf_op jit(solution)/shard_map/ppermute | solution.py:226
  39.0 15.8 %collective-permute-start.2 = (f32[16,4,8,128]{3,2,1,0:T(8,128)S(1)}, f32[16,4,8,128]{3,2,1,0:T(8,128)S(1)}, u32[]{:S(2)}, u32[]{:S(2)}) collective-permute-start(f32[16,4,8,128]{3,2,1,0:T(8,128)S(1)} %slice.12), channel_id=1, source_target_pairs={{0,1},{1,0},{2,3},{3,2},{4,5},{5,4},{6,7},{7,6},{8,9},{9,8},{10,11... | collective-permute-start | bytes 786440 | tf_op jit(solution)/shard_map/ppermute | solution.py:228
  52.7 3.4 %copy-start = (f32[42,4,8,128]{3,2,1,0:T(8,128)}, f32[42,4,8,128]{3,2,1,0:T(8,128)S(1)}, u32[]{:S(2)}) copy-start(f32[42,4,8,128]{3,2,1,0:T(8,128)S(1)} %collective-permute-done.low) | copy-start | bytes 2064388
  52.8 2.9 %collective-permute-start.3 = (f32[6,4,8,128]{3,2,1,0:T(8,128)S(1)}, f32[6,4,8,128]{3,2,1,0:T(8,128)S(1)}, u32[]{:S(2)}, u32[]{:S(2)}) collective-permute-start(f32[6,4,8,128]{3,2,1,0:T(8,128)S(1)} %slice.13), channel_id=1, source_target_pairs={{0,1},{1,0},{2,3},{3,2},{4,5},{5,4},{6,7},{7,6},{8,9},{9,8},{10,11... | collective-permute-start | bytes 294920 | tf_op jit(solution)/shard_map/ppermute | solution.py:229
  54.7 1.4 %copy-start.1 = (f32[42,4,8,128]{3,2,1,0:T(8,128)}, f32[42,4,8,128]{3,2,1,0:T(8,128)S(1)}, u32[]{:S(2)}) copy-start(f32[42,4,8,128]{3,2,1,0:T(8,128)S(1)} %collective-permute-done.1.high) | copy-start | bytes 2064388
  54.8 1.4 %collective-permute-start.4 = (f32[6,4,8,128]{3,2,1,0:T(8,128)S(1)}, f32[6,4,8,128]{3,2,1,0:T(8,128)S(1)}, u32[]{:S(2)}, u32[]{:S(2)}) collective-permute-start(f32[6,4,8,128]{3,2,1,0:T(8,128)S(1)} %slice.14), channel_id=1, source_target_pairs={{0,1},{1,0},{2,3},{3,2},{4,5},{5,4},{6,7},{7,6},{8,9},{9,8},{10,11... | collective-permute-start | bytes 294920 | tf_op jit(solution)/shard_map/ppermute | solution.py:230
  54.9 1.3 copy-start.2
  55.7 0.6 copy-start.3
  56.1 0.6 copy-start.4

commit v2 on v1

v2 whole, which is shorter than its diff:
```python
import functools

import jax
import jax.numpy as jnp
from jax import lax
from jax.experimental import pallas as pl
from jax.experimental.pallas import tpu as pltpu
from jax.sharding import Mesh
from jax.sharding import PartitionSpec as P

stencil_weights = (
    -5369.0 / 1800.0,
    12.0 / 7.0,
    -15.0 / 56.0,
    10.0 / 189.0,
    -1.0 / 112.0,
    2.0 / 1925.0,
    -1.0 / 16632.0,
)
grid_spacing = 0.5
filter_low = 4.0
filter_high = 46.0
centre_shift = 0.5 * (filter_high + filter_low)
half_width = 0.5 * (filter_high - filter_low)
kinetic = -0.5 / grid_spacing**2
diagonal = (kinetic * 3.0 * stencil_weights[0] - centre_shift) / half_width
coupling = tuple(kinetic * w / half_width for w in stencil_weights)
highest = lax.Precision.HIGHEST

REACH = 6
DEEP = 3 * REACH
FLAT = 2 * REACH
PAIR = 2
BX = 8
BLOCK = BX + 2
SLAB = 4 * BX
VMEM = pl.BlockSpec(memory_space=pltpu.VMEM)
SMEM = pl.BlockSpec(memory_space=pltpu.SMEM)


def gather(got, z, xi, yi):
    return got[pl.ds(((z * 4) * PAIR * BLOCK + xi) * BX + yi, 8, stride=BLOCK * BX), :]


def pack_kernel(got, up, down, up_pot, down_pot, mid_pot):
    for dest, first in ((up, SLAB - DEEP), (down, 0)):
        for i in range(DEEP):
            z, xi = divmod(first + i, BX)
            for yi in range(BX):
                dest[i, yi] = gather(got, z, xi, yi)
    for z in range(4):
        for k in range(2):
            for yi in range(BX):
                tile = gather(got, z, BX + k, yi)
                mid_pot[2 * z + k, yi] = tile
                if z >= 2:
                    up_pot[2 * z - 4 + k, yi] = tile
                else:
                    down_pot[2 * z + k, yi] = tile


def put(field, row, tiles):
    for yi in range(BX):
        field[row, REACH + yi] = tiles[yi]
        if yi >= BX - REACH:
            field[row, REACH + yi - BX] = pltpu.roll(tiles[yi], PAIR, 0)
        if yi < REACH:
            field[row, REACH + yi + BX] = pltpu.roll(tiles[yi], 8 - PAIR, 0)


def filter_kernel(
    core, got, low, high, low_pot, high_pot, mid_pot, far_low, far_high, far_mid,
    out, field0, field1, field2, pot,
):
    mine = core[0]

    def edge(i, carry):
        put(field0, i, [low[i, yi] for yi in range(BX)])
        put(field0, DEEP + SLAB + i, [high[i, yi] for yi in range(BX)])
        return carry

    lax.fori_loop(0, DEEP, edge, 0)
    for z in range(4):
        def inner(xi, carry, z=z):
            put(field0, DEEP + z * BX + xi, [gather(got, z, xi, yi) for yi in range(BX)])
            return carry

        lax.fori_loop(0, BX, inner, 0)

    odd = iota((8, 128), 0) % 2 == 1

    def put_pot(row, source, i, yi, parity, skip):
        tile = diagonal + source[i, yi] * (1.0 / half_width)
        if skip != 0:
            pot[row + parity, yi] = jnp.where(odd, pltpu.roll(tile, 1, 0), tile)
        if skip != 1:
            pot[row + 4 + parity, yi] = jnp.where(odd, tile, pltpu.roll(tile, 7, 0))

    for sources, row, count, skip in (
        ((low_pot, far_low), FLAT - 2 * BX, 2, (0, None)),
        ((mid_pot, far_mid), FLAT, 4, (None,) * 4),
        ((high_pot, far_high), FLAT + SLAB, 2, (None, 1)),
    ):
        for z in range(count):
            for k in range(2):
                for source, parity in zip(sources, (mine, 1 - mine)):
                    for yi in range(BX):
                        put_pot(
                            row + z * BX + 2 * k, source, 2 * z + k, yi, parity, skip[z]
                        )

    def apply(field, row, pot_row):
        line = [field[row, e] for e in range(BX + 2 * REACH)]
        totals = []
        for yi in range(BX):
            e = REACH + yi
            v = line[e]
            total = pot[pot_row, yi] * v
            for j in range(1, REACH + 1):
                near = (field[row + j, e] + field[row - j, e]) + (line[e + j] + line[e - j])
                near = near + (pltpu.roll(v, j, 1) + pltpu.roll(v, 128 - j, 1))
                total = total + coupling[j] * near
            totals.append(total)
        return totals

    def first(i, carry):
        put(field1, i, apply(field0, i + REACH, i))
        return carry

    lax.fori_loop(0, SLAB + 2 * FLAT, first, 0)

    def second(i, carry):
        ts = apply(field1, i + REACH, i + REACH)
        put(field2, i, [t + t - field0[i + FLAT, REACH + yi] for yi, t in enumerate(ts)])
        return carry

    lax.fori_loop(0, SLAB + FLAT, second, 0)

    for z in range(4):
        def third(xi, carry, z=z):
            i = z * BX + xi
            for yi, t in enumerate(apply(field2, i + REACH, i + FLAT)):
                start = (z * 4 * PAIR * BX + xi) * BX + yi
                out[pl.ds(start, 8, stride=BX * BX), :] = t + t - field1[i + FLAT, REACH + yi]
            return carry

        lax.fori_loop(0, BX, third, 0)


def iota(shape, dim):
    return lax.broadcasted_iota(jnp.int32, shape, dim)


def spread(orbital_count):
    shape = (orbital_count * BX, orbital_count)
    return (iota(shape, 0) // BX == iota(shape, 1)).astype(jnp.float32)


def same_y(orbital_count):
    shape = (orbital_count * BX, orbital_count * BX)
    return iota(shape, 0) % BX == iota(shape, 1) % BX


def dot(a, b, dims=((1,), (0,))):
    return lax.dot_general(
        a, b, (dims, ((), ())), precision=highest, preferred_element_type=jnp.float32
    )


def gram_kernel(scale, y, out):
    n = y.shape[0]
    total = None
    for x in range(BX):
        block = y[:, x].reshape(n * BX, 128)
        part = dot(block, block, ((1,), (1,)))
        total = part if total is None else total + part
    total = jnp.where(same_y(n), total, 0.0) * scale
    ones = spread(n)
    gram = dot(dot(ones, total, ((0,), (0,))), ones)
    wide = jnp.concatenate([gram[8 * k : 8 * k + 8] for k in range(n // 8)], axis=1)
    for d in range(out.shape[0]):
        out[d] = wide


def finish_kernel(parts, y, out, factor):
    n = y.shape[0]
    wide = jnp.sum(parts[...], axis=0)
    gram = jnp.concatenate([wide[:, n * k : n * k + n] for k in range(n // 8)], axis=0)
    unit = (iota((n, n), 0) == iota((n, n), 1)).astype(jnp.float32)
    left = jnp.concatenate([gram, unit, jnp.zeros((n, 128 - 2 * n), jnp.float32)], axis=1)
    row_of = iota((n, 128), 0)
    done = jnp.zeros((n, 128), jnp.float32)
    for k in range(n):
        inverse = lax.rsqrt(left[k : k + 1, k : k + 1])
        row = left[k : k + 1] * inverse
        column = left[:, k : k + 1] * inverse
        done = jnp.where(row_of == k, row, done)
        left = left - jnp.where(row_of > k, column, 0.0) * row
    factor[...] = jnp.where(iota((n, n), 0) <= iota((n, n), 1), done[:, :n], 0.0)
    mixer = done[:, n : 2 * n]
    ones = spread(n)
    wide_mixer = jnp.where(same_y(n), dot(dot(ones, mixer), ones, ((1,), (1,))), 0.0)
    for x in range(BX):
        block = y[:, x].reshape(n * BX, 128)
        out[:, x] = dot(wide_mixer, block).reshape(n, BX, 128)


def call(kernel, out_shape, in_specs, scratch=(), flops=0, moved=0):
    return pl.pallas_call(
        kernel,
        out_shape=out_shape,
        in_specs=in_specs,
        out_specs=jax.tree.map(lambda _: VMEM, out_shape),
        scratch_shapes=list(scratch),
        cost_estimate=pl.CostEstimate(flops=flops, bytes_accessed=moved, transcendentals=0),
    )


def f32(*shape):
    return jax.ShapeDtypeStruct(shape, jnp.float32)


def per_device(orbitals, potential):
    n = orbitals.shape[0]
    slabs = lax.axis_size("s")
    group = lax.axis_size("z") * lax.axis_size("gy")
    core = lax.axis_index("gy") % 2
    halves = potential.reshape(2, 2, 2, BX, 128).transpose(2, 0, 1, 3, 4)
    halves = jnp.broadcast_to(halves[None], (group // 2, 2, PAIR, 2, BX, 128))
    sent = jnp.concatenate(
        [orbitals.reshape(group, PAIR, BX, BX, 128), halves.reshape(group, PAIR, 2, BX, 128)],
        axis=2,
    )
    got = lax.all_to_all(sent, ("z", "gy"), 0, 0, tiled=True)
    got = got.reshape(group * PAIR * BLOCK * BX, 128)
    up, down, up_pot, down_pot, mid_pot = call(
        pack_kernel, (f32(DEEP, 8, 8, 128),) * 2 + (f32(4, 8, 8, 128),) * 2 + (f32(8, 8, 8, 128),), [VMEM]
    )(got)
    ring = [(i, (i + 1) % slabs) for i in range(slabs)]
    back_ring = [(j, i) for i, j in ring]
    twin = [(i, i ^ 1) for i in range(lax.axis_size("gy"))]
    low_pot = lax.ppermute(up_pot, "s", ring)
    high_pot = lax.ppermute(down_pot, "s", back_ring)
    low = lax.ppermute(up, "s", ring)
    high = lax.ppermute(down, "s", back_ring)
    far_mid = lax.ppermute(mid_pot, "gy", twin)
    far_low = lax.ppermute(low_pot, "gy", twin)
    far_high = lax.ppermute(high_pot, "gy", twin)
    wide = BX + 2 * REACH
    filtered = call(
        filter_kernel,
        f32(group * PAIR * BX * BX, 128),
        [SMEM] + [VMEM] * 9,
        [
            pltpu.VMEM((SLAB + 2 * DEEP, wide, 8, 128), jnp.float32),
            pltpu.VMEM((SLAB + 2 * FLAT, wide, 8, 128), jnp.float32),
            pltpu.VMEM((SLAB + FLAT, wide, 8, 128), jnp.float32),
            pltpu.VMEM((SLAB + 2 * FLAT, BX, 8, 128), jnp.float32),
        ],
    )(core.reshape(1), got, low, high, low_pot, high_pot, mid_pot, far_low, far_high, far_mid)
    filtered = filtered.reshape(group, PAIR, BX, BX, 128)
    back = lax.all_to_all(filtered, ("z", "gy"), 0, 0, tiled=True).reshape(n, BX, BX, 128)
    devices = slabs * group
    cells = float(devices * BX * BX * 128)
    parts = call(
        functools.partial(gram_kernel, 1.0 / cells), f32(devices, 8, 128), [VMEM]
    )(back)
    parts = lax.all_to_all(parts, ("s", "z", "gy"), 0, 0, tiled=True)
    return call(finish_kernel, (f32(n, BX, BX, 128), f32(n, n)), [VMEM, VMEM])(parts, back)


def solution(mesh):
    shape = mesh.devices.shape
    fine = Mesh(mesh.devices.reshape(shape[0] // 4, 4, shape[1]), ("s", "z", "gy"))
    return jax.shard_map(
        per_device,
        mesh=fine,
        in_specs=(P(None, ("s", "z"), "gy", None), P(("s", "z"), "gy", None)),
        out_specs=(P(None, ("s", "z"), "gy", None), P()),
        check_vma=False,
    )
```

time: 138 us -> 139 us (level)
  starting transfers between devices: 7.28 us -> 11.2 us
  waiting for transfers between devices: 13.4 us -> 11 us
    ppermute x1, waiting for transfers between devices: 12.1 us -> 0.01 us  [per_device(): low = lax.ppermute(up, 's', ring)]
    ppermute x4 -> x6, waiting for transfers between devices: 1.26 us -> 11 us  [the longest x1 9.72 us: per_device(): low_pot = lax.ppermute(up_pot, 's', ring)]
    ppermute x4 -> x6, starting transfers between devices: 6.07 us -> 10 us  [the longest x1 3.57 us: per_device(): high_pot = lax.ppermute(down_pot, 's', back_ring)]
  transfers between devices with their start and end apart: 5 -> 7, of which waited for: 3 -> 3; matrix products, arithmetic and copies ran while one was open for 1% -> 0% of each run, Pallas kernels for 0% -> 0%
where the time goes in v2:
time: 139 us
  blocking collectives  70.3 us (51%)
  Pallas kernels  42.1 us (30%)
  starting transfers between devices  11.2 us (8%)
  waiting for transfers between devices  11 us (8%)
  local copies, waits for them, and re-layouts  1.88 us (1%)
    all_to_all x1, blocking collectives, per_device(): got = lax.all_to_all(sent, ('z', 'gy'), 0, 0, tiled=True)  29.3 us
    pallas_call x1, Pallas kernels, per_device(): call(filter_kernel, f32(group * PAIR * BX * BX, 128), [SMEM] + [VMEM] * 9...  27.1 us
    all_to_all x1, blocking collectives, per_device(): lax.all_to_all(filtered, ('z', 'gy'), 0, 0, tiled=True)  21.3 us
    all_to_all x1, blocking collectives, per_device(): parts = lax.all_to_all(parts, ('s', 'z', 'gy'), 0, 0, tiled=True)  19.7 us
    ppermute x1, waiting for transfers between devices, per_device(): low_pot = lax.ppermute(up_pot, 's', ring)  9.72 us
    pallas_call x1, Pallas kernels, per_device(): call(finish_kernel, (f32(n, BX, BX, 128), f32(n, n)), [VMEM, VMEM])  7.7 us
    pallas_call x1, Pallas kernels, per_device(): call(functools.partial(gram_kernel, 1.0 / cells), f32(devices, 8, 128), [...  4.58 us
    ppermute x1, starting transfers between devices, per_device(): high_pot = lax.ppermute(down_pot, 's', back_ring)  3.57 us
  transfers between devices with their start and end apart: 7, of which 3 were waited for; matrix products, arithmetic and copies ran while one was open for 0% of the time, Pallas kernels for 0%

profile of v2, /device:TPU:1, one launch (start us, length us, event | category | flops | bytes accessed | tf_op | source)
XLA Modules:
  0.0 138.5 jit_solution(11966862080559705348)
XLA Ops:
  0.6 0.8 copy.4
  1.4 1.3 pad_maximum_fusion
  2.8 29.3 %all_to_all.15 = f32[16,2,10,8,128]{4,3,2,1,0:T(8,128)} all-to-all(f32[16,2,10,8,128]{4,3,2,1,0:T(8,128)S(1)} %pad_maximum_fusion), channel_id=1, replica_groups=mesh['s'=8,'z'=4,'gy'=4] {'z','gy'}, dimensions={0} | all-to-all | bytes 2621440 | tf_op jit(solution)/shard_map/all_to_all | solution.py:234
  32.0 2.7 %shard_map.41 = (f32[18,8,8,128]{3,2,1,0:T(8,128)}, f32[18,8,8,128]{3,2,1,0:T(8,128)}, f32[4,8,8,128]{3,2,1,0:T(8,128)}, f32[4,8,8,128]{3,2,1,0:T(8,128)}, f32[8,8,8,128]{3,2,1,0:T(8,128)}) custom-call(f32[2560,128]{1,0:T(8,128)} %bitcast.9), custom_call_target="tpu_custom_call" | custom-call | tf_op jit(solution)/shard_map/pallas_call | solution.py:236
  34.8 1.2 collective-permute-start
  36.0 2.4 %collective-permute-start.1 = (f32[18,8,8,128]{3,2,1,0:T(8,128)}, f32[18,8,8,128]{3,2,1,0:T(8,128)S(1)}, u32[]{:S(2)}, u32[]{:S(2)}) collective-permute-start(f32[18,8,8,128]{3,2,1,0:T(8,128)} %get-tuple-element.8), channel_id=1, source_target_pairs={{16,0},{32,16},{48,32},{64,48},{80,64},{96,80},{112,96},{0,112},{1... | collective-permute-start | bytes 1769480 | tf_op jit(solution)/shard_map/ppermute | solution.py:245
  38.3 0.0 collective-permute-start.2
  38.3 3.6 %collective-permute-start.3 = (f32[4,8,8,128]{3,2,1,0:T(8,128)}, f32[4,8,8,128]{3,2,1,0:T(8,128)S(1)}, u32[]{:S(2)}, u32[]{:S(2)}) collective-permute-start(f32[4,8,8,128]{3,2,1,0:T(8,128)} %get-tuple-element.10), channel_id=1, source_target_pairs={{16,0},{32,16},{48,32},{64,48},{80,64},{96,80},{112,96},{0,112},{1... | collective-permute-start | bytes 393224 | tf_op jit(solution)/shard_map/ppermute | solution.py:243
  41.9 2.1 %collective-permute-start.6 = (f32[8,8,8,128]{3,2,1,0:T(8,128)}, f32[8,8,8,128]{3,2,1,0:T(8,128)S(1)}, u32[]{:S(2)}, u32[]{:S(2)}) collective-permute-start(f32[8,8,8,128]{3,2,1,0:T(8,128)} %get-tuple-element.11.mid_pot), channel_id=1, source_target_pairs={{0,1},{1,0},{2,3},{3,2},{4,5},{5,4},{6,7},{7,6},{8,9},{9,8},{10,11... | collective-permute-start | bytes 786440 | tf_op jit(solution)/shard_map/ppermute | solution.py:246
  44.0 9.7 %collective-permute-done.2.low_pot = f32[4,8,8,128]{3,2,1,0:T(8,128)S(1)} collective-permute-done((f32[4,8,8,128]{3,2,1,0:T(8,128)}, f32[4,8,8,128]{3,2,1,0:T(8,128)S(1)}, u32[]{:S(2)}, u32[]{:S(2)}) %collective-permute-start.2) | collective-permute-done | bytes 131104 | tf_op jit(solution)/shard_map/ppermute | solution.py:242
  53.7 0.0 copy-start.3
  53.7 1.9 %collective-permute-start.4 = (f32[4,8,8,128]{3,2,1,0:T(8,128)S(1)}, f32[4,8,8,128]{3,2,1,0:T(8,128)S(1)}, u32[]{:S(2)}, u32[]{:S(2)}) collective-permute-start(f32[4,8,8,128]{3,2,1,0:T(8,128)S(1)} %collective-permute-done.2.low_pot), channel_id=1, source_target_pairs={{0,1},{1,0},{2,3},{3,2},{4,5},{5,4},{6,7},{7,6},{8,9},{9,8},{10,11... | collective-permute-start | bytes 393224 | tf_op jit(solution)/shard_map/ppermute | solution.py:247
  55.6 0.0 collective-permute-done.3.high_pot
  55.6 0.0 copy-start.4
  55.6 0.1 collective-permute-start.5
  55.7 0.9 collective-permute-done.4.far_low
  56.6 0.0 copy-start.5
  56.6 0.4 collective-permute-done.5.far_high
  57.0 0.0 copy-start.6
  57.0 0.0 collective-permute-done.6.far_mid
  57.0 0.0 copy-start.2
  57.0 0.0 collective-permute-done.low
  57.0 0.0 copy-start
  57.0 0.0 collective-permute-done.1.high
  57.0 0.0 copy-start.1
  57.0 0.0 copy-done.3
  57.0 0.0 copy-done.4
  57.1 0.2 copy-done.5
  57.3 0.4 copy-done.6
  57.6 0.1 copy-done.2
  57.8 0.2 copy-done
  58.0 0.2 copy-done.1
  58.1 27.1 %shard_map.42 = f32[2048,128]{1,0:T(8,128)} custom-call(s32[1]{0:T(128)} %bitcast.core, f32[2560,128]{1,0:T(8,128)} %bitcast.10, f32[18,8,8,128]{3,2,1,0:T(8,128)} %copy-done, f32[18,8,8,128]{3,2,1,0:T(8,128)} %copy-done.1, f32[4,8,8,128]{3,2,1,0:T(8,128)} %copy-done.3, f32[4,8,8,128]{3,2,1,0:T(8,128)} %copy-done.4, ...), custom_call_target="tpu_custom_call" | custom-call | tf_op jit(solution)/shard_map/pallas_call | solution.py:250
  85.2 21.3 %all_to_all.16 = f32[16,2,8,8,128]{4,3,2,1,0:T(8,128)} all-to-all(f32[16,2,8,8,128]{4,3,2,1,0:T(8,128)} %bitcast.13), channel_id=1, replica_groups=mesh['s'=8,'z'=4,'gy'=4] {'z','gy'}, dimensions={0} | all-to-all | bytes 2097152 | tf_op jit(solution)/shard_map/all_to_all | solution.py:262
  106.5 4.6 %shard_map.43 = f32[128,8,128]{2,1,0:T(8,128)} custom-call(f32[32,8,8,128]{3,2,1,0:T(8,128)} %bitcast.11), custom_call_target="tpu_custom_call" | custom-call | tf_op jit(solution)/shard_map/pallas_call | solution.py:265
  111.1 19.7 %all_to_all.17.parts = f32[128,8,128]{2,1,0:T(8,128)} all-to-all(f32[128,8,128]{2,1,0:T(8,128)} %shard_map.43), channel_id=1, replica_groups=mesh['s'=8,'z'=4,'gy'=4] {'s','z','gy'}, dimensions={0} | all-to-all | bytes 1048576 | tf_op jit(solution)/shard_map/all_to_all | solution.py:268
  130.8 7.7 %shard_map.44 = (f32[32,8,8,128]{3,2,1,0:T(8,128)}, f32[32,32]{1,0:T(8,128)}) custom-call(f32[128,8,128]{2,1,0:T(8,128)} %all_to_all.17.parts, f32[32,8,8,128]{3,2,1,0:T(8,128)} %bitcast.12), custom_call_target="tpu_custom_call" | custom-call | tf_op jit(solution)/shard_map/pallas_call | solution.py:269
  (1 shorter events, 0.0 us)
Async XLA Ops:
  34.8 22.2 %collective-permute-start = (f32[18,8,8,128]{3,2,1,0:T(8,128)}, f32[18,8,8,128]{3,2,1,0:T(8,128)S(1)}, u32[]{:S(2)}, u32[]{:S(2)}) collective-permute-start(f32[18,8,8,128]{3,2,1,0:T(8,128)} %get-tuple-element.7), channel_id=1, source_target_pairs={{0,16},{16,32},{32,48},{48,64},{64,80},{80,96},{96,112},{112,0},{1... | collective-permute-start | bytes 1769480 | tf_op jit(solution)/shard_map/ppermute | solution.py:244
  36.0 21.0 %collective-permute-start.1 = (f32[18,8,8,128]{3,2,1,0:T(8,128)}, f32[18,8,8,128]{3,2,1,0:T(8,128)S(1)}, u32[]{:S(2)}, u32[]{:S(2)}) collective-permute-start(f32[18,8,8,128]{3,2,1,0:T(8,128)} %get-tuple-element.8), channel_id=1, source_target_pairs={{16,0},{32,16},{48,32},{64,48},{80,64},{96,80},{112,96},{0,112},{1... | collective-permute-start | bytes 1769480 | tf_op jit(solution)/shard_map/ppermute | solution.py:245
  38.3 15.4 %collective-permute-start.2 = (f32[4,8,8,128]{3,2,1,0:T(8,128)}, f32[4,8,8,128]{3,2,1,0:T(8,128)S(1)}, u32[]{:S(2)}, u32[]{:S(2)}) collective-permute-start(f32[4,8,8,128]{3,2,1,0:T(8,128)} %get-tuple-element.9), channel_id=1, source_target_pairs={{0,16},{16,32},{32,48},{48,64},{64,80},{80,96},{96,112},{112,0},{1... | collective-permute-start | bytes 393224 | tf_op jit(solution)/shard_map/ppermute | solution.py:242
  38.3 17.3 %collective-permute-start.3 = (f32[4,8,8,128]{3,2,1,0:T(8,128)}, f32[4,8,8,128]{3,2,1,0:T(8,128)S(1)}, u32[]{:S(2)}, u32[]{:S(2)}) collective-permute-start(f32[4,8,8,128]{3,2,1,0:T(8,128)} %get-tuple-element.10), channel_id=1, source_target_pairs={{16,0},{32,16},{48,32},{64,48},{80,64},{96,80},{112,96},{0,112},{1... | collective-permute-start | bytes 393224 | tf_op jit(solution)/shard_map/ppermute | solution.py:243
  41.9 15.1 %collective-permute-start.6 = (f32[8,8,8,128]{3,2,1,0:T(8,128)}, f32[8,8,8,128]{3,2,1,0:T(8,128)S(1)}, u32[]{:S(2)}, u32[]{:S(2)}) collective-permute-start(f32[8,8,8,128]{3,2,1,0:T(8,128)} %get-tuple-element.11.mid_pot), channel_id=1, source_target_pairs={{0,1},{1,0},{2,3},{3,2},{4,5},{5,4},{6,7},{7,6},{8,9},{9,8},{10,11... | collective-permute-start | bytes 786440 | tf_op jit(solution)/shard_map/ppermute | solution.py:246
  53.7 3.3 %copy-start.3 = (f32[4,8,8,128]{3,2,1,0:T(8,128)}, f32[4,8,8,128]{3,2,1,0:T(8,128)S(1)}, u32[]{:S(2)}) copy-start(f32[4,8,8,128]{3,2,1,0:T(8,128)S(1)} %collective-permute-done.2.low_pot) | copy-start | bytes 393220
  53.7 2.9 %collective-permute-start.4 = (f32[4,8,8,128]{3,2,1,0:T(8,128)S(1)}, f32[4,8,8,128]{3,2,1,0:T(8,128)S(1)}, u32[]{:S(2)}, u32[]{:S(2)}) collective-permute-start(f32[4,8,8,128]{3,2,1,0:T(8,128)S(1)} %collective-permute-done.2.low_pot), channel_id=1, source_target_pairs={{0,1},{1,0},{2,3},{3,2},{4,5},{5,4},{6,7},{7,6},{8,9},{9,8},{10,11... | collective-permute-start | bytes 393224 | tf_op jit(solution)/shard_map/ppermute | solution.py:247
  55.6 1.4 %copy-start.4 = (f32[4,8,8,128]{3,2,1,0:T(8,128)}, f32[4,8,8,128]{3,2,1,0:T(8,128)S(1)}, u32[]{:S(2)}) copy-start(f32[4,8,8,128]{3,2,1,0:T(8,128)S(1)} %collective-permute-done.3.high_pot) | copy-start | bytes 393220
  55.6 1.3 collective-permute-start.5
  56.6 0.6 copy-start.5
  57.0 0.6 copy-start.6
  57.0 0.8 copy-start.2
  57.0 1.0 copy-start
  57.0 1.1 copy-start.1

commit v3 on v2

--- a/solution.py
+++ b/solution.py
@@ -33,6 +33,7 @@
 PAIR = 2
 BX = 8
 BLOCK = BX + 2
+CHUNK = 4
 SLAB = 4 * BX
 VMEM = pl.BlockSpec(memory_space=pltpu.VMEM)
 SMEM = pl.BlockSpec(memory_space=pltpu.SMEM)
@@ -68,11 +69,37 @@
             field[row, REACH + yi + BX] = pltpu.roll(tiles[yi], 8 - PAIR, 0)
 
 
+def parts_of(v):
+    high = v.astype(jnp.bfloat16)
+    rest = v - high.astype(jnp.float32)
+    middle = rest.astype(jnp.bfloat16)
+    return high, middle, (rest - middle.astype(jnp.float32)).astype(jnp.bfloat16)
+
+
+def band_parts():
+    apart = (iota((128, 128), 0) - iota((128, 128), 1)) % 128
+    band = jnp.zeros((128, 128), jnp.float32)
+    for j in range(1, REACH + 1):
+        band = jnp.where((apart == j) | (apart == 128 - j), coupling[j], band)
+    high, middle, low = parts_of(band)
+    top = jnp.concatenate([high, middle], axis=1)
+    return jnp.concatenate([top, top], axis=0)
+
+
+def band_product(v, bands):
+    high, middle, _ = parts_of(v)
+    both = jnp.dot(
+        jnp.concatenate([high, middle], axis=1), bands, preferred_element_type=jnp.float32
+    )
+    return both[:, :128] + both[:, 128:]
+
+
 def filter_kernel(
     core, got, low, high, low_pot, high_pot, mid_pot, far_low, far_high, far_mid,
-    out, field0, field1, field2, pot,
+    out, field0, field1, field2, pot, far_z,
 ):
     mine = core[0]
+    bands = band_parts()
 
     def edge(i, carry):
         put(field0, i, [low[i, yi] for yi in range(BX)])
@@ -109,42 +136,62 @@
                             row + z * BX + 2 * k, source, 2 * z + k, yi, parity, skip[z]
                         )
 
-    def apply(field, row, pot_row):
-        line = [field[row, e] for e in range(BX + 2 * REACH)]
-        totals = []
-        for yi in range(BX):
-            e = REACH + yi
-            v = line[e]
-            total = pot[pot_row, yi] * v
-            for j in range(1, REACH + 1):
-                near = (field[row + j, e] + field[row - j, e]) + (line[e + j] + line[e - j])
-                near = near + (pltpu.roll(v, j, 1) + pltpu.roll(v, 128 - j, 1))
-                total = total + coupling[j] * near
-            totals.append(total)
+    def along_z(field, start, i):
+        v = field[pl.ds(start, CHUNK), REACH : REACH + BX].reshape(CHUNK * BX * 8, 128)
+        far_z[pl.ds(i, CHUNK)] = band_product(v, bands).reshape(CHUNK, BX, 8, 128)
+
+    def sweep(field, rows, one):
+        along_z(field, REACH, 0)
+
+        def chunk(c, carry):
+            for r in range(0, CHUNK, 2):
+                one(c * CHUNK + r)
+            ahead = (c + 1) * CHUNK
+            along_z(field, REACH + ahead, ahead)
+            return carry
+
+        lax.fori_loop(0, rows // CHUNK, chunk, 0)
+
+    def apply(field, row, pot_row, i):
+        totals = [[], []]
+        for begin in range(0, BX, 4):
+            lines = [
+                [field[row + r, e] for e in range(begin, begin + 4 + 2 * REACH)] for r in range(2)
+            ]
+            for yi in range(begin, begin + 4):
+                e = REACH + yi - begin
+                x = {0: lines[0][e], 1: lines[1][e]}
+                for d in (*range(-REACH, 0), *range(2, REACH + 2)):
+                    x[d] = field[row + d, REACH + yi]
+                for r in range(2):
+                    line = lines[r]
+                    total = pot[pot_row + r, yi] * line[e] + far_z[i + r, yi]
+                    for j in range(1, REACH + 1):
+                        near = (x[r + j] + x[r - j]) + (line[e + j] + line[e - j])
+                        total = total + coupling[j] * near
+                    totals[r].append(total)
         return totals
 
-    def first(i, carry):
-        put(field1, i, apply(field0, i + REACH, i))
-        return carry
-
-    lax.fori_loop(0, SLAB + 2 * FLAT, first, 0)
-
-    def second(i, carry):
-        ts = apply(field1, i + REACH, i + REACH)
-        put(field2, i, [t + t - field0[i + FLAT, REACH + yi] for yi, t in enumerate(ts)])
-        return carry
-
-    lax.fori_loop(0, SLAB + FLAT, second, 0)
-
-    for z in range(4):
-        def third(xi, carry, z=z):
-            i = z * BX + xi
-            for yi, t in enumerate(apply(field2, i + REACH, i + FLAT)):
-                start = (z * 4 * PAIR * BX + xi) * BX + yi
-                out[pl.ds(start, 8, stride=BX * BX), :] = t + t - field1[i + FLAT, REACH + yi]
-            return carry
-
-        lax.fori_loop(0, BX, third, 0)
+    def first(i):
+        for r, ts in enumerate(apply(field0, i + REACH, i, i)):
+            put(field1, i + r, ts)
+
+    def second(i):
+        for r, ts in enumerate(apply(field1, i + REACH, i + REACH, i)):
+            before = i + r + FLAT
+            put(field2, i + r, [t + t - field0[before, REACH + yi] for yi, t in enumerate(ts)])
+
+    def third(i):
+        for r, ts in enumerate(apply(field2, i + REACH, i + FLAT, i)):
+            for yi, t in enumerate(ts):
+                start = ((i // BX) * 4 * PAIR * BX + i % BX + r) * BX + yi
+                out[pl.ds(start, 8, stride=BX * BX), :] = (
+                    t + t - field1[i + r + FLAT, REACH + yi]
+                )
+
+    sweep(field0, SLAB + 2 * FLAT, first)
+    sweep(field1, SLAB + FLAT, second)
+    sweep(field2, SLAB, third)
 
 
 def iota(shape, dim):
@@ -167,11 +214,16 @@
     )
 
 
+def pair_of_rows(y, x):
+    rows = y.shape[0] * BX
+    return jnp.concatenate([y[:, x].reshape(rows, 128), y[:, x + 1].reshape(rows, 128)], axis=1)
+
+
 def gram_kernel(scale, y, out):
     n = y.shape[0]
     total = None
-    for x in range(BX):
-        block = y[:, x].reshape(n * BX, 128)
+    for x in range(0, BX, 2):
+        block = pair_of_rows(y, x)
         part = dot(block, block, ((1,), (1,)))
         total = part if total is None else total + part
     total = jnp.where(same_y(n), total, 0.0) * scale
@@ -200,18 +252,20 @@
     mixer = done[:, n : 2 * n]
     ones = spread(n)
     wide_mixer = jnp.where(same_y(n), dot(dot(ones, mixer), ones, ((1,), (1,))), 0.0)
-    for x in range(BX):
-        block = y[:, x].reshape(n * BX, 128)
-        out[:, x] = dot(wide_mixer, block).reshape(n, BX, 128)
-
-
-def call(kernel, out_shape, in_specs, scratch=(), flops=0, moved=0):
+    for x in range(0, BX, 2):
+        mixed = dot(wide_mixer, pair_of_rows(y, x))
+        out[:, x] = mixed[:, :128].reshape(n, BX, 128)
+        out[:, x + 1] = mixed[:, 128:].reshape(n, BX, 128)
+
+
+def call(kernel, out_shape, in_specs, scratch=(), limit=8, flops=0, moved=0):
     return pl.pallas_call(
         kernel,
         out_shape=out_shape,
         in_specs=in_specs,
         out_specs=jax.tree.map(lambda _: VMEM, out_shape),
         scratch_shapes=list(scratch),
+        compiler_params=pltpu.CompilerParams(vmem_limit_bytes=limit << 20),
         cost_estimate=pl.CostEstimate(flops=flops, bytes_accessed=moved, transcendentals=0),
     )
 
@@ -256,7 +310,9 @@
             pltpu.VMEM((SLAB + 2 * FLAT, wide, 8, 128), jnp.float32),
             pltpu.VMEM((SLAB + FLAT, wide, 8, 128), jnp.float32),
             pltpu.VMEM((SLAB + 2 * FLAT, BX, 8, 128), jnp.float32),
+            pltpu.VMEM((SLAB + 2 * FLAT + CHUNK, BX, 8, 128), jnp.float32),
         ],
+        32,
     )(core.reshape(1), got, low, high, low_pot, high_pot, mid_pot, far_low, far_high, far_mid)
     filtered = filtered.reshape(group, PAIR, BX, BX, 128)
     back = lax.all_to_all(filtered, ("z", "gy"), 0, 0, tiled=True).reshape(n, BX, BX, 128)

time: 139 us -> 113 us (0.81)
  Pallas kernels: 42.1 us -> 19 us
  blocking collectives: 70.3 us -> 68.5 us
    pallas_call x1, Pallas kernels: 27.1 us -> 10.3 us  [per_device(): call(filter_kernel, f32(group * PAIR * BX * BX, 128), [SMEM] + [VMEM] * 9...]
    pallas_call x1, Pallas kernels: 4.58 us -> 1.79 us  [per_device(): call(functools.partial(gram_kernel, 1.0 / cells), f32(devices, 8, 128), [...]
    pallas_call x1, Pallas kernels: 7.7 us -> 5.51 us  [per_device(): call(finish_kernel, (f32(n, BX, BX, 128), f32(n, n)), [VMEM, VMEM])]
where the time goes in v3:
time: 113 us
  blocking collectives  68.5 us (61%)
  Pallas kernels  19 us (17%)
  starting transfers between devices  11.2 us (10%)
  waiting for transfers between devices  11.1 us (10%)
  other arithmetic  1.34 us (1%)
    all_to_all x1, blocking collectives, per_device(): got = lax.all_to_all(sent, ('z', 'gy'), 0, 0, tiled=True)  29.2 us
    all_to_all x1, blocking collectives, per_device(): lax.all_to_all(filtered, ('z', 'gy'), 0, 0, tiled=True)  20 us
    all_to_all x1, blocking collectives, per_device(): parts = lax.all_to_all(parts, ('s', 'z', 'gy'), 0, 0, tiled=True)  19.3 us
    pallas_call x1, Pallas kernels, per_device(): call(filter_kernel, f32(group * PAIR * BX * BX, 128), [SMEM] + [VMEM] * 9...  10.3 us
    ppermute x1, waiting for transfers between devices, per_device(): low_pot = lax.ppermute(up_pot, 's', ring)  9.72 us
    pallas_call x1, Pallas kernels, per_device(): call(finish_kernel, (f32(n, BX, BX, 128), f32(n, n)), [VMEM, VMEM])  5.51 us
    ppermute x1, starting transfers between devices, per_device(): high_pot = lax.ppermute(down_pot, 's', back_ring)  3.57 us
    ppermute x1, starting transfers between devices, per_device(): high = lax.ppermute(down, 's', back_ring)  2.36 us
  transfers between devices with their start and end apart: 7, of which 3 were waited for; matrix products, arithmetic and copies ran while one was open for 0% of the time, Pallas kernels for 0%

profile of v3, /device:TPU:1, one launch (start us, length us, event | category | flops | bytes accessed | tf_op | source)
XLA Modules:
  0.0 112.5 jit_solution(1341258097850861444)
XLA Ops:
  0.6 0.8 copy.4
  1.4 1.3 %pad_maximum_fusion = f32[16,2,10,8,128]{4,3,2,1,0:T(8,128)S(1)} fusion(f32[16,2,2,8,128]{4,3,2,1,0:T(8,128)S(1)} %bitcast.14, f32[16,2,8,8,128]{4,3,2,1,0:T(8,128)} %bitcast.15), kind=kLoop, calls=%fused_computation | loop fusion | flops 327680 | bytes 2621440 | tf_op jit(solution)/shard_map/concatenate | solution.py:284
  2.8 29.2 %all_to_all.15 = f32[16,2,10,8,128]{4,3,2,1,0:T(8,128)S(1)} all-to-all(f32[16,2,10,8,128]{4,3,2,1,0:T(8,128)S(1)} %pad_maximum_fusion), channel_id=1, replica_groups=mesh['s'=8,'z'=4,'gy'=4] {'z','gy'}, dimensions={0} | all-to-all | bytes 2621440 | tf_op jit(solution)/shard_map/all_to_all | solution.py:288
  31.9 1.5 %shard_map.41 = (f32[18,8,8,128]{3,2,1,0:T(8,128)}, f32[18,8,8,128]{3,2,1,0:T(8,128)}, f32[4,8,8,128]{3,2,1,0:T(8,128)S(1)}, f32[4,8,8,128]{3,2,1,0:T(8,128)S(1)}, f32[8,8,8,128]{3,2,1,0:T(8,128)S(1)}) custom-call(f32[2560,128]{1,0:T(8,128)S(1)} %bitcast.9), custom_call_target="tpu_custom_call" | custom-call | tf_op jit(solution)/shard_map/pallas_call | solution.py:290
  33.4 1.2 %collective-permute-start = (f32[18,8,8,128]{3,2,1,0:T(8,128)}, f32[18,8,8,128]{3,2,1,0:T(8,128)S(1)}, u32[]{:S(2)}, u32[]{:S(2)}) collective-permute-start(f32[18,8,8,128]{3,2,1,0:T(8,128)} %get-tuple-element.7), channel_id=1, source_target_pairs={{0,16},{16,32},{32,48},{48,64},{64,80},{80,96},{96,112},{112,0},{1... | collective-permute-start | bytes 1769480 | tf_op jit(solution)/shard_map/ppermute | solution.py:298
  34.6 2.4 %collective-permute-start.1 = (f32[18,8,8,128]{3,2,1,0:T(8,128)}, f32[18,8,8,128]{3,2,1,0:T(8,128)S(1)}, u32[]{:S(2)}, u32[]{:S(2)}) collective-permute-start(f32[18,8,8,128]{3,2,1,0:T(8,128)} %get-tuple-element.8), channel_id=1, source_target_pairs={{16,0},{32,16},{48,32},{64,48},{80,64},{96,80},{112,96},{0,112},{1... | collective-permute-start | bytes 1769480 | tf_op jit(solution)/shard_map/ppermute | solution.py:299
  37.0 0.0 collective-permute-start.2
  37.0 3.6 %collective-permute-start.3 = (f32[4,8,8,128]{3,2,1,0:T(8,128)S(1)}, f32[4,8,8,128]{3,2,1,0:T(8,128)S(1)}, u32[]{:S(2)}, u32[]{:S(2)}) collective-permute-start(f32[4,8,8,128]{3,2,1,0:T(8,128)S(1)} %get-tuple-element.10), channel_id=1, source_target_pairs={{16,0},{32,16},{48,32},{64,48},{80,64},{96,80},{112,96},{0,112},{1... | collective-permute-start | bytes 393224 | tf_op jit(solution)/shard_map/ppermute | solution.py:297
  40.5 2.1 %collective-permute-start.6 = (f32[8,8,8,128]{3,2,1,0:T(8,128)S(1)}, f32[8,8,8,128]{3,2,1,0:T(8,128)S(1)}, u32[]{:S(2)}, u32[]{:S(2)}) collective-permute-start(f32[8,8,8,128]{3,2,1,0:T(8,128)S(1)} %get-tuple-element.11.mid_pot), channel_id=1, source_target_pairs={{0,1},{1,0},{2,3},{3,2},{4,5},{5,4},{6,7},{7,6},{8,9},{9,8},{10,11... | collective-permute-start | bytes 786440 | tf_op jit(solution)/shard_map/ppermute | solution.py:300
  42.6 9.7 %collective-permute-done.2.low_pot = f32[4,8,8,128]{3,2,1,0:T(8,128)S(1)} collective-permute-done((f32[4,8,8,128]{3,2,1,0:T(8,128)S(1)}, f32[4,8,8,128]{3,2,1,0:T(8,128)S(1)}, u32[]{:S(2)}, u32[]{:S(2)}) %collective-permute-start.2) | collective-permute-done | bytes 131104 | tf_op jit(solution)/shard_map/ppermute | solution.py:296
  52.4 1.9 %collective-permute-start.4 = (f32[4,8,8,128]{3,2,1,0:T(8,128)S(1)}, f32[4,8,8,128]{3,2,1,0:T(8,128)S(1)}, u32[]{:S(2)}, u32[]{:S(2)}) collective-permute-start(f32[4,8,8,128]{3,2,1,0:T(8,128)S(1)} %collective-permute-done.2.low_pot), channel_id=1, source_target_pairs={{0,1},{1,0},{2,3},{3,2},{4,5},{5,4},{6,7},{7,6},{8,9},{9,8},{10,11... | collective-permute-start | bytes 393224 | tf_op jit(solution)/shard_map/ppermute | solution.py:301
  54.3 0.0 collective-permute-done.3.high_pot
  54.3 0.0 collective-permute-start.5
  54.3 1.0 collective-permute-done.4.far_low
  55.3 0.4 collective-permute-done.5.far_high
  55.6 0.0 collective-permute-done.6.far_mid
  55.6 0.0 collective-permute-done.low
  55.6 0.0 collective-permute-done.1.high
  55.6 10.3 %shard_map.42 = f32[2048,128]{1,0:T(8,128)S(1)} custom-call(s32[1]{0:T(128)} %bitcast.core, f32[2560,128]{1,0:T(8,128)S(1)} %bitcast.10, f32[18,8,8,128]{3,2,1,0:T(8,128)S(1)} %collective-permute-done.low, f32[18,8,8,128]{3,2,1,0:T(8,128)S(1)} %collective-permute-done.1.high, f32[4,8,8,128]{3,2,1,0:T(8,128)S(1)} %collective-permute-done.2.low_pot, ...), custom_call_target="tpu_custom_call" | custom-call | tf_op jit(solution)/shard_map/pallas_call | solution.py:304
  65.9 20.0 %all_to_all.16 = f32[16,2,8,8,128]{4,3,2,1,0:T(8,128)S(1)} all-to-all(f32[16,2,8,8,128]{4,3,2,1,0:T(8,128)S(1)} %bitcast.13), channel_id=1, replica_groups=mesh['s'=8,'z'=4,'gy'=4] {'z','gy'}, dimensions={0} | all-to-all | bytes 2097152 | tf_op jit(solution)/shard_map/all_to_all | solution.py:318
  85.9 1.8 %shard_map.43 = f32[128,8,128]{2,1,0:T(8,128)S(1)} custom-call(f32[32,8,8,128]{3,2,1,0:T(8,128)S(1)} %bitcast.11), custom_call_target="tpu_custom_call" | custom-call | tf_op jit(solution)/shard_map/pallas_call | solution.py:321
  87.7 19.3 %all_to_all.17.parts = f32[128,8,128]{2,1,0:T(8,128)S(1)} all-to-all(f32[128,8,128]{2,1,0:T(8,128)S(1)} %shard_map.43), channel_id=1, replica_groups=mesh['s'=8,'z'=4,'gy'=4] {'s','z','gy'}, dimensions={0} | all-to-all | bytes 1048576 | tf_op jit(solution)/shard_map/all_to_all | solution.py:324
  107.0 5.5 %shard_map.44 = (f32[32,8,8,128]{3,2,1,0:T(8,128)}, f32[32,32]{1,0:T(8,128)}) custom-call(f32[128,8,128]{2,1,0:T(8,128)S(1)} %all_to_all.17.parts, f32[32,8,8,128]{3,2,1,0:T(8,128)S(1)} %bitcast.12), custom_call_target="tpu_custom_call" | custom-call | tf_op jit(solution)/shard_map/pallas_call | solution.py:325
  (1 shorter events, 0.0 us)
Async XLA Ops:
  33.4 22.2 %collective-permute-start = (f32[18,8,8,128]{3,2,1,0:T(8,128)}, f32[18,8,8,128]{3,2,1,0:T(8,128)S(1)}, u32[]{:S(2)}, u32[]{:S(2)}) collective-permute-start(f32[18,8,8,128]{3,2,1,0:T(8,128)} %get-tuple-element.7), channel_id=1, source_target_pairs={{0,16},{16,32},{32,48},{48,64},{64,80},{80,96},{96,112},{112,0},{1... | collective-permute-start | bytes 1769480 | tf_op jit(solution)/shard_map/ppermute | solution.py:298
  34.6 21.0 %collective-permute-start.1 = (f32[18,8,8,128]{3,2,1,0:T(8,128)}, f32[18,8,8,128]{3,2,1,0:T(8,128)S(1)}, u32[]{:S(2)}, u32[]{:S(2)}) collective-permute-start(f32[18,8,8,128]{3,2,1,0:T(8,128)} %get-tuple-element.8), channel_id=1, source_target_pairs={{16,0},{32,16},{48,32},{64,48},{80,64},{96,80},{112,96},{0,112},{1... | collective-permute-start | bytes 1769480 | tf_op jit(solution)/shard_map/ppermute | solution.py:299
  37.0 15.4 %collective-permute-start.2 = (f32[4,8,8,128]{3,2,1,0:T(8,128)S(1)}, f32[4,8,8,128]{3,2,1,0:T(8,128)S(1)}, u32[]{:S(2)}, u32[]{:S(2)}) collective-permute-start(f32[4,8,8,128]{3,2,1,0:T(8,128)S(1)} %get-tuple-element.9), channel_id=1, source_target_pairs={{0,16},{16,32},{32,48},{48,64},{64,80},{80,96},{96,112},{112,0},{1... | collective-permute-start | bytes 393224 | tf_op jit(solution)/shard_map/ppermute | solution.py:296
  37.0 17.3 %collective-permute-start.3 = (f32[4,8,8,128]{3,2,1,0:T(8,128)S(1)}, f32[4,8,8,128]{3,2,1,0:T(8,128)S(1)}, u32[]{:S(2)}, u32[]{:S(2)}) collective-permute-start(f32[4,8,8,128]{3,2,1,0:T(8,128)S(1)} %get-tuple-element.10), channel_id=1, source_target_pairs={{16,0},{32,16},{48,32},{64,48},{80,64},{96,80},{112,96},{0,112},{1... | collective-permute-start | bytes 393224 | tf_op jit(solution)/shard_map/ppermute | solution.py:297
  40.5 15.1 %collective-permute-start.6 = (f32[8,8,8,128]{3,2,1,0:T(8,128)S(1)}, f32[8,8,8,128]{3,2,1,0:T(8,128)S(1)}, u32[]{:S(2)}, u32[]{:S(2)}) collective-permute-start(f32[8,8,8,128]{3,2,1,0:T(8,128)S(1)} %get-tuple-element.11.mid_pot), channel_id=1, source_target_pairs={{0,1},{1,0},{2,3},{3,2},{4,5},{5,4},{6,7},{7,6},{8,9},{9,8},{10,11... | collective-permute-start | bytes 786440 | tf_op jit(solution)/shard_map/ppermute | solution.py:300
  52.4 2.9 %collective-permute-start.4 = (f32[4,8,8,128]{3,2,1,0:T(8,128)S(1)}, f32[4,8,8,128]{3,2,1,0:T(8,128)S(1)}, u32[]{:S(2)}, u32[]{:S(2)}) collective-permute-start(f32[4,8,8,128]{3,2,1,0:T(8,128)S(1)} %collective-permute-done.2.low_pot), channel_id=1, source_target_pairs={{0,1},{1,0},{2,3},{3,2},{4,5},{5,4},{6,7},{7,6},{8,9},{9,8},{10,11... | collective-permute-start | bytes 393224 | tf_op jit(solution)/shard_map/ppermute | solution.py:301
  54.3 1.3 %collective-permute-start.5 = (f32[4,8,8,128]{3,2,1,0:T(8,128)S(1)}, f32[4,8,8,128]{3,2,1,0:T(8,128)S(1)}, u32[]{:S(2)}, u32[]{:S(2)}) collective-permute-start(f32[4,8,8,128]{3,2,1,0:T(8,128)S(1)} %collective-permute-done.3.high_pot), channel_id=1, source_target_pairs={{0,1},{1,0},{2,3},{3,2},{4,5},{5,4},{6,7},{7,6},{8,9},{9,8},{10,11... | collective-permute-start | bytes 393224 | tf_op jit(solution)/shard_map/ppermute | solution.py:302

commit v4 on v3

--- a/solution.py
+++ b/solution.py
@@ -30,10 +30,10 @@
 REACH = 6
 DEEP = 3 * REACH
 FLAT = 2 * REACH
+STEP = 4
 PAIR = 2
 BX = 8
 BLOCK = BX + 2
-CHUNK = 4
 SLAB = 4 * BX
 VMEM = pl.BlockSpec(memory_space=pltpu.VMEM)
 SMEM = pl.BlockSpec(memory_space=pltpu.SMEM)
@@ -62,11 +62,13 @@
 
 def put(field, row, tiles):
     for yi in range(BX):
-        field[row, REACH + yi] = tiles[yi]
-        if yi >= BX - REACH:
-            field[row, REACH + yi - BX] = pltpu.roll(tiles[yi], PAIR, 0)
-        if yi < REACH:
-            field[row, REACH + yi + BX] = pltpu.roll(tiles[yi], 8 - PAIR, 0)
+        field[row, yi, 0:8] = tiles[yi]
+        field[row, yi, 8:16] = tiles[yi]
+
+
+def take(field, row, yi):
+    first = 8 - PAIR if yi < 0 else PAIR if yi >= BX else 0
+    return field[row, yi % BX, first : first + 8]
 
 
 def parts_of(v):
@@ -136,33 +138,36 @@
                             row + z * BX + 2 * k, source, 2 * z + k, yi, parity, skip[z]
                         )
 
-    def along_z(field, start, i):
-        v = field[pl.ds(start, CHUNK), REACH : REACH + BX].reshape(CHUNK * BX * 8, 128)
-        far_z[pl.ds(i, CHUNK)] = band_product(v, bands).reshape(CHUNK, BX, 8, 128)
-
-    def sweep(field, rows, one):
-        along_z(field, REACH, 0)
+    def along_z(field, start, i, count):
+        v = field[pl.ds(start, count), :, 0:8].reshape(count * BX * 8, 128)
+        far_z[pl.ds(i, count)] = band_product(v, bands).reshape(count, BX, 8, 128)
+
+    def sweep(field, rows, count, one):
+        along_z(field, REACH, 0, count)
 
         def chunk(c, carry):
-            for r in range(0, CHUNK, 2):
-                one(c * CHUNK + r)
-            ahead = (c + 1) * CHUNK
-            along_z(field, REACH + ahead, ahead)
+            for r in range(0, count, 2):
+                one(c * count + r)
+            ahead = (c + 1) * count
+            along_z(field, REACH + ahead, ahead, count)
             return carry
 
-        lax.fori_loop(0, rows // CHUNK, chunk, 0)
+        lax.fori_loop(0, rows // count - 1, chunk, 0)
+        for r in range(rows - count, rows, 2):
+            one(r)
 
     def apply(field, row, pot_row, i):
         totals = [[], []]
         for begin in range(0, BX, 4):
             lines = [
-                [field[row + r, e] for e in range(begin, begin + 4 + 2 * REACH)] for r in range(2)
+                [take(field, row + r, y) for y in range(begin - REACH, begin + 4 + REACH)]
+                for r in range(2)
             ]
             for yi in range(begin, begin + 4):
                 e = REACH + yi - begin
                 x = {0: lines[0][e], 1: lines[1][e]}
                 for d in (*range(-REACH, 0), *range(2, REACH + 2)):
-                    x[d] = field[row + d, REACH + yi]
+                    x[d] = take(field, row + d, yi)
                 for r in range(2):
                     line = lines[r]
                     total = pot[pot_row + r, yi] * line[e] + far_z[i + r, yi]
@@ -179,19 +184,19 @@
     def second(i):
         for r, ts in enumerate(apply(field1, i + REACH, i + REACH, i)):
             before = i + r + FLAT
-            put(field2, i + r, [t + t - field0[before, REACH + yi] for yi, t in enumerate(ts)])
+            put(field2, i + r, [t + t - take(field0, before, yi) for yi, t in enumerate(ts)])
 
     def third(i):
         for r, ts in enumerate(apply(field2, i + REACH, i + FLAT, i)):
             for yi, t in enumerate(ts):
                 start = ((i // BX) * 4 * PAIR * BX + i % BX + r) * BX + yi
                 out[pl.ds(start, 8, stride=BX * BX), :] = (
-                    t + t - field1[i + r + FLAT, REACH + yi]
+                    t + t - take(field1, i + r + FLAT, yi)
                 )
 
-    sweep(field0, SLAB + 2 * FLAT, first)
-    sweep(field1, SLAB + FLAT, second)
-    sweep(field2, SLAB, third)
+    sweep(field0, SLAB + 2 * FLAT, 14, first)
+    sweep(field1, SLAB + FLAT, 22, second)
+    sweep(field2, SLAB, 16, third)
 
 
 def iota(shape, dim):
@@ -229,29 +234,81 @@
     total = jnp.where(same_y(n), total, 0.0) * scale
     ones = spread(n)
     gram = dot(dot(ones, total, ((0,), (0,))), ones)
-    wide = jnp.concatenate([gram[8 * k : 8 * k + 8] for k in range(n // 8)], axis=1)
-    for d in range(out.shape[0]):
-        out[d] = wide
+    half = n // 2
+    upper = iota((half, half), 0) <= iota((half, half), 1)
+    kept = jnp.concatenate(
+        [jnp.where(upper, gram[:half, :half], gram[half:, half:]), gram[:half, half:]], axis=1
+    )
+    unit = iota((half, half), 0) == iota((half, half), 1)
+    ends = jnp.sum(jnp.where(unit, gram[half:, half:], 0.0), axis=0, keepdims=True)
+    ends = jnp.concatenate([ends, jnp.zeros((1, 128 - half), jnp.float32)], axis=1)
+    rows = jnp.concatenate([kept[4 * k : 4 * k + 4] for k in range(4)], axis=1)
+    rows = jnp.concatenate([rows, ends], axis=0)
+    for d in range(out.shape[0] // 5):
+        out[5 * d : 5 * d + 5] = rows
 
 
 def finish_kernel(parts, y, out, factor):
     n = y.shape[0]
-    wide = jnp.sum(parts[...], axis=0)
-    gram = jnp.concatenate([wide[:, n * k : n * k + n] for k in range(n // 8)], axis=0)
+    half = n // 2
+    rows = []
+    for r in range(5):
+        total = None
+        for d in range(0, parts.shape[0] // 5, 8):
+            tile = parts[pl.ds(5 * d + r, 8, stride=5), :]
+            total = tile if total is None else total + tile
+        rows.append(jnp.sum(total, axis=0, keepdims=True))
+    rows = jnp.concatenate(rows, axis=0)
+    kept = jnp.concatenate([rows[:4, n * k : n * k + n] for k in range(4)], axis=0)
+    across = kept[:, half:]
+    unit = iota((half, half), 0) == iota((half, half), 1)
+    upper = iota((half, half), 0) < iota((half, half), 1)
+    mixed = kept[:, :half]
+    turned = mixed.T
+    first = jnp.where(upper | unit, mixed, turned)
+    last = jnp.where(upper, turned, mixed)
+    last = jnp.where(unit, jnp.broadcast_to(rows[4:5, :half], (half, half)), last)
+    gram = jnp.concatenate(
+        [jnp.concatenate([first, across], axis=1), jnp.concatenate([across.T, last], axis=1)],
+        axis=0,
+    )
     unit = (iota((n, n), 0) == iota((n, n), 1)).astype(jnp.float32)
     left = jnp.concatenate([gram, unit, jnp.zeros((n, 128 - 2 * n), jnp.float32)], axis=1)
     row_of = iota((n, 128), 0)
-    done = jnp.zeros((n, 128), jnp.float32)
-    for k in range(n):
-        inverse = lax.rsqrt(left[k : k + 1, k : k + 1])
-        row = left[k : k + 1] * inverse
-        column = left[:, k : k + 1] * inverse
-        done = jnp.where(row_of == k, row, done)
-        left = left - jnp.where(row_of > k, column, 0.0) * row
+    finished = []
+    for k in range(0, n, STEP):
+        entry = {
+            (i, j): jnp.broadcast_to(left[k + i : k + i + 1, k + j : k + j + 1], (1, 128))
+            for i in range(STEP)
+            for j in range(i + 1)
+        }
+        columns = [
+            jnp.broadcast_to(left[:, k + j : k + j + 1], (n, 128)) for j in range(STEP)
+        ]
+        lines = [left[k + j : k + j + 1] for j in range(STEP)]
+        for j in range(STEP):
+            inverse = lax.rsqrt(entry[j, j])
+            lines[j] = lines[j] * inverse
+            columns[j] = columns[j] * inverse
+            for i in range(j + 1, STEP):
+                entry[i, j] = entry[i, j] * inverse
+            for i in range(j + 1, STEP):
+                for m in range(j + 1, i + 1):
+                    entry[i, m] = entry[i, m] - entry[i, j] * entry[m, j]
+                lines[i] = lines[i] - entry[i, j] * lines[j]
+                columns[i] = columns[i] - entry[i, j] * columns[j]
+        finished += lines
+        change = None
+        for line, column in zip(lines, columns):
+            part = column * line
+            change = part if change is None else change + part
+        left = jnp.where(row_of >= k + STEP, left - change, left)
+    done = jnp.concatenate(finished, axis=0)
     factor[...] = jnp.where(iota((n, n), 0) <= iota((n, n), 1), done[:, :n], 0.0)
     mixer = done[:, n : 2 * n]
     ones = spread(n)
-    wide_mixer = jnp.where(same_y(n), dot(dot(ones, mixer), ones, ((1,), (1,))), 0.0)
+    tall = jnp.broadcast_to(mixer[:, None], (n, BX, n)).reshape(n * BX, n)
+    wide_mixer = jnp.where(same_y(n), dot(tall, ones, ((1,), (1,))), 0.0)
     for x in range(0, BX, 2):
         mixed = dot(wide_mixer, pair_of_rows(y, x))
         out[:, x] = mixed[:, :128].reshape(n, BX, 128)
@@ -278,7 +335,7 @@
     n = orbitals.shape[0]
     slabs = lax.axis_size("s")
     group = lax.axis_size("z") * lax.axis_size("gy")
-    core = lax.axis_index("gy") % 2
+    core = lax.axis_index("gy") & 1
     halves = potential.reshape(2, 2, 2, BX, 128).transpose(2, 0, 1, 3, 4)
     halves = jnp.broadcast_to(halves[None], (group // 2, 2, PAIR, 2, BX, 128))
     sent = jnp.concatenate(
@@ -300,17 +357,16 @@
     far_mid = lax.ppermute(mid_pot, "gy", twin)
     far_low = lax.ppermute(low_pot, "gy", twin)
     far_high = lax.ppermute(high_pot, "gy", twin)
-    wide = BX + 2 * REACH
     filtered = call(
         filter_kernel,
         f32(group * PAIR * BX * BX, 128),
         [SMEM] + [VMEM] * 9,
         [
-            pltpu.VMEM((SLAB + 2 * DEEP, wide, 8, 128), jnp.float32),
-            pltpu.VMEM((SLAB + 2 * FLAT, wide, 8, 128), jnp.float32),
-            pltpu.VMEM((SLAB + FLAT, wide, 8, 128), jnp.float32),
+            pltpu.VMEM((SLAB + 2 * DEEP, BX, 16, 128), jnp.float32),
+            pltpu.VMEM((SLAB + 2 * FLAT, BX, 16, 128), jnp.float32),
+            pltpu.VMEM((SLAB + FLAT, BX, 16, 128), jnp.float32),
             pltpu.VMEM((SLAB + 2 * FLAT, BX, 8, 128), jnp.float32),
-            pltpu.VMEM((SLAB + 2 * FLAT + CHUNK, BX, 8, 128), jnp.float32),
+            pltpu.VMEM((SLAB + 2 * FLAT, BX, 8, 128), jnp.float32),
         ],
         32,
     )(core.reshape(1), got, low, high, low_pot, high_pot, mid_pot, far_low, far_high, far_mid)
@@ -319,9 +375,11 @@
     devices = slabs * group
     cells = float(devices * BX * BX * 128)
     parts = call(
-        functools.partial(gram_kernel, 1.0 / cells), f32(devices, 8, 128), [VMEM]
+        functools.partial(gram_kernel, 1.0 / cells), f32(devices * 5, 128), [VMEM]
     )(back)
-    parts = lax.all_to_all(parts, ("s", "z", "gy"), 0, 0, tiled=True)
+    parts = lax.all_to_all(
+        parts.reshape(devices, 1, 5 * 128), ("s", "z", "gy"), 0, 0, tiled=True
+    ).reshape(devices * 5, 128)
     return call(finish_kernel, (f32(n, BX, BX, 128), f32(n, n)), [VMEM, VMEM])(parts, back)
 
 

time: 113 us -> 108 us (0.956)
  Pallas kernels: 19 us -> 15.7 us
  blocking collectives: 68.5 us -> 66.6 us
    pallas_call x1, Pallas kernels: 5.51 us -> 3.43 us  [per_device(): call(finish_kernel, (f32(n, BX, BX, 128), f32(n, n)), [VMEM, VMEM])]
    all_to_all x1, blocking collectives: 19.3 us -> 17.4 us  [per_device(): lax.all_to_all(parts.reshape(devices, 1, 5 * 128), ('s', 'z', 'gy'), 0, 0...]
    pallas_call x1, Pallas kernels: 10.3 us -> 8.95 us  [per_device(): call(filter_kernel, f32(group * PAIR * BX * BX, 128), [SMEM] + [VMEM] * 9...]
where the time goes in v4:
time: 108 us; the launch traced here: 107 us
  blocking collectives  66.6 us (62%)
  Pallas kernels  15.7 us (15%)
  starting transfers between devices  11.2 us (10%)
  waiting for transfers between devices  11.1 us (10%)
  other arithmetic  1.34 us (1%)
    all_to_all x1, blocking collectives, per_device(): got = lax.all_to_all(sent, ('z', 'gy'), 0, 0, tiled=True)  29.2 us
    all_to_all x1, blocking collectives, per_device(): lax.all_to_all(filtered, ('z', 'gy'), 0, 0, tiled=True)  19.9 us
    all_to_all x1, blocking collectives, per_device(): lax.all_to_all(parts.reshape(devices, 1, 5 * 128), ('s', 'z', 'gy'), 0, 0...  17.4 us
    ppermute x1, waiting for transfers between devices, per_device(): low_pot = lax.ppermute(up_pot, 's', ring)  9.72 us
    pallas_call x1, Pallas kernels, per_device(): call(filter_kernel, f32(group * PAIR * BX * BX, 128), [SMEM] + [VMEM] * 9...  8.95 us
    ppermute x1, starting transfers between devices, per_device(): high_pot = lax.ppermute(down_pot, 's', back_ring)  3.57 us
    pallas_call x1, Pallas kernels, per_device(): call(finish_kernel, (f32(n, BX, BX, 128), f32(n, n)), [VMEM, VMEM])  3.43 us
    ppermute x1, starting transfers between devices, per_device(): high = lax.ppermute(down, 's', back_ring)  2.36 us
  transfers between devices with their start and end apart: 7, of which 3 were waited for; matrix products, arithmetic and copies ran while one was open for 0% of the time, Pallas kernels for 0%

profile of v4, /device:TPU:1, one launch (start us, length us, event | category | flops | bytes accessed | tf_op | source)
XLA Modules:
  0.0 107.3 jit_solution(18007440860910734244)
XLA Ops:
  0.6 0.8 copy.5
  1.4 1.3 %pad_maximum_fusion = f32[16,2,10,8,128]{4,3,2,1,0:T(8,128)S(1)} fusion(f32[16,2,2,8,128]{4,3,2,1,0:T(8,128)S(1)} %bitcast.18, f32[16,2,8,8,128]{4,3,2,1,0:T(8,128)} %bitcast.19), kind=kLoop, calls=%fused_computation | loop fusion | flops 327680 | bytes 2621440 | tf_op jit(solution)/shard_map/concatenate | solution.py:341
  2.8 29.2 %all_to_all.15 = f32[16,2,10,8,128]{4,3,2,1,0:T(8,128)S(1)} all-to-all(f32[16,2,10,8,128]{4,3,2,1,0:T(8,128)S(1)} %pad_maximum_fusion), channel_id=1, replica_groups=mesh['s'=8,'z'=4,'gy'=4] {'z','gy'}, dimensions={0} | all-to-all | bytes 2621440 | tf_op jit(solution)/shard_map/all_to_all | solution.py:345
  31.9 1.5 %shard_map.41 = (f32[18,8,8,128]{3,2,1,0:T(8,128)}, f32[18,8,8,128]{3,2,1,0:T(8,128)}, f32[4,8,8,128]{3,2,1,0:T(8,128)S(1)}, f32[4,8,8,128]{3,2,1,0:T(8,128)S(1)}, f32[8,8,8,128]{3,2,1,0:T(8,128)S(1)}) custom-call(f32[2560,128]{1,0:T(8,128)S(1)} %bitcast.11), custom_call_target="tpu_custom_call" | custom-call | tf_op jit(solution)/shard_map/pallas_call | solution.py:347
  33.4 1.2 %collective-permute-start = (f32[18,8,8,128]{3,2,1,0:T(8,128)}, f32[18,8,8,128]{3,2,1,0:T(8,128)S(1)}, u32[]{:S(2)}, u32[]{:S(2)}) collective-permute-start(f32[18,8,8,128]{3,2,1,0:T(8,128)} %get-tuple-element.7), channel_id=1, source_target_pairs={{0,16},{16,32},{32,48},{48,64},{64,80},{80,96},{96,112},{112,0},{1... | collective-permute-start | bytes 1769480 | tf_op jit(solution)/shard_map/ppermute | solution.py:355
  34.6 2.4 %collective-permute-start.1 = (f32[18,8,8,128]{3,2,1,0:T(8,128)}, f32[18,8,8,128]{3,2,1,0:T(8,128)S(1)}, u32[]{:S(2)}, u32[]{:S(2)}) collective-permute-start(f32[18,8,8,128]{3,2,1,0:T(8,128)} %get-tuple-element.8), channel_id=1, source_target_pairs={{16,0},{32,16},{48,32},{64,48},{80,64},{96,80},{112,96},{0,112},{1... | collective-permute-start | bytes 1769480 | tf_op jit(solution)/shard_map/ppermute | solution.py:356
  37.0 0.0 collective-permute-start.2
  37.0 3.6 %collective-permute-start.3 = (f32[4,8,8,128]{3,2,1,0:T(8,128)S(1)}, f32[4,8,8,128]{3,2,1,0:T(8,128)S(1)}, u32[]{:S(2)}, u32[]{:S(2)}) collective-permute-start(f32[4,8,8,128]{3,2,1,0:T(8,128)S(1)} %get-tuple-element.10), channel_id=1, source_target_pairs={{16,0},{32,16},{48,32},{64,48},{80,64},{96,80},{112,96},{0,112},{1... | collective-permute-start | bytes 393224 | tf_op jit(solution)/shard_map/ppermute | solution.py:354
  40.5 2.1 %collective-permute-start.6 = (f32[8,8,8,128]{3,2,1,0:T(8,128)S(1)}, f32[8,8,8,128]{3,2,1,0:T(8,128)S(1)}, u32[]{:S(2)}, u32[]{:S(2)}) collective-permute-start(f32[8,8,8,128]{3,2,1,0:T(8,128)S(1)} %get-tuple-element.11.mid_pot), channel_id=1, source_target_pairs={{0,1},{1,0},{2,3},{3,2},{4,5},{5,4},{6,7},{7,6},{8,9},{9,8},{10,11... | collective-permute-start | bytes 786440 | tf_op jit(solution)/shard_map/ppermute | solution.py:357
  42.6 9.7 %collective-permute-done.2.low_pot = f32[4,8,8,128]{3,2,1,0:T(8,128)S(1)} collective-permute-done((f32[4,8,8,128]{3,2,1,0:T(8,128)S(1)}, f32[4,8,8,128]{3,2,1,0:T(8,128)S(1)}, u32[]{:S(2)}, u32[]{:S(2)}) %collective-permute-start.2) | collective-permute-done | bytes 131104 | tf_op jit(solution)/shard_map/ppermute | solution.py:353
  52.4 1.9 %collective-permute-start.4 = (f32[4,8,8,128]{3,2,1,0:T(8,128)S(1)}, f32[4,8,8,128]{3,2,1,0:T(8,128)S(1)}, u32[]{:S(2)}, u32[]{:S(2)}) collective-permute-start(f32[4,8,8,128]{3,2,1,0:T(8,128)S(1)} %collective-permute-done.2.low_pot), channel_id=1, source_target_pairs={{0,1},{1,0},{2,3},{3,2},{4,5},{5,4},{6,7},{7,6},{8,9},{9,8},{10,11... | collective-permute-start | bytes 393224 | tf_op jit(solution)/shard_map/ppermute | solution.py:358
  54.3 0.0 collective-permute-done.3.high_pot
  54.3 0.0 collective-permute-start.5
  54.3 1.0 collective-permute-done.4.far_low
  55.3 0.4 collective-permute-done.5.far_high
  55.6 0.0 collective-permute-done.6.far_mid
  55.6 0.0 collective-permute-done.low
  55.6 0.0 collective-permute-done.1.high
  55.6 9.0 %shard_map.42 = f32[2048,128]{1,0:T(8,128)S(1)} custom-call(s32[1]{0:T(128)} %bitcast.core, f32[2560,128]{1,0:T(8,128)S(1)} %bitcast.12, f32[18,8,8,128]{3,2,1,0:T(8,128)S(1)} %collective-permute-done.low, f32[18,8,8,128]{3,2,1,0:T(8,128)S(1)} %collective-permute-done.1.high, f32[4,8,8,128]{3,2,1,0:T(8,128)S(1)} %collective-permute-done.2.low_pot, ...), custom_call_target="tpu_custom_call" | custom-call | tf_op jit(solution)/shard_map/pallas_call | solution.py:360
  64.6 19.9 %all_to_all.16 = f32[16,2,8,8,128]{4,3,2,1,0:T(8,128)S(1)} all-to-all(f32[16,2,8,8,128]{4,3,2,1,0:T(8,128)S(1)} %bitcast.15), channel_id=1, replica_groups=mesh['s'=8,'z'=4,'gy'=4] {'z','gy'}, dimensions={0} | all-to-all | bytes 2097152 | tf_op jit(solution)/shard_map/all_to_all | solution.py:374
  84.5 1.9 %shard_map.43 = f32[640,128]{1,0:T(8,128)S(1)} custom-call(f32[32,8,8,128]{3,2,1,0:T(8,128)S(1)} %bitcast.13), custom_call_target="tpu_custom_call" | custom-call | tf_op jit(solution)/shard_map/pallas_call | solution.py:377
  86.4 17.4 %all_to_all.17 = f32[128,1,640]{2,1,0:T(1,128)S(1)} all-to-all(f32[128,1,640]{2,1,0:T(1,128)S(1)} %bitcast.17), channel_id=1, replica_groups=mesh['s'=8,'z'=4,'gy'=4] {'s','z','gy'}, dimensions={0} | all-to-all | bytes 655360 | tf_op jit(solution)/shard_map/all_to_all | solution.py:380
  103.9 3.4 %shard_map.44 = (f32[32,8,8,128]{3,2,1,0:T(8,128)}, f32[32,32]{1,0:T(8,128)}) custom-call(f32[640,128]{1,0:T(8,128)S(1)} %bitcast.16, f32[32,8,8,128]{3,2,1,0:T(8,128)S(1)} %bitcast.14), custom_call_target="tpu_custom_call" | custom-call | tf_op jit(solution)/shard_map/pallas_call | solution.py:383
  (1 shorter events, 0.0 us)
Async XLA Ops:
  33.4 22.2 %collective-permute-start = (f32[18,8,8,128]{3,2,1,0:T(8,128)}, f32[18,8,8,128]{3,2,1,0:T(8,128)S(1)}, u32[]{:S(2)}, u32[]{:S(2)}) collective-permute-start(f32[18,8,8,128]{3,2,1,0:T(8,128)} %get-tuple-element.7), channel_id=1, source_target_pairs={{0,16},{16,32},{32,48},{48,64},{64,80},{80,96},{96,112},{112,0},{1... | collective-permute-start | bytes 1769480 | tf_op jit(solution)/shard_map/ppermute | solution.py:355
  34.6 21.0 %collective-permute-start.1 = (f32[18,8,8,128]{3,2,1,0:T(8,128)}, f32[18,8,8,128]{3,2,1,0:T(8,128)S(1)}, u32[]{:S(2)}, u32[]{:S(2)}) collective-permute-start(f32[18,8,8,128]{3,2,1,0:T(8,128)} %get-tuple-element.8), channel_id=1, source_target_pairs={{16,0},{32,16},{48,32},{64,48},{80,64},{96,80},{112,96},{0,112},{1... | collective-permute-start | bytes 1769480 | tf_op jit(solution)/shard_map/ppermute | solution.py:356
  37.0 15.4 %collective-permute-start.2 = (f32[4,8,8,128]{3,2,1,0:T(8,128)S(1)}, f32[4,8,8,128]{3,2,1,0:T(8,128)S(1)}, u32[]{:S(2)}, u32[]{:S(2)}) collective-permute-start(f32[4,8,8,128]{3,2,1,0:T(8,128)S(1)} %get-tuple-element.9), channel_id=1, source_target_pairs={{0,16},{16,32},{32,48},{48,64},{64,80},{80,96},{96,112},{112,0},{1... | collective-permute-start | bytes 393224 | tf_op jit(solution)/shard_map/ppermute | solution.py:353
  37.0 17.3 %collective-permute-start.3 = (f32[4,8,8,128]{3,2,1,0:T(8,128)S(1)}, f32[4,8,8,128]{3,2,1,0:T(8,128)S(1)}, u32[]{:S(2)}, u32[]{:S(2)}) collective-permute-start(f32[4,8,8,128]{3,2,1,0:T(8,128)S(1)} %get-tuple-element.10), channel_id=1, source_target_pairs={{16,0},{32,16},{48,32},{64,48},{80,64},{96,80},{112,96},{0,112},{1... | collective-permute-start | bytes 393224 | tf_op jit(solution)/shard_map/ppermute | solution.py:354
  40.5 15.1 %collective-permute-start.6 = (f32[8,8,8,128]{3,2,1,0:T(8,128)S(1)}, f32[8,8,8,128]{3,2,1,0:T(8,128)S(1)}, u32[]{:S(2)}, u32[]{:S(2)}) collective-permute-start(f32[8,8,8,128]{3,2,1,0:T(8,128)S(1)} %get-tuple-element.11.mid_pot), channel_id=1, source_target_pairs={{0,1},{1,0},{2,3},{3,2},{4,5},{5,4},{6,7},{7,6},{8,9},{9,8},{10,11... | collective-permute-start | bytes 786440 | tf_op jit(solution)/shard_map/ppermute | solution.py:357
  52.4 2.9 %collective-permute-start.4 = (f32[4,8,8,128]{3,2,1,0:T(8,128)S(1)}, f32[4,8,8,128]{3,2,1,0:T(8,128)S(1)}, u32[]{:S(2)}, u32[]{:S(2)}) collective-permute-start(f32[4,8,8,128]{3,2,1,0:T(8,128)S(1)} %collective-permute-done.2.low_pot), channel_id=1, source_target_pairs={{0,1},{1,0},{2,3},{3,2},{4,5},{5,4},{6,7},{7,6},{8,9},{9,8},{10,11... | collective-permute-start | bytes 393224 | tf_op jit(solution)/shard_map/ppermute | solution.py:358
  54.3 1.3 %collective-permute-start.5 = (f32[4,8,8,128]{3,2,1,0:T(8,128)S(1)}, f32[4,8,8,128]{3,2,1,0:T(8,128)S(1)}, u32[]{:S(2)}, u32[]{:S(2)}) collective-permute-start(f32[4,8,8,128]{3,2,1,0:T(8,128)S(1)} %collective-permute-done.3.high_pot), channel_id=1, source_target_pairs={{0,1},{1,0},{2,3},{3,2},{4,5},{5,4},{6,7},{7,6},{8,9},{9,8},{10,11... | collective-permute-start | bytes 393224 | tf_op jit(solution)/shard_map/ppermute | solution.py:359

commit v5 on v4

--- a/solution.py
+++ b/solution.py
@@ -32,6 +32,8 @@
 FLAT = 2 * REACH
 STEP = 4
 PAIR = 2
+IN1 = (DEEP, DEEP + 20)
+IN2 = (DEEP, DEEP + 8)
 BX = 8
 BLOCK = BX + 2
 SLAB = 4 * BX
@@ -41,6 +43,15 @@
 
 def gather(got, z, xi, yi):
     return got[pl.ds(((z * 4) * PAIR * BLOCK + xi) * BX + yi, 8, stride=BLOCK * BX), :]
+
+
+def message_kernel(orbitals, potential, out):
+    for d in range(out.shape[0]):
+        for o in range(PAIR):
+            for xi in range(BX):
+                out[d, o, xi] = orbitals[d, o, xi]
+            for k in range(2):
+                out[d, o, BX + k] = potential[4 * o + 2 * k + d % 2]
 
 
 def pack_kernel(got, up, down, up_pot, down_pot, mid_pot):
@@ -96,11 +107,89 @@
     return both[:, :128] + both[:, 128:]
 
 
-def filter_kernel(
-    core, got, low, high, low_pot, high_pot, mid_pot, far_low, far_high, far_mid,
+def sweep(field, far_z, bands, first, last, count, one):
+    def chunk(c, carry):
+        start = first + c * count
+        along_z(field, far_z, bands, start + REACH, start, count)
+        for r in range(0, count, 2):
+            one(start + r)
+        return carry
+
+    lax.fori_loop(0, (last - first) // count, chunk, 0)
+
+
+def along_z(field, far_z, bands, row, i, count):
+    v = field[pl.ds(row, count), :, 0:8].reshape(count * BX * 8, 128)
+    far_z[pl.ds(i, count)] = band_product(v, bands).reshape(count, BX, 8, 128)
+
+
+def apply(field, pot, far_z, row, pot_row, i):
+    totals = [[], []]
+    for begin in range(0, BX, 4):
+        lines = [
+            [take(field, row + r, y) for y in range(begin - REACH, begin + 4 + REACH)]
+            for r in range(2)
+        ]
+        for yi in range(begin, begin + 4):
+            e = REACH + yi - begin
+            x = {0: lines[0][e], 1: lines[1][e]}
+            for d in (*range(-REACH, 0), *range(2, REACH + 2)):
+                x[d] = take(field, row + d, yi)
+            for r in range(2):
+                line = lines[r]
+                total = pot[pot_row + r, yi] * line[e] + far_z[i + r, yi]
+                for j in range(1, REACH + 1):
+                    near = (x[r + j] + x[r - j]) + (line[e + j] + line[e - j])
+                    total = total + coupling[j] * near
+                totals[r].append(total)
+    return totals
+
+
+def put_pots(pot, mine, sources, row, skip):
+    odd = iota((8, 128), 0) % 2 == 1
+    for z in range(len(skip)):
+        for k in range(2):
+            for source, parity in zip(sources, (mine, 1 - mine)):
+                at = row + z * BX + 2 * k + parity
+                for yi in range(BX):
+                    tile = diagonal + source[2 * z + k, yi] * (1.0 / half_width)
+                    if skip[z] != 0:
+                        pot[at, yi] = jnp.where(odd, pltpu.roll(tile, 1, 0), tile)
+                    if skip[z] != 1:
+                        pot[at + 4, yi] = jnp.where(odd, tile, pltpu.roll(tile, 7, 0))
+
+
+def steps(field0, field1, field2, pot, far_z):
+    def first(i):
+        for r, ts in enumerate(apply(field0, pot, far_z, i + REACH, i, i)):
+            put(field1, i + r, ts)
+
+    def second(i):
+        for r, ts in enumerate(apply(field1, pot, far_z, i + REACH, i + REACH, i)):
+            before = i + r + FLAT
+            put(field2, i + r, [t + t - take(field0, before, yi) for yi, t in enumerate(ts)])
+
+    return first, second
+
+
+def inner_kernel(core, got, mid_pot, far_mid, field0, field1, field2, pot, far_z):
+    bands = band_parts()
+    for z in range(4):
+        def fill(xi, carry, z=z):
+            put(field0, DEEP + z * BX + xi, [gather(got, z, xi, yi) for yi in range(BX)])
+            return carry
+
+        lax.fori_loop(0, BX, fill, 0)
+    put_pots(pot, core[0], (mid_pot, far_mid), FLAT, (None,) * 4)
+    first, second = steps(field0, field1, field2, pot, far_z)
+    sweep(field0, far_z, bands, *IN1, IN1[1] - IN1[0], first)
+    sweep(field1, far_z, bands, *IN2, IN2[1] - IN2[0], second)
+
+
+def outer_kernel(
+    core, low, high, low_pot, high_pot, far_low, far_high, _0, _1, _2, _3,
     out, field0, field1, field2, pot, far_z,
 ):
-    mine = core[0]
     bands = band_parts()
 
     def edge(i, carry):
@@ -109,94 +198,25 @@
         return carry
 
     lax.fori_loop(0, DEEP, edge, 0)
-    for z in range(4):
-        def inner(xi, carry, z=z):
-            put(field0, DEEP + z * BX + xi, [gather(got, z, xi, yi) for yi in range(BX)])
-            return carry
-
-        lax.fori_loop(0, BX, inner, 0)
-
-    odd = iota((8, 128), 0) % 2 == 1
-
-    def put_pot(row, source, i, yi, parity, skip):
-        tile = diagonal + source[i, yi] * (1.0 / half_width)
-        if skip != 0:
-            pot[row + parity, yi] = jnp.where(odd, pltpu.roll(tile, 1, 0), tile)
-        if skip != 1:
-            pot[row + 4 + parity, yi] = jnp.where(odd, tile, pltpu.roll(tile, 7, 0))
-
-    for sources, row, count, skip in (
-        ((low_pot, far_low), FLAT - 2 * BX, 2, (0, None)),
-        ((mid_pot, far_mid), FLAT, 4, (None,) * 4),
-        ((high_pot, far_high), FLAT + SLAB, 2, (None, 1)),
-    ):
-        for z in range(count):
-            for k in range(2):
-                for source, parity in zip(sources, (mine, 1 - mine)):
-                    for yi in range(BX):
-                        put_pot(
-                            row + z * BX + 2 * k, source, 2 * z + k, yi, parity, skip[z]
-                        )
-
-    def along_z(field, start, i, count):
-        v = field[pl.ds(start, count), :, 0:8].reshape(count * BX * 8, 128)
-        far_z[pl.ds(i, count)] = band_product(v, bands).reshape(count, BX, 8, 128)
-
-    def sweep(field, rows, count, one):
-        along_z(field, REACH, 0, count)
-
-        def chunk(c, carry):
-            for r in range(0, count, 2):
-                one(c * count + r)
-            ahead = (c + 1) * count
-            along_z(field, REACH + ahead, ahead, count)
-            return carry
-
-        lax.fori_loop(0, rows // count - 1, chunk, 0)
-        for r in range(rows - count, rows, 2):
-            one(r)
-
-    def apply(field, row, pot_row, i):
-        totals = [[], []]
-        for begin in range(0, BX, 4):
-            lines = [
-                [take(field, row + r, y) for y in range(begin - REACH, begin + 4 + REACH)]
-                for r in range(2)
-            ]
-            for yi in range(begin, begin + 4):
-                e = REACH + yi - begin
-                x = {0: lines[0][e], 1: lines[1][e]}
-                for d in (*range(-REACH, 0), *range(2, REACH + 2)):
-                    x[d] = take(field, row + d, yi)
-                for r in range(2):
-                    line = lines[r]
-                    total = pot[pot_row + r, yi] * line[e] + far_z[i + r, yi]
-                    for j in range(1, REACH + 1):
-                        near = (x[r + j] + x[r - j]) + (line[e + j] + line[e - j])
-                        total = total + coupling[j] * near
-                    totals[r].append(total)
-        return totals
-
-    def first(i):
-        for r, ts in enumerate(apply(field0, i + REACH, i, i)):
-            put(field1, i + r, ts)
-
-    def second(i):
-        for r, ts in enumerate(apply(field1, i + REACH, i + REACH, i)):
-            before = i + r + FLAT
-            put(field2, i + r, [t + t - take(field0, before, yi) for yi, t in enumerate(ts)])
+    mine = core[0]
+    put_pots(pot, mine, (low_pot, far_low), FLAT - 2 * BX, (0, None))
+    put_pots(pot, mine, (high_pot, far_high), FLAT + SLAB, (None, 1))
+    first, second = steps(field0, field1, field2, pot, far_z)
 
     def third(i):
-        for r, ts in enumerate(apply(field2, i + REACH, i + FLAT, i)):
+        for r, ts in enumerate(apply(field2, pot, far_z, i + REACH, i + FLAT, i)):
             for yi, t in enumerate(ts):
                 start = ((i // BX) * 4 * PAIR * BX + i % BX + r) * BX + yi
                 out[pl.ds(start, 8, stride=BX * BX), :] = (
                     t + t - take(field1, i + r + FLAT, yi)
                 )
 
-    sweep(field0, SLAB + 2 * FLAT, 14, first)
-    sweep(field1, SLAB + FLAT, 22, second)
-    sweep(field2, SLAB, 16, third)
+    ends1, ends2 = SLAB + 2 * FLAT, SLAB + FLAT
+    sweep(field0, far_z, bands, 0, IN1[0], IN1[0], first)
+    sweep(field0, far_z, bands, IN1[1], ends1, ends1 - IN1[1], first)
+    sweep(field1, far_z, bands, 0, IN2[0], IN2[0], second)
+    sweep(field1, far_z, bands, IN2[1], ends2, ends2 - IN2[1], second)
+    sweep(field2, far_z, bands, 0, SLAB, SLAB // 2, third)
 
 
 def iota(shape, dim):
@@ -315,13 +335,14 @@
         out[:, x + 1] = mixed[:, 128:].reshape(n, BX, 128)
 
 
-def call(kernel, out_shape, in_specs, scratch=(), limit=8, flops=0, moved=0):
+def call(kernel, out_shape, in_specs, scratch=(), limit=8, flops=0, moved=0, aliases={}):
     return pl.pallas_call(
         kernel,
         out_shape=out_shape,
         in_specs=in_specs,
         out_specs=jax.tree.map(lambda _: VMEM, out_shape),
         scratch_shapes=list(scratch),
+        input_output_aliases=aliases,
         compiler_params=pltpu.CompilerParams(vmem_limit_bytes=limit << 20),
         cost_estimate=pl.CostEstimate(flops=flops, bytes_accessed=moved, transcendentals=0),
     )
@@ -336,12 +357,11 @@
     slabs = lax.axis_size("s")
     group = lax.axis_size("z") * lax.axis_size("gy")
     core = lax.axis_index("gy") & 1
-    halves = potential.reshape(2, 2, 2, BX, 128).transpose(2, 0, 1, 3, 4)
-    halves = jnp.broadcast_to(halves[None], (group // 2, 2, PAIR, 2, BX, 128))
-    sent = jnp.concatenate(
-        [orbitals.reshape(group, PAIR, BX, BX, 128), halves.reshape(group, PAIR, 2, BX, 128)],
-        axis=2,
-    )
+    sent = call(
+        message_kernel,
+        f32(group, PAIR, BLOCK, BX, 128),
+        [VMEM, VMEM],
+    )(orbitals.reshape(group, PAIR, BX, BX, 128), potential)
     got = lax.all_to_all(sent, ("z", "gy"), 0, 0, tiled=True)
     got = got.reshape(group * PAIR * BLOCK * BX, 128)
     up, down, up_pot, down_pot, mid_pot = call(
@@ -355,21 +375,24 @@
     low = lax.ppermute(up, "s", ring)
     high = lax.ppermute(down, "s", back_ring)
     far_mid = lax.ppermute(mid_pot, "gy", twin)
+    own = (core.reshape(1),)
+    fields = tuple(f32(rows, BX, 16, 128) for rows in (SLAB + 2 * DEEP, SLAB + 2 * FLAT, SLAB + FLAT))
+    fields += (f32(SLAB + 2 * FLAT, BX, 8, 128),)
+    far_z = [pltpu.VMEM((SLAB + 2 * FLAT, BX, 8, 128), jnp.float32)]
+    inner = call(inner_kernel, fields, [SMEM] + [VMEM] * 3, far_z, 10, flops=1 << 32)(
+        *own, got, mid_pot, far_mid
+    )
+    low_pot, high_pot, inner = lax.optimization_barrier((low_pot, high_pot, inner))
     far_low = lax.ppermute(low_pot, "gy", twin)
     far_high = lax.ppermute(high_pot, "gy", twin)
     filtered = call(
-        filter_kernel,
-        f32(group * PAIR * BX * BX, 128),
-        [SMEM] + [VMEM] * 9,
-        [
-            pltpu.VMEM((SLAB + 2 * DEEP, BX, 16, 128), jnp.float32),
-            pltpu.VMEM((SLAB + 2 * FLAT, BX, 16, 128), jnp.float32),
-            pltpu.VMEM((SLAB + FLAT, BX, 16, 128), jnp.float32),
-            pltpu.VMEM((SLAB + 2 * FLAT, BX, 8, 128), jnp.float32),
-            pltpu.VMEM((SLAB + 2 * FLAT, BX, 8, 128), jnp.float32),
-        ],
-        32,
-    )(core.reshape(1), got, low, high, low_pot, high_pot, mid_pot, far_low, far_high, far_mid)
+        outer_kernel,
+        (f32(group * PAIR * BX * BX, 128),) + fields,
+        [SMEM] + [VMEM] * 10,
+        far_z,
+        10,
+        aliases={7 + k: 1 + k for k in range(4)},
+    )(*own, low, high, low_pot, high_pot, far_low, far_high, *inner)[0]
     filtered = filtered.reshape(group, PAIR, BX, BX, 128)
     back = lax.all_to_all(filtered, ("z", "gy"), 0, 0, tiled=True).reshape(n, BX, BX, 128)
     devices = slabs * group

time: 108 us -> 106 us (0.981)
  starting transfers between devices: 11.2 us -> 8.92 us
  local copies, waits for them, and re-layouts: 0.78 us -> 2.64 us
  other arithmetic: 1.34 us -> 0 us
    unnamed x0 -> x6, local copies, waits for them, and re-layouts: none -> 2.64 us
    concatenate x1 -> x0, other arithmetic: 1.34 us -> none  [per_device(): jnp.concatenate([orbitals.reshape(group, PAIR, BX, BX, 128), halves.resha...]
    ppermute x1, starting transfers between devices: 2.1 us -> 0.98 us  [per_device(): far_mid = lax.ppermute(mid_pot, 'gy', twin)]
    ppermute x1, starting transfers between devices: 1.9 us -> 0.79 us  [per_device(): far_low = lax.ppermute(low_pot, 'gy', twin)]
    pallas_call x1 -> x3, Pallas kernels: 8.95 us -> 9.17 us  [the longest x1 6.17 us: per_device(): call(outer_kernel, (f32(group * PAIR * BX * BX, 128),) + fields, [SMEM] +...]
  transfers between devices with their start and end apart: 7 -> 7, of which waited for: 3 -> 3; matrix products, arithmetic and copies ran while one was open for 0% -> 0% of each run, Pallas kernels for 0% -> 3%
where the time goes in v5:
time: 106 us
  blocking collectives  66.3 us (63%)
  Pallas kernels  15.7 us (15%)
  waiting for transfers between devices  11.4 us (11%)
  starting transfers between devices  8.92 us (8%)
  local copies, waits for them, and re-layouts  2.64 us (2%)
    all_to_all x1, blocking collectives, per_device(): got = lax.all_to_all(sent, ('z', 'gy'), 0, 0, tiled=True)  29.2 us
    all_to_all x1, blocking collectives, per_device(): lax.all_to_all(filtered, ('z', 'gy'), 0, 0, tiled=True)  19.6 us
    all_to_all x1, blocking collectives, per_device(): lax.all_to_all(parts.reshape(devices, 1, 5 * 128), ('s', 'z', 'gy'), 0, 0...  17.5 us
    ppermute x1, waiting for transfers between devices, per_device(): low_pot = lax.ppermute(up_pot, 's', ring)  10 us
    pallas_call x1, Pallas kernels, per_device(): call(outer_kernel, (f32(group * PAIR * BX * BX, 128),) + fields, [SMEM] +...  6.17 us
    ppermute x1, starting transfers between devices, per_device(): high_pot = lax.ppermute(down_pot, 's', back_ring)  3.57 us
    pallas_call x1, Pallas kernels, per_device(): call(finish_kernel, (f32(n, BX, BX, 128), f32(n, n)), [VMEM, VMEM])  3.42 us
    pallas_call x1, Pallas kernels, per_device(): call(inner_kernel, fields, [SMEM] + [VMEM] * 3, far_z, 10, flops=1 << 32)  2.91 us
  transfers between devices with their start and end apart: 7, of which 3 were waited for; matrix products, arithmetic and copies ran while one was open for 0% of the time, Pallas kernels for 3%

profile of v5, /device:TPU:1, one launch (start us, length us, event | category | flops | bytes accessed | tf_op | source)
XLA Modules:
  0.0 105.6 jit_solution(14658557748199579963)
XLA Ops:
  0.6 0.0 copy-start
  0.6 1.2 %copy-done = f32[32,8,8,128]{3,2,1,0:T(8,128)S(1)} copy-done((f32[32,8,8,128]{3,2,1,0:T(8,128)S(1)}, f32[32,8,8,128]{3,2,1,0:T(8,128)}, u32[]{:S(2)}) %copy-start) | copy-done | bytes 1048600
  1.9 0.0 copy-start.1
  1.9 0.8 copy-done.1
  2.6 0.1 shard_map.41
  2.7 29.2 %all_to_all.15 = f32[16,2,10,8,128]{4,3,2,1,0:T(8,128)S(1)} all-to-all(f32[16,2,10,8,128]{4,3,2,1,0:T(8,128)S(1)} %shard_map.41), channel_id=1, replica_groups=mesh['s'=8,'z'=4,'gy'=4] {'z','gy'}, dimensions={0} | all-to-all | bytes 2621440 | tf_op jit(solution)/shard_map/all_to_all | solution.py:365
  31.9 1.3 %shard_map.42 = (f32[18,8,8,128]{3,2,1,0:T(8,128)}, f32[18,8,8,128]{3,2,1,0:T(8,128)S(1)}, f32[4,8,8,128]{3,2,1,0:T(8,128)S(1)}, f32[4,8,8,128]{3,2,1,0:T(8,128)S(1)}, f32[8,8,8,128]{3,2,1,0:T(8,128)S(1)}) custom-call(f32[2560,128]{1,0:T(8,128)S(1)} %bitcast.9), custom_call_target="tpu_custom_call" | custom-call | tf_op jit(solution)/shard_map/pallas_call | solution.py:367
  33.1 0.0 copy-start.2
  33.1 0.7 copy-done.2
  33.8 1.0 collective-permute-start.4
  34.8 1.2 %collective-permute-start = (f32[18,8,8,128]{3,2,1,0:T(8,128)}, f32[18,8,8,128]{3,2,1,0:T(8,128)S(1)}, u32[]{:S(2)}, u32[]{:S(2)}) collective-permute-start(f32[18,8,8,128]{3,2,1,0:T(8,128)} %get-tuple-element.18), channel_id=1, source_target_pairs={{0,16},{16,32},{32,48},{48,64},{64,80},{80,96},{96,112},{112,0},{1... | collective-permute-start | bytes 1769480 | tf_op jit(solution)/shard_map/ppermute | solution.py:375
  36.0 2.4 %collective-permute-start.1 = (f32[18,8,8,128]{3,2,1,0:T(8,128)S(1)}, f32[18,8,8,128]{3,2,1,0:T(8,128)S(1)}, u32[]{:S(2)}, u32[]{:S(2)}) collective-permute-start(f32[18,8,8,128]{3,2,1,0:T(8,128)S(1)} %get-tuple-element.19), channel_id=1, source_target_pairs={{16,0},{32,16},{48,32},{64,48},{80,64},{96,80},{112,96},{0,112},{1... | collective-permute-start | bytes 1769480 | tf_op jit(solution)/shard_map/ppermute | solution.py:376
  38.4 0.0 collective-permute-start.2
  38.4 3.6 %collective-permute-start.3 = (f32[4,8,8,128]{3,2,1,0:T(8,128)S(1)}, f32[4,8,8,128]{3,2,1,0:T(8,128)S(1)}, u32[]{:S(2)}, u32[]{:S(2)}) collective-permute-start(f32[4,8,8,128]{3,2,1,0:T(8,128)S(1)} %get-tuple-element.21), channel_id=1, source_target_pairs={{16,0},{32,16},{48,32},{64,48},{80,64},{96,80},{112,96},{0,112},{1... | collective-permute-start | bytes 393224 | tf_op jit(solution)/shard_map/ppermute | solution.py:374
  41.9 0.0 collective-permute-done.4.far_mid
  41.9 2.9 %shard_map.43 = (f32[68,8,16,128]{3,2,1,0:T(8,128)S(1)}, f32[56,8,16,128]{3,2,1,0:T(8,128)S(1)}, f32[44,8,16,128]{3,2,1,0:T(8,128)S(1)}, f32[56,8,8,128]{3,2,1,0:T(8,128)S(1)}) custom-call(s32[1]{0:T(128)} %bitcast.core, f32[2560,128]{1,0:T(8,128)S(1)} %bitcast.10, f32[8,8,8,128]{3,2,1,0:T(8,128)S(1)} %get-tuple-element.22.mid_pot, ...), custom_call_target="tpu_custom_call" | custom-call | flops 4294967296 | tf_op jit(solution)/shard_map/pallas_call | solution.py:382
  44.9 10.0 %collective-permute-done.2.low_pot = f32[4,8,8,128]{3,2,1,0:T(8,128)S(1)} collective-permute-done((f32[4,8,8,128]{3,2,1,0:T(8,128)}, f32[4,8,8,128]{3,2,1,0:T(8,128)S(1)}, u32[]{:S(2)}, u32[]{:S(2)}) %collective-permute-start.2) | collective-permute-done | bytes 131104 | tf_op jit(solution)/shard_map/ppermute | solution.py:373
  54.9 0.0 collective-permute-done.3.high_pot
  54.9 0.8 collective-permute-start.5
  55.7 0.0 collective-permute-start.6
  55.7 1.0 collective-permute-done.5.far_low
  56.7 0.4 collective-permute-done.6.far_high
  57.0 0.0 collective-permute-done.low
  57.0 0.0 collective-permute-done.1.high
  57.0 6.2 %shard_map.44 = (f32[2048,128]{1,0:T(8,128)S(1)}, f32[68,8,16,128]{3,2,1,0:T(8,128)S(1)}, f32[56,8,16,128]{3,2,1,0:T(8,128)S(1)}, f32[44,8,16,128]{3,2,1,0:T(8,128)S(1)}, f32[56,8,8,128]{3,2,1,0:T(8,128)S(1)}) custom-call(s32[1]{0:T(128)} %bitcast.core, ...), custom_call_target="tpu_custom_call", output_to_operand_aliasing={{1}: (7, {}), {2}: (8, {}), {3}: (9, {}), {4}: (10, {})} | custom-call | tf_op jit(solution)/shard_map/pallas_call | solution.py:388
  63.2 19.6 %all_to_all.16 = f32[16,2,8,8,128]{4,3,2,1,0:T(8,128)S(1)} all-to-all(f32[16,2,8,8,128]{4,3,2,1,0:T(8,128)S(1)} %bitcast.14), channel_id=1, replica_groups=mesh['s'=8,'z'=4,'gy'=4] {'z','gy'}, dimensions={0} | all-to-all | bytes 2097152 | tf_op jit(solution)/shard_map/all_to_all | solution.py:397
  82.8 1.9 %shard_map.45 = f32[640,128]{1,0:T(8,128)S(1)} custom-call(f32[32,8,8,128]{3,2,1,0:T(8,128)S(1)} %bitcast.7), custom_call_target="tpu_custom_call" | custom-call | tf_op jit(solution)/shard_map/pallas_call | solution.py:400
  84.7 17.5 %all_to_all.17 = f32[128,1,640]{2,1,0:T(1,128)S(1)} all-to-all(f32[128,1,640]{2,1,0:T(1,128)S(1)} %bitcast.12), channel_id=1, replica_groups=mesh['s'=8,'z'=4,'gy'=4] {'s','z','gy'}, dimensions={0} | all-to-all | bytes 655360 | tf_op jit(solution)/shard_map/all_to_all | solution.py:403
  102.2 3.4 %shard_map.46 = (f32[32,8,8,128]{3,2,1,0:T(8,128)}, f32[32,32]{1,0:T(8,128)}) custom-call(f32[640,128]{1,0:T(8,128)S(1)} %bitcast.11, f32[32,8,8,128]{3,2,1,0:T(8,128)S(1)} %bitcast.8), custom_call_target="tpu_custom_call" | custom-call | tf_op jit(solution)/shard_map/pallas_call | solution.py:406
Async XLA Ops:
  0.6 1.2 %copy-start = (f32[32,8,8,128]{3,2,1,0:T(8,128)S(1)}, f32[32,8,8,128]{3,2,1,0:T(8,128)}, u32[]{:S(2)}) copy-start(f32[32,8,8,128]{3,2,1,0:T(8,128)} %param.2) | copy-start | bytes 3145732
  1.9 0.8 copy-start.1
  33.1 0.7 copy-start.2
  33.8 8.1 %collective-permute-start.4 = (f32[8,8,8,128]{3,2,1,0:T(8,128)S(1)}, f32[8,8,8,128]{3,2,1,0:T(8,128)}, u32[]{:S(2)}, u32[]{:S(2)}) collective-permute-start(f32[8,8,8,128]{3,2,1,0:T(8,128)S(1)} %get-tuple-element.22.mid_pot), channel_id=1, source_target_pairs={{0,1},{1,0},{2,3},{3,2},{4,5},{5,4},{6,7},{7,6},{8,9},{9,8},{10,11... | collective-permute-start | bytes 786440 | tf_op jit(solution)/shard_map/ppermute | solution.py:377
  34.8 22.2 %collective-permute-start = (f32[18,8,8,128]{3,2,1,0:T(8,128)}, f32[18,8,8,128]{3,2,1,0:T(8,128)S(1)}, u32[]{:S(2)}, u32[]{:S(2)}) collective-permute-start(f32[18,8,8,128]{3,2,1,0:T(8,128)} %get-tuple-element.18), channel_id=1, source_target_pairs={{0,16},{16,32},{32,48},{48,64},{64,80},{80,96},{96,112},{112,0},{1... | collective-permute-start | bytes 1769480 | tf_op jit(solution)/shard_map/ppermute | solution.py:375
  36.0 21.0 %collective-permute-start.1 = (f32[18,8,8,128]{3,2,1,0:T(8,128)S(1)}, f32[18,8,8,128]{3,2,1,0:T(8,128)S(1)}, u32[]{:S(2)}, u32[]{:S(2)}) collective-permute-start(f32[18,8,8,128]{3,2,1,0:T(8,128)S(1)} %get-tuple-element.19), channel_id=1, source_target_pairs={{16,0},{32,16},{48,32},{64,48},{80,64},{96,80},{112,96},{0,112},{1... | collective-permute-start | bytes 1769480 | tf_op jit(solution)/shard_map/ppermute | solution.py:376
  38.4 16.5 %collective-permute-start.2 = (f32[4,8,8,128]{3,2,1,0:T(8,128)}, f32[4,8,8,128]{3,2,1,0:T(8,128)S(1)}, u32[]{:S(2)}, u32[]{:S(2)}) collective-permute-start(f32[4,8,8,128]{3,2,1,0:T(8,128)} %copy-done.2), channel_id=1, source_target_pairs={{0,16},{16,32},{32,48},{48,64},{64,80},{80,96},{96,112},{112,0},{1... | collective-permute-start | bytes 393224 | tf_op jit(solution)/shard_map/ppermute | solution.py:373
  38.4 16.5 %collective-permute-start.3 = (f32[4,8,8,128]{3,2,1,0:T(8,128)S(1)}, f32[4,8,8,128]{3,2,1,0:T(8,128)S(1)}, u32[]{:S(2)}, u32[]{:S(2)}) collective-permute-start(f32[4,8,8,128]{3,2,1,0:T(8,128)S(1)} %get-tuple-element.21), channel_id=1, source_target_pairs={{16,0},{32,16},{48,32},{64,48},{80,64},{96,80},{112,96},{0,112},{1... | collective-permute-start | bytes 393224 | tf_op jit(solution)/shard_map/ppermute | solution.py:374
  54.9 1.8 %collective-permute-start.5 = (f32[4,8,8,128]{3,2,1,0:T(8,128)S(1)}, f32[4,8,8,128]{3,2,1,0:T(8,128)S(1)}, u32[]{:S(2)}, u32[]{:S(2)}) collective-permute-start(f32[4,8,8,128]{3,2,1,0:T(8,128)S(1)} %collective-permute-done.2.low_pot), channel_id=1, source_target_pairs={{0,1},{1,0},{2,3},{3,2},{4,5},{5,4},{6,7},{7,6},{8,9},{9,8},{10,11... | collective-permute-start | bytes 393224 | tf_op jit(solution)/shard_map/ppermute | solution.py:386
  55.7 1.3 %collective-permute-start.6 = (f32[4,8,8,128]{3,2,1,0:T(8,128)S(1)}, f32[4,8,8,128]{3,2,1,0:T(8,128)S(1)}, u32[]{:S(2)}, u32[]{:S(2)}) collective-permute-start(f32[4,8,8,128]{3,2,1,0:T(8,128)S(1)} %collective-permute-done.3.high_pot), channel_id=1, source_target_pairs={{0,1},{1,0},{2,3},{3,2},{4,5},{5,4},{6,7},{7,6},{8,9},{9,8},{10,11... | collective-permute-start | bytes 393224 | tf_op jit(solution)/shard_map/ppermute | solution.py:387

commit v6 on v5

--- a/solution.py
+++ b/solution.py
@@ -45,13 +45,17 @@
     return got[pl.ds(((z * 4) * PAIR * BLOCK + xi) * BX + yi, 8, stride=BLOCK * BX), :]
 
 
-def message_kernel(orbitals, potential, out):
+def message_kernel(orbitals, potential, out, rows, arrived):
+    copy = pltpu.make_async_copy(orbitals, out.at[:, :, 0:BX], arrived.at[0])
+    flat = pltpu.make_async_copy(potential, rows, arrived.at[1])
+    flat.start()
+    copy.start()
+    flat.wait()
     for d in range(out.shape[0]):
         for o in range(PAIR):
-            for xi in range(BX):
-                out[d, o, xi] = orbitals[d, o, xi]
             for k in range(2):
-                out[d, o, BX + k] = potential[4 * o + 2 * k + d % 2]
+                out[d, o, BX + k] = rows[4 * o + 2 * k + d % 2]
+    copy.wait()
 
 
 def pack_kernel(got, up, down, up_pot, down_pot, mid_pot):
@@ -60,15 +64,17 @@
             z, xi = divmod(first + i, BX)
             for yi in range(BX):
                 dest[i, yi] = gather(got, z, xi, yi)
-    for z in range(4):
+    odd = iota((8, 128), 0) % 2 == 1
+    for yi in range(BX):
+        tiles = [[gather(got, z, BX + k, yi) for k in range(2)] for z in range(4)]
+        for z in range(4):
+            for k in range(2):
+                mid_pot[2 * z + k, yi] = tiles[z][k]
+        up_pot[0, yi] = jnp.where(odd, tiles[2][1], pltpu.roll(tiles[2][0], 7, 0))
+        down_pot[2, yi] = jnp.where(odd, pltpu.roll(tiles[1][1], 1, 0), tiles[1][0])
         for k in range(2):
-            for yi in range(BX):
-                tile = gather(got, z, BX + k, yi)
-                mid_pot[2 * z + k, yi] = tile
-                if z >= 2:
-                    up_pot[2 * z - 4 + k, yi] = tile
-                else:
-                    down_pot[2 * z + k, yi] = tile
+            up_pot[1 + k, yi] = tiles[3][k]
+            down_pot[k, yi] = tiles[0][k]
 
 
 def put(field, row, tiles):
@@ -145,18 +151,17 @@
     return totals
 
 
-def put_pots(pot, mine, sources, row, skip):
+WHOLE = tuple((8 * z + 2 * k, 8 * z + 2 * k + 4) for z in range(4) for k in range(2))
+
+
+def put_pots(pot, mine, sources, slots, row):
     odd = iota((8, 128), 0) % 2 == 1
-    for z in range(len(skip)):
-        for k in range(2):
-            for source, parity in zip(sources, (mine, 1 - mine)):
-                at = row + z * BX + 2 * k + parity
-                for yi in range(BX):
-                    tile = diagonal + source[2 * z + k, yi] * (1.0 / half_width)
-                    if skip[z] != 0:
-                        pot[at, yi] = jnp.where(odd, pltpu.roll(tile, 1, 0), tile)
-                    if skip[z] != 1:
-                        pot[at + 4, yi] = jnp.where(odd, tile, pltpu.roll(tile, 7, 0))
+    for slot, (even_row, odd_row) in enumerate(slots):
+        for source, parity in zip(sources, (mine, 1 - mine)):
+            for yi in range(BX):
+                tile = diagonal + source[slot, yi] * (1.0 / half_width)
+                pot[row + even_row + parity, yi] = jnp.where(odd, pltpu.roll(tile, 1, 0), tile)
+                pot[row + odd_row + parity, yi] = jnp.where(odd, tile, pltpu.roll(tile, 7, 0))
 
 
 def steps(field0, field1, field2, pot, far_z):
@@ -180,16 +185,13 @@
             return carry
 
         lax.fori_loop(0, BX, fill, 0)
-    put_pots(pot, core[0], (mid_pot, far_mid), FLAT, (None,) * 4)
+    put_pots(pot, core[0], (mid_pot, far_mid), WHOLE, FLAT)
     first, second = steps(field0, field1, field2, pot, far_z)
     sweep(field0, far_z, bands, *IN1, IN1[1] - IN1[0], first)
     sweep(field1, far_z, bands, *IN2, IN2[1] - IN2[0], second)
 
 
-def outer_kernel(
-    core, low, high, low_pot, high_pot, far_low, far_high, _0, _1, _2, _3,
-    out, field0, field1, field2, pot, far_z,
-):
+def edge_kernel(low, high, _, field0, far_z):
     bands = band_parts()
 
     def edge(i, carry):
@@ -198,9 +200,18 @@
         return carry
 
     lax.fori_loop(0, DEEP, edge, 0)
+    along_z(field0, far_z, bands, REACH, 0, IN1[0])
+    along_z(field0, far_z, bands, REACH + IN1[1], IN1[1], SLAB + 2 * FLAT - IN1[1])
+
+
+def outer_kernel(
+    core, low_pot, high_pot, far_low, far_high, field0, _1, _2, _3, _4,
+    out, field1, field2, pot, far_z,
+):
+    bands = band_parts()
     mine = core[0]
-    put_pots(pot, mine, (low_pot, far_low), FLAT - 2 * BX, (0, None))
-    put_pots(pot, mine, (high_pot, far_high), FLAT + SLAB, (None, 1))
+    put_pots(pot, mine, (low_pot, far_low), ((0, 2), (4, 8), (6, 10)), 0)
+    put_pots(pot, mine, (high_pot, far_high), ((0, 4), (2, 6), (8, 10)), FLAT + SLAB)
     first, second = steps(field0, field1, field2, pot, far_z)
 
     def third(i):
@@ -212,8 +223,9 @@
                 )
 
     ends1, ends2 = SLAB + 2 * FLAT, SLAB + FLAT
-    sweep(field0, far_z, bands, 0, IN1[0], IN1[0], first)
-    sweep(field0, far_z, bands, IN1[1], ends1, ends1 - IN1[1], first)
+    for begin, end in ((0, IN1[0]), (IN1[1], ends1)):
+        for r in range(begin, end, 2):
+            first(r)
     sweep(field1, far_z, bands, 0, IN2[0], IN2[0], second)
     sweep(field1, far_z, bands, IN2[1], ends2, ends2 - IN2[1], second)
     sweep(field2, far_z, bands, 0, SLAB, SLAB // 2, third)
@@ -357,15 +369,20 @@
     slabs = lax.axis_size("s")
     group = lax.axis_size("z") * lax.axis_size("gy")
     core = lax.axis_index("gy") & 1
+    away = pl.BlockSpec(memory_space=pltpu.HBM)
     sent = call(
         message_kernel,
         f32(group, PAIR, BLOCK, BX, 128),
-        [VMEM, VMEM],
-    )(orbitals.reshape(group, PAIR, BX, BX, 128), potential)
+        [away, away],
+        [pltpu.VMEM((BX, BX, 128), jnp.float32), pltpu.SemaphoreType.DMA((2,))],
+    )(
+        pltpu.with_memory_space_constraint(orbitals.reshape(group, PAIR, BX, BX, 128), pltpu.HBM),
+        pltpu.with_memory_space_constraint(potential, pltpu.HBM),
+    )
     got = lax.all_to_all(sent, ("z", "gy"), 0, 0, tiled=True)
     got = got.reshape(group * PAIR * BLOCK * BX, 128)
     up, down, up_pot, down_pot, mid_pot = call(
-        pack_kernel, (f32(DEEP, 8, 8, 128),) * 2 + (f32(4, 8, 8, 128),) * 2 + (f32(8, 8, 8, 128),), [VMEM]
+        pack_kernel, (f32(DEEP, 8, 8, 128),) * 2 + (f32(3, 8, 8, 128),) * 2 + (f32(8, 8, 8, 128),), [VMEM]
     )(got)
     ring = [(i, (i + 1) % slabs) for i in range(slabs)]
     back_ring = [(j, i) for i, j in ring]
@@ -385,14 +402,18 @@
     low_pot, high_pot, inner = lax.optimization_barrier((low_pot, high_pot, inner))
     far_low = lax.ppermute(low_pot, "gy", twin)
     far_high = lax.ppermute(high_pot, "gy", twin)
+    field0, field1, field2, pot = inner
+    field0, products = call(
+        edge_kernel, (fields[0], fields[3]), [VMEM] * 3, (), 10, flops=1 << 30, aliases={2: 0}
+    )(low, high, field0)
     filtered = call(
         outer_kernel,
-        (f32(group * PAIR * BX * BX, 128),) + fields,
-        [SMEM] + [VMEM] * 10,
-        far_z,
+        (f32(group * PAIR * BX * BX, 128),) + fields[1:] + (fields[3],),
+        [SMEM] + [VMEM] * 9,
+        (),
         10,
-        aliases={7 + k: 1 + k for k in range(4)},
-    )(*own, low, high, low_pot, high_pot, far_low, far_high, *inner)[0]
+        aliases={6 + k: 1 + k for k in range(4)},
+    )(*own, low_pot, high_pot, far_low, far_high, field0, field1, field2, pot, products)[0]
     filtered = filtered.reshape(group, PAIR, BX, BX, 128)
     back = lax.all_to_all(filtered, ("z", "gy"), 0, 0, tiled=True).reshape(n, BX, BX, 128)
     devices = slabs * group

time: 106 us -> 104 us (0.981)
  local copies, waits for them, and re-layouts: 2.64 us -> 0 us
  Pallas kernels: 15.7 us -> 17.8 us
  waiting for transfers between devices: 11.4 us -> 9.74 us
    unnamed x6 -> x0, local copies, waits for them, and re-layouts: 2.64 us -> none
    pallas_call x3 -> x4, Pallas kernels: 7.53 us -> 9.45 us  [the longest x1 6.15 us: per_device(): call(outer_kernel, (f32(group * PAIR * BX * BX, 128),) + fields[1:] + (fi...]
  transfers between devices with their start and end apart: 7 -> 7, of which waited for: 3 -> 3; matrix products, arithmetic and copies ran while one was open for 0% -> 0% of each run, Pallas kernels for 3% -> 4%
where the time goes in v6:
time: 104 us; the launch traced here: 103 us
  blocking collectives  66.2 us (64%)
  Pallas kernels  17.8 us (17%)
  waiting for transfers between devices  9.74 us (9%)
  starting transfers between devices  8.92 us (9%)
    all_to_all x1, blocking collectives, per_device(): got = lax.all_to_all(sent, ('z', 'gy'), 0, 0, tiled=True)  29.2 us
    all_to_all x1, blocking collectives, per_device(): lax.all_to_all(filtered, ('z', 'gy'), 0, 0, tiled=True)  19.6 us
    all_to_all x1, blocking collectives, per_device(): lax.all_to_all(parts.reshape(devices, 1, 5 * 128), ('s', 'z', 'gy'), 0, 0...  17.5 us
    ppermute x1, waiting for transfers between devices, per_device(): low_pot = lax.ppermute(up_pot, 's', ring)  9.2 us
    pallas_call x1, Pallas kernels, per_device(): call(outer_kernel, (f32(group * PAIR * BX * BX, 128),) + fields[1:] + (fi...  6.15 us
    ppermute x1, starting transfers between devices, per_device(): high_pot = lax.ppermute(down_pot, 's', back_ring)  3.57 us
    pallas_call x1, Pallas kernels, per_device(): call(finish_kernel, (f32(n, BX, BX, 128), f32(n, n)), [VMEM, VMEM])  3.42 us
    pallas_call x1, Pallas kernels, per_device(): call(inner_kernel, fields, [SMEM] + [VMEM] * 3, far_z, 10, flops=1 << 32)  3.02 us
  transfers between devices with their start and end apart: 7, of which 3 were waited for; matrix products, arithmetic and copies ran while one was open for 0% of the time, Pallas kernels for 4%

profile of v6, /device:TPU:1, one launch (start us, length us, event | category | flops | bytes accessed | tf_op | source)
XLA Modules:
  0.0 103.3 jit_solution(6000418298629023101)
XLA Ops:
  0.6 1.3 %shard_map.41 = f32[16,2,10,8,128]{4,3,2,1,0:T(8,128)S(1)} custom-call(f32[16,2,8,8,128]{4,3,2,1,0:T(8,128)} %bitcast.14, f32[8,8,128]{2,1,0:T(8,128)} %potential.1), custom_call_target="tpu_custom_call" | custom-call | tf_op jit(solution)/shard_map/pallas_call | solution.py:373
  1.9 29.2 %all_to_all.15 = f32[16,2,10,8,128]{4,3,2,1,0:T(8,128)S(1)} all-to-all(f32[16,2,10,8,128]{4,3,2,1,0:T(8,128)S(1)} %shard_map.41), channel_id=1, replica_groups=mesh['s'=8,'z'=4,'gy'=4] {'z','gy'}, dimensions={0} | all-to-all | bytes 2621440 | tf_op jit(solution)/shard_map/all_to_all | solution.py:382
  31.1 1.3 %shard_map.42 = (f32[18,8,8,128]{3,2,1,0:T(8,128)}, f32[18,8,8,128]{3,2,1,0:T(8,128)S(1)}, f32[3,8,8,128]{3,2,1,0:T(8,128)S(1)}, f32[3,8,8,128]{3,2,1,0:T(8,128)S(1)}, f32[8,8,8,128]{3,2,1,0:T(8,128)S(1)}) custom-call(f32[2560,128]{1,0:T(8,128)S(1)} %bitcast.9), custom_call_target="tpu_custom_call" | custom-call | tf_op jit(solution)/shard_map/pallas_call | solution.py:384
  32.3 1.0 collective-permute-start.2
  33.3 1.2 %collective-permute-start.5 = (f32[18,8,8,128]{3,2,1,0:T(8,128)}, f32[18,8,8,128]{3,2,1,0:T(8,128)S(1)}, u32[]{:S(2)}, u32[]{:S(2)}) collective-permute-start(f32[18,8,8,128]{3,2,1,0:T(8,128)} %get-tuple-element.29), channel_id=1, source_target_pairs={{0,16},{16,32},{32,48},{48,64},{64,80},{80,96},{96,112},{112,0},{1... | collective-permute-start | bytes 1769480 | tf_op jit(solution)/shard_map/ppermute | solution.py:392
  34.5 2.4 %collective-permute-start.6 = (f32[18,8,8,128]{3,2,1,0:T(8,128)S(1)}, f32[18,8,8,128]{3,2,1,0:T(8,128)S(1)}, u32[]{:S(2)}, u32[]{:S(2)}) collective-permute-start(f32[18,8,8,128]{3,2,1,0:T(8,128)S(1)} %get-tuple-element.30), channel_id=1, source_target_pairs={{16,0},{32,16},{48,32},{64,48},{80,64},{96,80},{112,96},{0,112},{1... | collective-permute-start | bytes 1769480 | tf_op jit(solution)/shard_map/ppermute | solution.py:393
  36.9 0.0 collective-permute-start
  36.9 3.6 %collective-permute-start.1 = (f32[3,8,8,128]{3,2,1,0:T(8,128)S(1)}, f32[3,8,8,128]{3,2,1,0:T(8,128)S(1)}, u32[]{:S(2)}, u32[]{:S(2)}) collective-permute-start(f32[3,8,8,128]{3,2,1,0:T(8,128)S(1)} %get-tuple-element.21), channel_id=1, source_target_pairs={{16,0},{32,16},{48,32},{64,48},{80,64},{96,80},{112,96},{0,112},{1... | collective-permute-start | bytes 294920 | tf_op jit(solution)/shard_map/ppermute | solution.py:391
  40.5 0.0 collective-permute-done.2.far_mid
  40.5 3.0 %shard_map.43 = (f32[68,8,16,128]{3,2,1,0:T(8,128)S(1)}, f32[56,8,16,128]{3,2,1,0:T(8,128)S(1)}, f32[44,8,16,128]{3,2,1,0:T(8,128)S(1)}, f32[56,8,8,128]{3,2,1,0:T(8,128)S(1)}) custom-call(s32[1]{0:T(128)} %bitcast.core, f32[2560,128]{1,0:T(8,128)S(1)} %bitcast.10, f32[8,8,8,128]{3,2,1,0:T(8,128)S(1)} %get-tuple-element.22.mid_pot, ...), custom_call_target="tpu_custom_call" | custom-call | flops 4294967296 | tf_op jit(solution)/shard_map/pallas_call | solution.py:399
  43.5 9.2 %collective-permute-done.low_pot = f32[3,8,8,128]{3,2,1,0:T(8,128)S(1)} collective-permute-done((f32[3,8,8,128]{3,2,1,0:T(8,128)S(1)}, f32[3,8,8,128]{3,2,1,0:T(8,128)S(1)}, u32[]{:S(2)}, u32[]{:S(2)}) %collective-permute-start) | collective-permute-done | bytes 98336 | tf_op jit(solution)/shard_map/ppermute | solution.py:390
  52.7 0.0 collective-permute-done.1.high_pot
  52.7 0.8 collective-permute-start.3
  53.5 0.0 collective-permute-start.4
  53.5 0.0 collective-permute-done.5.low
  53.5 0.0 collective-permute-done.6.high
  53.5 0.8 shard_map.44
  54.3 0.2 collective-permute-done.3.far_low
  54.4 0.4 collective-permute-done.4.far_high
  54.8 6.2 %shard_map.45 = (f32[2048,128]{1,0:T(8,128)S(1)}, f32[56,8,16,128]{3,2,1,0:T(8,128)S(1)}, f32[44,8,16,128]{3,2,1,0:T(8,128)S(1)}, f32[56,8,8,128]{3,2,1,0:T(8,128)S(1)}, f32[56,8,8,128]{3,2,1,0:T(8,128)S(1)}) custom-call(s32[1]{0:T(128)} %bitcast.core, ...), custom_call_target="tpu_custom_call", output_to_operand_aliasing={{1}: (6, {}), {2}: (7, {}), {3}: (8, {}), {4}: (9, {})} | custom-call | tf_op jit(solution)/shard_map/pallas_call | solution.py:409
  61.0 19.6 %all_to_all.16 = f32[16,2,8,8,128]{4,3,2,1,0:T(8,128)S(1)} all-to-all(f32[16,2,8,8,128]{4,3,2,1,0:T(8,128)S(1)} %bitcast.13), channel_id=1, replica_groups=mesh['s'=8,'z'=4,'gy'=4] {'z','gy'}, dimensions={0} | all-to-all | bytes 2097152 | tf_op jit(solution)/shard_map/all_to_all | solution.py:418
  80.6 1.9 %shard_map.46 = f32[640,128]{1,0:T(8,128)S(1)} custom-call(f32[32,8,8,128]{3,2,1,0:T(8,128)S(1)} %bitcast.7), custom_call_target="tpu_custom_call" | custom-call | tf_op jit(solution)/shard_map/pallas_call | solution.py:421
  82.4 17.5 %all_to_all.17 = f32[128,1,640]{2,1,0:T(1,128)S(1)} all-to-all(f32[128,1,640]{2,1,0:T(1,128)S(1)} %bitcast.12), channel_id=1, replica_groups=mesh['s'=8,'z'=4,'gy'=4] {'s','z','gy'}, dimensions={0} | all-to-all | bytes 655360 | tf_op jit(solution)/shard_map/all_to_all | solution.py:424
  99.9 3.4 %shard_map.47 = (f32[32,8,8,128]{3,2,1,0:T(8,128)}, f32[32,32]{1,0:T(8,128)}) custom-call(f32[640,128]{1,0:T(8,128)S(1)} %bitcast.11, f32[32,8,8,128]{3,2,1,0:T(8,128)S(1)} %bitcast.8), custom_call_target="tpu_custom_call" | custom-call | tf_op jit(solution)/shard_map/pallas_call | solution.py:427
Async XLA Ops:
  32.3 8.1 %collective-permute-start.2 = (f32[8,8,8,128]{3,2,1,0:T(8,128)S(1)}, f32[8,8,8,128]{3,2,1,0:T(8,128)}, u32[]{:S(2)}, u32[]{:S(2)}) collective-permute-start(f32[8,8,8,128]{3,2,1,0:T(8,128)S(1)} %get-tuple-element.22.mid_pot), channel_id=1, source_target_pairs={{0,1},{1,0},{2,3},{3,2},{4,5},{5,4},{6,7},{7,6},{8,9},{9,8},{10,11... | collective-permute-start | bytes 786440 | tf_op jit(solution)/shard_map/ppermute | solution.py:394
  33.3 20.2 %collective-permute-start.5 = (f32[18,8,8,128]{3,2,1,0:T(8,128)}, f32[18,8,8,128]{3,2,1,0:T(8,128)S(1)}, u32[]{:S(2)}, u32[]{:S(2)}) collective-permute-start(f32[18,8,8,128]{3,2,1,0:T(8,128)} %get-tuple-element.29), channel_id=1, source_target_pairs={{0,16},{16,32},{32,48},{48,64},{64,80},{80,96},{96,112},{112,0},{1... | collective-permute-start | bytes 1769480 | tf_op jit(solution)/shard_map/ppermute | solution.py:392
  34.5 19.0 %collective-permute-start.6 = (f32[18,8,8,128]{3,2,1,0:T(8,128)S(1)}, f32[18,8,8,128]{3,2,1,0:T(8,128)S(1)}, u32[]{:S(2)}, u32[]{:S(2)}) collective-permute-start(f32[18,8,8,128]{3,2,1,0:T(8,128)S(1)} %get-tuple-element.30), channel_id=1, source_target_pairs={{16,0},{32,16},{48,32},{64,48},{80,64},{96,80},{112,96},{0,112},{1... | collective-permute-start | bytes 1769480 | tf_op jit(solution)/shard_map/ppermute | solution.py:393
  36.9 15.8 %collective-permute-start = (f32[3,8,8,128]{3,2,1,0:T(8,128)S(1)}, f32[3,8,8,128]{3,2,1,0:T(8,128)S(1)}, u32[]{:S(2)}, u32[]{:S(2)}) collective-permute-start(f32[3,8,8,128]{3,2,1,0:T(8,128)S(1)} %get-tuple-element.20), channel_id=1, source_target_pairs={{0,16},{16,32},{32,48},{48,64},{64,80},{80,96},{96,112},{112,0},{1... | collective-permute-start | bytes 294920 | tf_op jit(solution)/shard_map/ppermute | solution.py:390
  36.9 15.8 %collective-permute-start.1 = (f32[3,8,8,128]{3,2,1,0:T(8,128)S(1)}, f32[3,8,8,128]{3,2,1,0:T(8,128)S(1)}, u32[]{:S(2)}, u32[]{:S(2)}) collective-permute-start(f32[3,8,8,128]{3,2,1,0:T(8,128)S(1)} %get-tuple-element.21), channel_id=1, source_target_pairs={{16,0},{32,16},{48,32},{64,48},{80,64},{96,80},{112,96},{0,112},{1... | collective-permute-start | bytes 294920 | tf_op jit(solution)/shard_map/ppermute | solution.py:391
  52.7 1.7 %collective-permute-start.3 = (f32[3,8,8,128]{3,2,1,0:T(8,128)S(1)}, f32[3,8,8,128]{3,2,1,0:T(8,128)S(1)}, u32[]{:S(2)}, u32[]{:S(2)}) collective-permute-start(f32[3,8,8,128]{3,2,1,0:T(8,128)S(1)} %collective-permute-done.low_pot), channel_id=1, source_target_pairs={{0,1},{1,0},{2,3},{3,2},{4,5},{5,4},{6,7},{7,6},{8,9},{9,8},{10,11... | collective-permute-start | bytes 294920 | tf_op jit(solution)/shard_map/ppermute | solution.py:403
  53.5 1.3 %collective-permute-start.4 = (f32[3,8,8,128]{3,2,1,0:T(8,128)S(1)}, f32[3,8,8,128]{3,2,1,0:T(8,128)S(1)}, u32[]{:S(2)}, u32[]{:S(2)}) collective-permute-start(f32[3,8,8,128]{3,2,1,0:T(8,128)S(1)} %collective-permute-done.1.high_pot), channel_id=1, source_target_pairs={{0,1},{1,0},{2,3},{3,2},{4,5},{5,4},{6,7},{7,6},{8,9},{9,8},{10,11... | collective-permute-start | bytes 294920 | tf_op jit(solution)/shard_map/ppermute | solution.py:404

commit v7 on v6

--- a/solution.py
+++ b/solution.py
@@ -30,6 +30,7 @@
 REACH = 6
 DEEP = 3 * REACH
 FLAT = 2 * REACH
+FLOWS = 4
 STEP = 4
 PAIR = 2
 IN1 = (DEEP, DEEP + 20)
@@ -46,19 +47,26 @@
 
 
 def message_kernel(orbitals, potential, out, rows, arrived):
-    copy = pltpu.make_async_copy(orbitals, out.at[:, :, 0:BX], arrived.at[0])
-    flat = pltpu.make_async_copy(potential, rows, arrived.at[1])
+    flat = pltpu.make_async_copy(potential, rows, arrived.at[FLOWS])
     flat.start()
-    copy.start()
+    part = out.shape[0] // FLOWS
+    copies = []
+    for f in range(FLOWS):
+        some = pl.ds(f * part, part)
+        copies.append(
+            pltpu.make_async_copy(orbitals.at[some], out.at[some, :, 0:BX], arrived.at[f])
+        )
+        copies[-1].start()
     flat.wait()
     for d in range(out.shape[0]):
         for o in range(PAIR):
             for k in range(2):
                 out[d, o, BX + k] = rows[4 * o + 2 * k + d % 2]
-    copy.wait()
-
-
-def pack_kernel(got, up, down, up_pot, down_pot, mid_pot):
+    for copy in copies:
+        copy.wait()
+
+
+def pack_kernel(got, up, down, mid_pot):
     for dest, first in ((up, SLAB - DEEP), (down, 0)):
         for i in range(DEEP):
             z, xi = divmod(first + i, BX)
@@ -70,11 +78,11 @@
         for z in range(4):
             for k in range(2):
                 mid_pot[2 * z + k, yi] = tiles[z][k]
-        up_pot[0, yi] = jnp.where(odd, tiles[2][1], pltpu.roll(tiles[2][0], 7, 0))
-        down_pot[2, yi] = jnp.where(odd, pltpu.roll(tiles[1][1], 1, 0), tiles[1][0])
+        up[DEEP, yi] = jnp.where(odd, tiles[2][1], pltpu.roll(tiles[2][0], 7, 0))
+        down[DEEP + 2, yi] = jnp.where(odd, pltpu.roll(tiles[1][1], 1, 0), tiles[1][0])
         for k in range(2):
-            up_pot[1 + k, yi] = tiles[3][k]
-            down_pot[k, yi] = tiles[0][k]
+            up[DEEP + 1 + k, yi] = tiles[3][k]
+            down[DEEP + k, yi] = tiles[0][k]
 
 
 def put(field, row, tiles):
@@ -191,6 +199,11 @@
     sweep(field1, far_z, bands, *IN2, IN2[1] - IN2[0], second)
 
 
+def pots_kernel(low, high, low_pot, high_pot):
+    low_pot[...] = low[DEEP:]
+    high_pot[...] = high[DEEP:]
+
+
 def edge_kernel(low, high, _, field0, far_z):
     bands = band_parts()
 
@@ -256,16 +269,22 @@
     return jnp.concatenate([y[:, x].reshape(rows, 128), y[:, x + 1].reshape(rows, 128)], axis=1)
 
 
+def across(a, b):
+    return lax.dot_general(a, b, (((1,), (1,)), ((), ())), preferred_element_type=jnp.float32)
+
+
 def gram_kernel(scale, y, out):
     n = y.shape[0]
     total = None
     for x in range(0, BX, 2):
-        block = pair_of_rows(y, x)
-        part = dot(block, block, ((1,), (1,)))
+        high, middle, low = parts_of(pair_of_rows(y, x))
+        part = 0.5 * (across(high, high) + across(middle, middle))
+        part = part + (across(high, middle) + across(high, low))
         total = part if total is None else total + part
     total = jnp.where(same_y(n), total, 0.0) * scale
     ones = spread(n)
     gram = dot(dot(ones, total, ((0,), (0,))), ones)
+    gram = gram + gram.T
     half = n // 2
     upper = iota((half, half), 0) <= iota((half, half), 1)
     kept = jnp.concatenate(
@@ -374,21 +393,19 @@
         message_kernel,
         f32(group, PAIR, BLOCK, BX, 128),
         [away, away],
-        [pltpu.VMEM((BX, BX, 128), jnp.float32), pltpu.SemaphoreType.DMA((2,))],
+        [pltpu.VMEM((BX, BX, 128), jnp.float32), pltpu.SemaphoreType.DMA((FLOWS + 1,))],
     )(
         pltpu.with_memory_space_constraint(orbitals.reshape(group, PAIR, BX, BX, 128), pltpu.HBM),
         pltpu.with_memory_space_constraint(potential, pltpu.HBM),
     )
     got = lax.all_to_all(sent, ("z", "gy"), 0, 0, tiled=True)
     got = got.reshape(group * PAIR * BLOCK * BX, 128)
-    up, down, up_pot, down_pot, mid_pot = call(
-        pack_kernel, (f32(DEEP, 8, 8, 128),) * 2 + (f32(3, 8, 8, 128),) * 2 + (f32(8, 8, 8, 128),), [VMEM]
+    up, down, mid_pot = call(
+        pack_kernel, (f32(DEEP + 3, 8, 8, 128),) * 2 + (f32(8, 8, 8, 128),), [VMEM]
     )(got)
     ring = [(i, (i + 1) % slabs) for i in range(slabs)]
     back_ring = [(j, i) for i, j in ring]
     twin = [(i, i ^ 1) for i in range(lax.axis_size("gy"))]
-    low_pot = lax.ppermute(up_pot, "s", ring)
-    high_pot = lax.ppermute(down_pot, "s", back_ring)
     low = lax.ppermute(up, "s", ring)
     high = lax.ppermute(down, "s", back_ring)
     far_mid = lax.ppermute(mid_pot, "gy", twin)
@@ -399,7 +416,8 @@
     inner = call(inner_kernel, fields, [SMEM] + [VMEM] * 3, far_z, 10, flops=1 << 32)(
         *own, got, mid_pot, far_mid
     )
-    low_pot, high_pot, inner = lax.optimization_barrier((low_pot, high_pot, inner))
+    low, high, inner = lax.optimization_barrier((low, high, inner))
+    low_pot, high_pot = call(pots_kernel, (f32(3, 8, 8, 128),) * 2, [VMEM] * 2)(low, high)
     far_low = lax.ppermute(low_pot, "gy", twin)
     far_high = lax.ppermute(high_pot, "gy", twin)
     field0, field1, field2, pot = inner
@@ -422,7 +440,7 @@
         functools.partial(gram_kernel, 1.0 / cells), f32(devices * 5, 128), [VMEM]
     )(back)
     parts = lax.all_to_all(
-        parts.reshape(devices, 1, 5 * 128), ("s", "z", "gy"), 0, 0, tiled=True
+        parts.reshape(devices, 1, 5 * 128), ("gy", "z", "s"), 0, 0, tiled=True
     ).reshape(devices * 5, 128)
     return call(finish_kernel, (f32(n, BX, BX, 128), f32(n, n)), [VMEM, VMEM])(parts, back)
 

time: 104 us -> 103 us (level)
  starting transfers between devices: 8.92 us -> 7.18 us
    ppermute x2 -> x0, waiting for transfers between devices: 9.21 us -> none  [the longest x1 9.2 us: per_device(): low_pot = lax.ppermute(up_pot, 's', ring)]
    ppermute x1, waiting for transfers between devices: 0.01 us -> 8.54 us  [per_device(): low = lax.ppermute(up, 's', ring)]
    ppermute x2 -> x0, starting transfers between devices: 3.58 us -> none  [the longest x1 3.57 us: per_device(): high_pot = lax.ppermute(down_pot, 's', back_ring)]
    ppermute x1, waiting for transfers between devices: 0.01 us -> 1.5 us  [per_device(): far_mid = lax.ppermute(mid_pot, 'gy', twin)]
    ppermute x1, starting transfers between devices: 0.79 us -> 1.98 us  [per_device(): far_low = lax.ppermute(low_pot, 'gy', twin)]
  transfers between devices with their start and end apart: 7 -> 5, of which waited for: 3 -> 4; matrix products, arithmetic and copies ran while one was open for 0% -> 0% of each run, Pallas kernels for 4% -> 4%
where the time goes in v7:
time: 103 us
  blocking collectives  66.7 us (65%)
  Pallas kernels  17.5 us (17%)
  waiting for transfers between devices  10.5 us (10%)
  starting transfers between devices  7.18 us (7%)
    all_to_all x1, blocking collectives, per_device(): got = lax.all_to_all(sent, ('z', 'gy'), 0, 0, tiled=True)  29.2 us
    all_to_all x1, blocking collectives, per_device(): lax.all_to_all(filtered, ('z', 'gy'), 0, 0, tiled=True)  19.9 us
    all_to_all x1, blocking collectives, per_device(): lax.all_to_all(parts.reshape(devices, 1, 5 * 128), ('gy', 'z', 's'), 0, 0...  17.6 us
    ppermute x1, waiting for transfers between devices, per_device(): low = lax.ppermute(up, 's', ring)  8.54 us
    pallas_call x1, Pallas kernels, per_device(): call(outer_kernel, (f32(group * PAIR * BX * BX, 128),) + fields[1:] + (fi...  6.1 us
    pallas_call x1, Pallas kernels, per_device(): call(finish_kernel, (f32(n, BX, BX, 128), f32(n, n)), [VMEM, VMEM])  3.42 us
    pallas_call x1, Pallas kernels, per_device(): call(inner_kernel, fields, [SMEM] + [VMEM] * 3, far_z, 10, flops=1 << 32)  3.1 us
    ppermute x1, starting transfers between devices, per_device(): high = lax.ppermute(down, 's', back_ring)  2.36 us
  transfers between devices with their start and end apart: 5, of which 4 were waited for; matrix products, arithmetic and copies ran while one was open for 0% of the time, Pallas kernels for 4%

profile of v7, /device:TPU:1, one launch (start us, length us, event | category | flops | bytes accessed | tf_op | source)
XLA Modules:
  0.0 102.6 jit_solution(14616277931338892243)
XLA Ops:
  0.6 1.2 %shard_map.41 = f32[16,2,10,8,128]{4,3,2,1,0:T(8,128)S(1)} custom-call(f32[16,2,8,8,128]{4,3,2,1,0:T(8,128)} %bitcast.14, f32[8,8,128]{2,1,0:T(8,128)} %potential.1), custom_call_target="tpu_custom_call" | custom-call | tf_op jit(solution)/shard_map/pallas_call | solution.py:392
  1.9 29.2 %all_to_all.15 = f32[16,2,10,8,128]{4,3,2,1,0:T(8,128)S(1)} all-to-all(f32[16,2,10,8,128]{4,3,2,1,0:T(8,128)S(1)} %shard_map.41), channel_id=1, replica_groups=mesh['s'=8,'z'=4,'gy'=4] {'z','gy'}, dimensions={0} | all-to-all | bytes 2621440 | tf_op jit(solution)/shard_map/all_to_all | solution.py:401
  31.1 1.4 %shard_map.42 = (f32[21,8,8,128]{3,2,1,0:T(8,128)}, f32[21,8,8,128]{3,2,1,0:T(8,128)S(1)}, f32[8,8,8,128]{3,2,1,0:T(8,128)}) custom-call(f32[2560,128]{1,0:T(8,128)S(1)} %bitcast.9), custom_call_target="tpu_custom_call" | custom-call | tf_op jit(solution)/shard_map/pallas_call | solution.py:403
  32.4 1.2 %collective-permute-start = (f32[21,8,8,128]{3,2,1,0:T(8,128)}, f32[21,8,8,128]{3,2,1,0:T(8,128)S(1)}, u32[]{:S(2)}, u32[]{:S(2)}) collective-permute-start(f32[21,8,8,128]{3,2,1,0:T(8,128)} %get-tuple-element.20), channel_id=1, source_target_pairs={{0,16},{16,32},{32,48},{48,64},{64,80},{80,96},{96,112},{112,0},{1... | collective-permute-start | bytes 2064392 | tf_op jit(solution)/shard_map/ppermute | solution.py:409
  33.7 2.4 %collective-permute-start.1 = (f32[21,8,8,128]{3,2,1,0:T(8,128)S(1)}, f32[21,8,8,128]{3,2,1,0:T(8,128)S(1)}, u32[]{:S(2)}, u32[]{:S(2)}) collective-permute-start(f32[21,8,8,128]{3,2,1,0:T(8,128)S(1)} %get-tuple-element.21), channel_id=1, source_target_pairs={{16,0},{32,16},{48,32},{64,48},{80,64},{96,80},{112,96},{0,112},{1... | collective-permute-start | bytes 2064392 | tf_op jit(solution)/shard_map/ppermute | solution.py:410
  36.0 1.5 %collective-permute-start.2 = (f32[8,8,8,128]{3,2,1,0:T(8,128)}, f32[8,8,8,128]{3,2,1,0:T(8,128)}, u32[]{:S(2)}, u32[]{:S(2)}) collective-permute-start(f32[8,8,8,128]{3,2,1,0:T(8,128)} %get-tuple-element.22.mid_pot), channel_id=1, source_target_pairs={{0,1},{1,0},{2,3},{3,2},{4,5},{5,4},{6,7},{7,6},{8,9},{9,8},{10,11... | collective-permute-start | bytes 786440 | tf_op jit(solution)/shard_map/ppermute | solution.py:411
  37.6 1.5 %collective-permute-done.2.far_mid = f32[8,8,8,128]{3,2,1,0:T(8,128)} collective-permute-done((f32[8,8,8,128]{3,2,1,0:T(8,128)}, f32[8,8,8,128]{3,2,1,0:T(8,128)}, u32[]{:S(2)}, u32[]{:S(2)}) %collective-permute-start.2) | collective-permute-done | bytes 262176 | tf_op jit(solution)/shard_map/ppermute | solution.py:411
  39.1 3.1 %shard_map.43 = (f32[68,8,16,128]{3,2,1,0:T(8,128)S(1)}, f32[56,8,16,128]{3,2,1,0:T(8,128)S(1)}, f32[44,8,16,128]{3,2,1,0:T(8,128)S(1)}, f32[56,8,8,128]{3,2,1,0:T(8,128)S(1)}) custom-call(s32[1]{0:T(128)} %bitcast.core, f32[2560,128]{1,0:T(8,128)S(1)} %bitcast.10, f32[8,8,8,128]{3,2,1,0:T(8,128)} %get-tuple-element.22.mid_pot, ...), custom_call_target="tpu_custom_call" | custom-call | flops 4294967296 | tf_op jit(solution)/shard_map/pallas_call | solution.py:416
  42.2 8.5 %collective-permute-done.low = f32[21,8,8,128]{3,2,1,0:T(8,128)S(1)} collective-permute-done((f32[21,8,8,128]{3,2,1,0:T(8,128)}, f32[21,8,8,128]{3,2,1,0:T(8,128)S(1)}, u32[]{:S(2)}, u32[]{:S(2)}) %collective-permute-start) | collective-permute-done | bytes 688160 | tf_op jit(solution)/shard_map/ppermute | solution.py:409
  50.7 0.0 collective-permute-done.1.high
  50.7 2.0 %collective-permute-start.3 = (f32[3,8,8,128]{3,2,1,0:T(8,128)S(1)}, f32[3,8,8,128]{3,2,1,0:T(8,128)S(1)}, u32[]{:S(2)}, u32[]{:S(2)}) collective-permute-start(f32[3,8,8,128]{3,2,1,0:T(8,128)S(1)} %get-tuple-element.29.low_pot), channel_id=1, source_target_pairs={{0,1},{1,0},{2,3},{3,2},{4,5},{5,4},{6,7},{7,6},{8,9},{9,8},{10,11... | collective-permute-start | bytes 294920 | tf_op jit(solution)/shard_map/ppermute | solution.py:421
  52.7 0.1 collective-permute-start.4
  52.8 0.8 shard_map.45
  53.6 0.1 collective-permute-done.3.far_low
  53.7 0.4 collective-permute-done.4.far_high
  54.0 6.1 %shard_map.46 = (f32[2048,128]{1,0:T(8,128)S(1)}, f32[56,8,16,128]{3,2,1,0:T(8,128)S(1)}, f32[44,8,16,128]{3,2,1,0:T(8,128)S(1)}, f32[56,8,8,128]{3,2,1,0:T(8,128)S(1)}, f32[56,8,8,128]{3,2,1,0:T(8,128)S(1)}) custom-call(s32[1]{0:T(128)} %bitcast.core, ...), custom_call_target="tpu_custom_call", output_to_operand_aliasing={{1}: (6, {}), {2}: (7, {}), {3}: (8, {}), {4}: (9, {})} | custom-call | tf_op jit(solution)/shard_map/pallas_call | solution.py:427
  60.1 19.9 %all_to_all.16 = f32[16,2,8,8,128]{4,3,2,1,0:T(8,128)S(1)} all-to-all(f32[16,2,8,8,128]{4,3,2,1,0:T(8,128)S(1)} %bitcast.13), channel_id=1, replica_groups=mesh['s'=8,'z'=4,'gy'=4] {'z','gy'}, dimensions={0} | all-to-all | bytes 2097152 | tf_op jit(solution)/shard_map/all_to_all | solution.py:436
  80.1 1.5 %shard_map.47 = f32[640,128]{1,0:T(8,128)S(1)} custom-call(f32[32,8,8,128]{3,2,1,0:T(8,128)S(1)} %bitcast.7), custom_call_target="tpu_custom_call" | custom-call | tf_op jit(solution)/shard_map/pallas_call | solution.py:439
  81.6 17.6 %all_to_all.17 = f32[128,1,640]{2,1,0:T(1,128)S(1)} all-to-all(f32[128,1,640]{2,1,0:T(1,128)S(1)} %bitcast.12), channel_id=1, replica_groups=mesh['s'=8,'z'=4,'gy'=4] {'gy','z','s'}, dimensions={0} | all-to-all | bytes 655360 | tf_op jit(solution)/shard_map/all_to_all | solution.py:442
  99.1 3.4 %shard_map.48 = (f32[32,8,8,128]{3,2,1,0:T(8,128)}, f32[32,32]{1,0:T(8,128)}) custom-call(f32[640,128]{1,0:T(8,128)S(1)} %bitcast.11, f32[32,8,8,128]{3,2,1,0:T(8,128)S(1)} %bitcast.8), custom_call_target="tpu_custom_call" | custom-call | tf_op jit(solution)/shard_map/pallas_call | solution.py:445
  (1 shorter events, 0.0 us)
Async XLA Ops:
  32.4 18.3 %collective-permute-start = (f32[21,8,8,128]{3,2,1,0:T(8,128)}, f32[21,8,8,128]{3,2,1,0:T(8,128)S(1)}, u32[]{:S(2)}, u32[]{:S(2)}) collective-permute-start(f32[21,8,8,128]{3,2,1,0:T(8,128)} %get-tuple-element.20), channel_id=1, source_target_pairs={{0,16},{16,32},{32,48},{48,64},{64,80},{80,96},{96,112},{112,0},{1... | collective-permute-start | bytes 2064392 | tf_op jit(solution)/shard_map/ppermute | solution.py:409
  33.7 17.1 %collective-permute-start.1 = (f32[21,8,8,128]{3,2,1,0:T(8,128)S(1)}, f32[21,8,8,128]{3,2,1,0:T(8,128)S(1)}, u32[]{:S(2)}, u32[]{:S(2)}) collective-permute-start(f32[21,8,8,128]{3,2,1,0:T(8,128)S(1)} %get-tuple-element.21), channel_id=1, source_target_pairs={{16,0},{32,16},{48,32},{64,48},{80,64},{96,80},{112,96},{0,112},{1... | collective-permute-start | bytes 2064392 | tf_op jit(solution)/shard_map/ppermute | solution.py:410
  36.0 3.0 %collective-permute-start.2 = (f32[8,8,8,128]{3,2,1,0:T(8,128)}, f32[8,8,8,128]{3,2,1,0:T(8,128)}, u32[]{:S(2)}, u32[]{:S(2)}) collective-permute-start(f32[8,8,8,128]{3,2,1,0:T(8,128)} %get-tuple-element.22.mid_pot), channel_id=1, source_target_pairs={{0,1},{1,0},{2,3},{3,2},{4,5},{5,4},{6,7},{7,6},{8,9},{9,8},{10,11... | collective-permute-start | bytes 786440 | tf_op jit(solution)/shard_map/ppermute | solution.py:411
  50.7 2.9 %collective-permute-start.3 = (f32[3,8,8,128]{3,2,1,0:T(8,128)S(1)}, f32[3,8,8,128]{3,2,1,0:T(8,128)S(1)}, u32[]{:S(2)}, u32[]{:S(2)}) collective-permute-start(f32[3,8,8,128]{3,2,1,0:T(8,128)S(1)} %get-tuple-element.29.low_pot), channel_id=1, source_target_pairs={{0,1},{1,0},{2,3},{3,2},{4,5},{5,4},{6,7},{7,6},{8,9},{9,8},{10,11... | collective-permute-start | bytes 294920 | tf_op jit(solution)/shard_map/ppermute | solution.py:421
  52.7 1.3 %collective-permute-start.4 = (f32[3,8,8,128]{3,2,1,0:T(8,128)S(1)}, f32[3,8,8,128]{3,2,1,0:T(8,128)S(1)}, u32[]{:S(2)}, u32[]{:S(2)}) collective-permute-start(f32[3,8,8,128]{3,2,1,0:T(8,128)S(1)} %get-tuple-element.30.high_pot), channel_id=1, source_target_pairs={{0,1},{1,0},{2,3},{3,2},{4,5},{5,4},{6,7},{7,6},{8,9},{9,8},{10,11... | collective-permute-start | bytes 294920 | tf_op jit(solution)/shard_map/ppermute | solution.py:422

commit v8 on v7

--- a/solution.py
+++ b/solution.py
@@ -31,7 +31,7 @@
 DEEP = 3 * REACH
 FLAT = 2 * REACH
 FLOWS = 4
-STEP = 4
+STEP = 8
 PAIR = 2
 IN1 = (DEEP, DEEP + 20)
 IN2 = (DEEP, DEEP + 8)
@@ -235,13 +235,21 @@
                     t + t - take(field1, i + r + FLAT, yi)
                 )
 
-    ends1, ends2 = SLAB + 2 * FLAT, SLAB + FLAT
-    for begin, end in ((0, IN1[0]), (IN1[1], ends1)):
+    ends1, ends2, half = SLAB + 2 * FLAT, SLAB + FLAT, SLAB // 2
+
+    def rows(one, begin, end):
         for r in range(begin, end, 2):
-            first(r)
-    sweep(field1, far_z, bands, 0, IN2[0], IN2[0], second)
-    sweep(field1, far_z, bands, IN2[1], ends2, ends2 - IN2[1], second)
-    sweep(field2, far_z, bands, 0, SLAB, SLAB // 2, third)
+            one(r)
+
+    def ahead(field, begin, end):
+        along_z(field, far_z, bands, begin + REACH, begin, end - begin)
+
+    rows(first, 0, IN1[0])
+    rows(first, IN1[1], ends1), ahead(field1, 0, IN2[0])
+    rows(second, 0, IN2[0]), ahead(field1, IN2[1], ends2)
+    rows(second, IN2[1], ends2), ahead(field2, 0, half)
+    rows(third, 0, half), ahead(field2, half, SLAB)
+    rows(third, half, SLAB)
 
 
 def iota(shape, dim):
@@ -299,8 +307,8 @@
         out[5 * d : 5 * d + 5] = rows
 
 
-def finish_kernel(parts, y, out, factor):
-    n = y.shape[0]
+def finish_kernel(parts, y2, out, factor):
+    n = factor.shape[0]
     half = n // 2
     rows = []
     for r in range(5):
@@ -357,13 +365,20 @@
     done = jnp.concatenate(finished, axis=0)
     factor[...] = jnp.where(iota((n, n), 0) <= iota((n, n), 1), done[:, :n], 0.0)
     mixer = done[:, n : 2 * n]
-    ones = spread(n)
-    tall = jnp.broadcast_to(mixer[:, None], (n, BX, n)).reshape(n * BX, n)
-    wide_mixer = jnp.where(same_y(n), dot(tall, ones, ((1,), (1,))), 0.0)
-    for x in range(0, BX, 2):
-        mixed = dot(wide_mixer, pair_of_rows(y, x))
-        out[:, x] = mixed[:, :128].reshape(n, BX, 128)
-        out[:, x + 1] = mixed[:, 128:].reshape(n, BX, 128)
+    m_high, m_middle, m_low = parts_of(mixer)
+    wide = jnp.concatenate([m_high, m_high, m_high, m_middle, m_middle, m_low], axis=1)
+    wide = jnp.concatenate([wide, jnp.zeros((n, 256 - 6 * n), jnp.bfloat16)], axis=1)
+    for xy in range(0, BX * BX, 2):
+        both = []
+        for r in range(2):
+            both.append(jnp.concatenate([y2[pl.ds(xy + r + 512 * k, 8, stride=64), :] for k in range(n // 8)], axis=0))
+        v = jnp.concatenate(both, axis=1)
+        high, middle, low = parts_of(v)
+        stack = jnp.concatenate([high, middle, low, high, middle, high, jnp.zeros((256 - 6 * n, 256), jnp.bfloat16)], axis=0)
+        mixed = jnp.dot(wide, stack, preferred_element_type=jnp.float32)
+        for r in range(2):
+            for k in range(n // 8):
+                out[pl.ds(xy + r + 512 * k, 8, stride=64), :] = mixed[8 * k : 8 * k + 8, 128 * r : 128 * r + 128]
 
 
 def call(kernel, out_shape, in_specs, scratch=(), limit=8, flops=0, moved=0, aliases={}):
@@ -442,7 +457,10 @@
     parts = lax.all_to_all(
         parts.reshape(devices, 1, 5 * 128), ("gy", "z", "s"), 0, 0, tiled=True
     ).reshape(devices * 5, 128)
-    return call(finish_kernel, (f32(n, BX, BX, 128), f32(n, n)), [VMEM, VMEM])(parts, back)
+    made, factor = call(finish_kernel, (f32(n * BX * BX, 128), f32(n, n)), [VMEM, VMEM])(
+        parts, back.reshape(n * BX * BX, 128)
+    )
+    return made.reshape(n, BX, BX, 128), factor
 
 
 def solution(mesh):

time: 103 us -> 102 us (level)
  no operation moved by 1% of the time
where the time goes in v8:
time: 102 us
  blocking collectives  66.7 us (65%)
  Pallas kernels  17.1 us (17%)
  waiting for transfers between devices  10.5 us (10%)
  starting transfers between devices  7.18 us (7%)
    all_to_all x1, blocking collectives, per_device(): got = lax.all_to_all(sent, ('z', 'gy'), 0, 0, tiled=True)  29.2 us
    all_to_all x1, blocking collectives, per_device(): lax.all_to_all(filtered, ('z', 'gy'), 0, 0, tiled=True)  19.9 us
    all_to_all x1, blocking collectives, per_device(): lax.all_to_all(parts.reshape(devices, 1, 5 * 128), ('gy', 'z', 's'), 0, 0...  17.6 us
    ppermute x1, waiting for transfers between devices, per_device(): low = lax.ppermute(up, 's', ring)  8.54 us
    pallas_call x1, Pallas kernels, per_device(): call(outer_kernel, (f32(group * PAIR * BX * BX, 128),) + fields[1:] + (fi...  5.99 us
    pallas_call x1, Pallas kernels, per_device(): call(inner_kernel, fields, [SMEM] + [VMEM] * 3, far_z, 10, flops=1 << 32)  3.1 us
    pallas_call x1, Pallas kernels, per_device(): call(finish_kernel, (f32(n * BX * BX, 128), f32(n, n)), [VMEM, VMEM])  3.09 us
    ppermute x1, starting transfers between devices, per_device(): high = lax.ppermute(down, 's', back_ring)  2.36 us
  transfers between devices with their start and end apart: 5, of which 4 were waited for; matrix products, arithmetic and copies ran while one was open for 0% of the time, Pallas kernels for 4%

profile of v8, /device:TPU:1, one launch (start us, length us, event | category | flops | bytes accessed | tf_op | source)
XLA Modules:
  0.0 102.1 jit_solution(8969371883090228103)
XLA Ops:
  0.6 1.2 %shard_map.41 = f32[16,2,10,8,128]{4,3,2,1,0:T(8,128)S(1)} custom-call(f32[16,2,8,8,128]{4,3,2,1,0:T(8,128)} %bitcast.16, f32[8,8,128]{2,1,0:T(8,128)} %potential.1), custom_call_target="tpu_custom_call" | custom-call | tf_op jit(solution)/shard_map/pallas_call | solution.py:407
  1.9 29.2 %all_to_all.15 = f32[16,2,10,8,128]{4,3,2,1,0:T(8,128)S(1)} all-to-all(f32[16,2,10,8,128]{4,3,2,1,0:T(8,128)S(1)} %shard_map.41), channel_id=1, replica_groups=mesh['s'=8,'z'=4,'gy'=4] {'z','gy'}, dimensions={0} | all-to-all | bytes 2621440 | tf_op jit(solution)/shard_map/all_to_all | solution.py:416
  31.1 1.4 %shard_map.42 = (f32[21,8,8,128]{3,2,1,0:T(8,128)}, f32[21,8,8,128]{3,2,1,0:T(8,128)S(1)}, f32[8,8,8,128]{3,2,1,0:T(8,128)}) custom-call(f32[2560,128]{1,0:T(8,128)S(1)} %bitcast.11), custom_call_target="tpu_custom_call" | custom-call | tf_op jit(solution)/shard_map/pallas_call | solution.py:418
  32.5 1.2 %collective-permute-start = (f32[21,8,8,128]{3,2,1,0:T(8,128)}, f32[21,8,8,128]{3,2,1,0:T(8,128)S(1)}, u32[]{:S(2)}, u32[]{:S(2)}) collective-permute-start(f32[21,8,8,128]{3,2,1,0:T(8,128)} %get-tuple-element.22), channel_id=1, source_target_pairs={{0,16},{16,32},{32,48},{48,64},{64,80},{80,96},{96,112},{112,0},{1... | collective-permute-start | bytes 2064392 | tf_op jit(solution)/shard_map/ppermute | solution.py:424
  33.7 2.4 %collective-permute-start.1 = (f32[21,8,8,128]{3,2,1,0:T(8,128)S(1)}, f32[21,8,8,128]{3,2,1,0:T(8,128)S(1)}, u32[]{:S(2)}, u32[]{:S(2)}) collective-permute-start(f32[21,8,8,128]{3,2,1,0:T(8,128)S(1)} %get-tuple-element.23), channel_id=1, source_target_pairs={{16,0},{32,16},{48,32},{64,48},{80,64},{96,80},{112,96},{0,112},{1... | collective-permute-start | bytes 2064392 | tf_op jit(solution)/shard_map/ppermute | solution.py:425
  36.0 1.5 %collective-permute-start.2 = (f32[8,8,8,128]{3,2,1,0:T(8,128)}, f32[8,8,8,128]{3,2,1,0:T(8,128)}, u32[]{:S(2)}, u32[]{:S(2)}) collective-permute-start(f32[8,8,8,128]{3,2,1,0:T(8,128)} %get-tuple-element.24.mid_pot), channel_id=1, source_target_pairs={{0,1},{1,0},{2,3},{3,2},{4,5},{5,4},{6,7},{7,6},{8,9},{9,8},{10,11... | collective-permute-start | bytes 786440 | tf_op jit(solution)/shard_map/ppermute | solution.py:426
  37.6 1.5 %collective-permute-done.2.far_mid = f32[8,8,8,128]{3,2,1,0:T(8,128)} collective-permute-done((f32[8,8,8,128]{3,2,1,0:T(8,128)}, f32[8,8,8,128]{3,2,1,0:T(8,128)}, u32[]{:S(2)}, u32[]{:S(2)}) %collective-permute-start.2) | collective-permute-done | bytes 262176 | tf_op jit(solution)/shard_map/ppermute | solution.py:426
  39.1 3.1 %shard_map.43 = (f32[68,8,16,128]{3,2,1,0:T(8,128)S(1)}, f32[56,8,16,128]{3,2,1,0:T(8,128)S(1)}, f32[44,8,16,128]{3,2,1,0:T(8,128)S(1)}, f32[56,8,8,128]{3,2,1,0:T(8,128)S(1)}) custom-call(s32[1]{0:T(128)} %bitcast.core, f32[2560,128]{1,0:T(8,128)S(1)} %bitcast.12, f32[8,8,8,128]{3,2,1,0:T(8,128)} %get-tuple-element.24.mid_pot, ...), custom_call_target="tpu_custom_call" | custom-call | flops 4294967296 | tf_op jit(solution)/shard_map/pallas_call | solution.py:431
  42.2 8.5 %collective-permute-done.low = f32[21,8,8,128]{3,2,1,0:T(8,128)S(1)} collective-permute-done((f32[21,8,8,128]{3,2,1,0:T(8,128)}, f32[21,8,8,128]{3,2,1,0:T(8,128)S(1)}, u32[]{:S(2)}, u32[]{:S(2)}) %collective-permute-start) | collective-permute-done | bytes 688160 | tf_op jit(solution)/shard_map/ppermute | solution.py:424
  50.7 0.0 collective-permute-done.1.high
  50.8 2.0 %collective-permute-start.3 = (f32[3,8,8,128]{3,2,1,0:T(8,128)S(1)}, f32[3,8,8,128]{3,2,1,0:T(8,128)S(1)}, u32[]{:S(2)}, u32[]{:S(2)}) collective-permute-start(f32[3,8,8,128]{3,2,1,0:T(8,128)S(1)} %get-tuple-element.31.low_pot), channel_id=1, source_target_pairs={{0,1},{1,0},{2,3},{3,2},{4,5},{5,4},{6,7},{7,6},{8,9},{9,8},{10,11... | collective-permute-start | bytes 294920 | tf_op jit(solution)/shard_map/ppermute | solution.py:436
  52.7 0.1 collective-permute-start.4
  52.8 0.7 shard_map.45
  53.6 0.1 collective-permute-done.3.far_low
  53.7 0.4 collective-permute-done.4.far_high
  54.0 6.0 %shard_map.46 = (f32[2048,128]{1,0:T(8,128)S(1)}, f32[56,8,16,128]{3,2,1,0:T(8,128)S(1)}, f32[44,8,16,128]{3,2,1,0:T(8,128)S(1)}, f32[56,8,8,128]{3,2,1,0:T(8,128)S(1)}, f32[56,8,8,128]{3,2,1,0:T(8,128)S(1)}) custom-call(s32[1]{0:T(128)} %bitcast.core, ...), custom_call_target="tpu_custom_call", output_to_operand_aliasing={{1}: (6, {}), {2}: (7, {}), {3}: (8, {}), {4}: (9, {})} | custom-call | tf_op jit(solution)/shard_map/pallas_call | solution.py:442
  60.0 19.9 %all_to_all.16 = f32[16,2,8,8,128]{4,3,2,1,0:T(8,128)S(1)} all-to-all(f32[16,2,8,8,128]{4,3,2,1,0:T(8,128)S(1)} %bitcast.15), channel_id=1, replica_groups=mesh['s'=8,'z'=4,'gy'=4] {'z','gy'}, dimensions={0} | all-to-all | bytes 2097152 | tf_op jit(solution)/shard_map/all_to_all | solution.py:451
  80.0 1.5 %shard_map.47 = f32[640,128]{1,0:T(8,128)S(1)} custom-call(f32[32,8,8,128]{3,2,1,0:T(8,128)S(1)} %bitcast.9), custom_call_target="tpu_custom_call" | custom-call | tf_op jit(solution)/shard_map/pallas_call | solution.py:454
  81.5 17.6 %all_to_all.17 = f32[128,1,640]{2,1,0:T(1,128)S(1)} all-to-all(f32[128,1,640]{2,1,0:T(1,128)S(1)} %bitcast.14), channel_id=1, replica_groups=mesh['s'=8,'z'=4,'gy'=4] {'gy','z','s'}, dimensions={0} | all-to-all | bytes 655360 | tf_op jit(solution)/shard_map/all_to_all | solution.py:457
  99.0 3.1 %shard_map.48 = (f32[2048,128]{1,0:T(8,128)}, f32[32,32]{1,0:T(8,128)}) custom-call(f32[640,128]{1,0:T(8,128)S(1)} %bitcast.13, f32[2048,128]{1,0:T(8,128)S(1)} %bitcast.10), custom_call_target="tpu_custom_call" | custom-call | tf_op jit(solution)/shard_map/pallas_call | solution.py:460
  (1 shorter events, 0.0 us)
Async XLA Ops:
  32.5 18.3 %collective-permute-start = (f32[21,8,8,128]{3,2,1,0:T(8,128)}, f32[21,8,8,128]{3,2,1,0:T(8,128)S(1)}, u32[]{:S(2)}, u32[]{:S(2)}) collective-permute-start(f32[21,8,8,128]{3,2,1,0:T(8,128)} %get-tuple-element.22), channel_id=1, source_target_pairs={{0,16},{16,32},{32,48},{48,64},{64,80},{80,96},{96,112},{112,0},{1... | collective-permute-start | bytes 2064392 | tf_op jit(solution)/shard_map/ppermute | solution.py:424
  33.7 17.1 %collective-permute-start.1 = (f32[21,8,8,128]{3,2,1,0:T(8,128)S(1)}, f32[21,8,8,128]{3,2,1,0:T(8,128)S(1)}, u32[]{:S(2)}, u32[]{:S(2)}) collective-permute-start(f32[21,8,8,128]{3,2,1,0:T(8,128)S(1)} %get-tuple-element.23), channel_id=1, source_target_pairs={{16,0},{32,16},{48,32},{64,48},{80,64},{96,80},{112,96},{0,112},{1... | collective-permute-start | bytes 2064392 | tf_op jit(solution)/shard_map/ppermute | solution.py:425
  36.0 3.0 %collective-permute-start.2 = (f32[8,8,8,128]{3,2,1,0:T(8,128)}, f32[8,8,8,128]{3,2,1,0:T(8,128)}, u32[]{:S(2)}, u32[]{:S(2)}) collective-permute-start(f32[8,8,8,128]{3,2,1,0:T(8,128)} %get-tuple-element.24.mid_pot), channel_id=1, source_target_pairs={{0,1},{1,0},{2,3},{3,2},{4,5},{5,4},{6,7},{7,6},{8,9},{9,8},{10,11... | collective-permute-start | bytes 786440 | tf_op jit(solution)/shard_map/ppermute | solution.py:426
  50.8 2.9 %collective-permute-start.3 = (f32[3,8,8,128]{3,2,1,0:T(8,128)S(1)}, f32[3,8,8,128]{3,2,1,0:T(8,128)S(1)}, u32[]{:S(2)}, u32[]{:S(2)}) collective-permute-start(f32[3,8,8,128]{3,2,1,0:T(8,128)S(1)} %get-tuple-element.31.low_pot), channel_id=1, source_target_pairs={{0,1},{1,0},{2,3},{3,2},{4,5},{5,4},{6,7},{7,6},{8,9},{9,8},{10,11... | collective-permute-start | bytes 294920 | tf_op jit(solution)/shard_map/ppermute | solution.py:436
  52.7 1.3 %collective-permute-start.4 = (f32[3,8,8,128]{3,2,1,0:T(8,128)S(1)}, f32[3,8,8,128]{3,2,1,0:T(8,128)S(1)}, u32[]{:S(2)}, u32[]{:S(2)}) collective-permute-start(f32[3,8,8,128]{3,2,1,0:T(8,128)S(1)} %get-tuple-element.32.high_pot), channel_id=1, source_target_pairs={{0,1},{1,0},{2,3},{3,2},{4,5},{5,4},{6,7},{7,6},{8,9},{9,8},{10,11... | collective-permute-start | bytes 294920 | tf_op jit(solution)/shard_map/ppermute | solution.py:437

commit v9 on v8

--- a/solution.py
+++ b/solution.py
@@ -34,6 +34,8 @@
 STEP = 8
 PAIR = 2
 IN1 = (DEEP, DEEP + 20)
+OWN = range(DEEP, DEEP + 32)
+BEGUN = (DEEP - REACH, DEEP + 20)
 IN2 = (DEEP, DEEP + 8)
 BX = 8
 BLOCK = BX + 2
@@ -137,7 +139,7 @@
     far_z[pl.ds(i, count)] = band_product(v, bands).reshape(count, BX, 8, 128)
 
 
-def apply(field, pot, far_z, row, pot_row, i):
+def apply(field, pot, far_z, row, pot_row, i, known=None):
     totals = [[], []]
     for begin in range(0, BX, 4):
         lines = [
@@ -148,12 +150,16 @@
             e = REACH + yi - begin
             x = {0: lines[0][e], 1: lines[1][e]}
             for d in (*range(-REACH, 0), *range(2, REACH + 2)):
-                x[d] = take(field, row + d, yi)
+                if known is None or row + d in known:
+                    x[d] = take(field, row + d, yi)
             for r in range(2):
                 line = lines[r]
                 total = pot[pot_row + r, yi] * line[e] + far_z[i + r, yi]
                 for j in range(1, REACH + 1):
-                    near = (x[r + j] + x[r - j]) + (line[e + j] + line[e - j])
+                    near = line[e + j] + line[e - j]
+                    beside = [x[d] for d in (r + j, r - j) if d in x]
+                    if beside:
+                        near = sum(beside[1:], beside[0]) + near
                     total = total + coupling[j] * near
                 totals[r].append(total)
     return totals
@@ -185,7 +191,7 @@
     return first, second
 
 
-def inner_kernel(core, got, mid_pot, far_mid, field0, field1, field2, pot, far_z):
+def inner_kernel(core, got, mid_pot, far_mid, field0, field1, field2, pot, begun, far_z):
     bands = band_parts()
     for z in range(4):
         def fill(xi, carry, z=z):
@@ -197,6 +203,14 @@
     first, second = steps(field0, field1, field2, pot, far_z)
     sweep(field0, far_z, bands, *IN1, IN1[1] - IN1[0], first)
     sweep(field1, far_z, bands, *IN2, IN2[1] - IN2[0], second)
+    for at, start in enumerate(BEGUN):
+        along_z(field0, far_z, bands, start + REACH, start, REACH)
+        for r in range(0, REACH, 2):
+            i = start + r
+            totals = apply(field0, pot, far_z, i + REACH, i, i, OWN)
+            for k in range(2):
+                for yi in range(BX):
+                    begun[at * REACH + r + k, yi] = totals[k][yi]
 
 
 def pots_kernel(low, high, low_pot, high_pot):
@@ -213,12 +227,12 @@
         return carry
 
     lax.fori_loop(0, DEEP, edge, 0)
-    along_z(field0, far_z, bands, REACH, 0, IN1[0])
-    along_z(field0, far_z, bands, REACH + IN1[1], IN1[1], SLAB + 2 * FLAT - IN1[1])
+    along_z(field0, far_z, bands, REACH, 0, FLAT)
+    along_z(field0, far_z, bands, REACH + FLAT + SLAB, FLAT + SLAB, FLAT)
 
 
 def outer_kernel(
-    core, low_pot, high_pot, far_low, far_high, field0, _1, _2, _3, _4,
+    core, low_pot, high_pot, far_low, far_high, field0, begun, _1, _2, _3, _4,
     out, field1, field2, pot, far_z,
 ):
     bands = band_parts()
@@ -244,8 +258,21 @@
     def ahead(field, begin, end):
         along_z(field, far_z, bands, begin + REACH, begin, end - begin)
 
-    rows(first, 0, IN1[0])
-    rows(first, IN1[1], ends1), ahead(field1, 0, IN2[0])
+    def complete(at):
+        for r in range(REACH):
+            i = BEGUN[at] + r
+            tiles = []
+            for yi in range(BX):
+                total = begun[at * REACH + r, yi]
+                for j in range(1, REACH + 1):
+                    for row in (i + REACH - j, i + REACH + j):
+                        if row not in OWN:
+                            total = total + coupling[j] * take(field0, row, yi)
+                tiles.append(total)
+            put(field1, i, tiles)
+
+    rows(first, 0, FLAT), complete(0)
+    complete(1), rows(first, FLAT + SLAB, ends1), ahead(field1, 0, IN2[0])
     rows(second, 0, IN2[0]), ahead(field1, IN2[1], ends2)
     rows(second, IN2[1], ends2), ahead(field2, 0, half)
     rows(third, 0, half), ahead(field2, half, SLAB)
@@ -428,25 +455,25 @@
     fields = tuple(f32(rows, BX, 16, 128) for rows in (SLAB + 2 * DEEP, SLAB + 2 * FLAT, SLAB + FLAT))
     fields += (f32(SLAB + 2 * FLAT, BX, 8, 128),)
     far_z = [pltpu.VMEM((SLAB + 2 * FLAT, BX, 8, 128), jnp.float32)]
-    inner = call(inner_kernel, fields, [SMEM] + [VMEM] * 3, far_z, 10, flops=1 << 32)(
+    inner = call(inner_kernel, fields + (f32(2 * REACH, BX, 8, 128),), [SMEM] + [VMEM] * 3, far_z, 10, flops=1 << 32)(
         *own, got, mid_pot, far_mid
     )
     low, high, inner = lax.optimization_barrier((low, high, inner))
     low_pot, high_pot = call(pots_kernel, (f32(3, 8, 8, 128),) * 2, [VMEM] * 2)(low, high)
     far_low = lax.ppermute(low_pot, "gy", twin)
     far_high = lax.ppermute(high_pot, "gy", twin)
-    field0, field1, field2, pot = inner
+    field0, field1, field2, pot, begun = inner
     field0, products = call(
         edge_kernel, (fields[0], fields[3]), [VMEM] * 3, (), 10, flops=1 << 30, aliases={2: 0}
     )(low, high, field0)
     filtered = call(
         outer_kernel,
         (f32(group * PAIR * BX * BX, 128),) + fields[1:] + (fields[3],),
-        [SMEM] + [VMEM] * 9,
+        [SMEM] + [VMEM] * 10,
         (),
         10,
-        aliases={6 + k: 1 + k for k in range(4)},
-    )(*own, low_pot, high_pot, far_low, far_high, field0, field1, field2, pot, products)[0]
+        aliases={7 + k: 1 + k for k in range(4)},
+    )(*own, low_pot, high_pot, far_low, far_high, field0, begun, field1, field2, pot, products)[0]
     filtered = filtered.reshape(group, PAIR, BX, BX, 128)
     back = lax.all_to_all(filtered, ("z", "gy"), 0, 0, tiled=True).reshape(n, BX, BX, 128)
     devices = slabs * group

time: 102 us -> 102 us (level)
  no operation moved by 1% of the time
where the time goes in v9:
time: 102 us
  blocking collectives  66.7 us (65%)
  Pallas kernels  17.1 us (17%)
  waiting for transfers between devices  10.1 us (10%)
  starting transfers between devices  7.18 us (7%)
    all_to_all x1, blocking collectives, per_device(): got = lax.all_to_all(sent, ('z', 'gy'), 0, 0, tiled=True)  29.2 us
    all_to_all x1, blocking collectives, per_device(): lax.all_to_all(filtered, ('z', 'gy'), 0, 0, tiled=True)  19.9 us
    all_to_all x1, blocking collectives, per_device(): lax.all_to_all(parts.reshape(devices, 1, 5 * 128), ('gy', 'z', 's'), 0, 0...  17.6 us
    ppermute x1, waiting for transfers between devices, per_device(): low = lax.ppermute(up, 's', ring)  8.08 us
    pallas_call x1, Pallas kernels, per_device(): call(outer_kernel, (f32(group * PAIR * BX * BX, 128),) + fields[1:] + (fi...  5.67 us
    pallas_call x1, Pallas kernels, per_device(): call(inner_kernel, fields + (f32(2 * REACH, BX, 8, 128),), [SMEM] + [VMEM...  3.57 us
    pallas_call x1, Pallas kernels, per_device(): call(finish_kernel, (f32(n * BX * BX, 128), f32(n, n)), [VMEM, VMEM])  3.09 us
    ppermute x1, starting transfers between devices, per_device(): high = lax.ppermute(down, 's', back_ring)  2.36 us
  transfers between devices with their start and end apart: 5, of which 4 were waited for; matrix products, arithmetic and copies ran while one was open for 0% of the time, Pallas kernels for 4%

profile of v9, /device:TPU:1, one launch (start us, length us, event | category | flops | bytes accessed | tf_op | source)
XLA Modules:
  0.0 101.8 jit_solution(7190080467089046763)
XLA Ops:
  0.6 1.2 %shard_map.41 = f32[16,2,10,8,128]{4,3,2,1,0:T(8,128)S(1)} custom-call(f32[16,2,8,8,128]{4,3,2,1,0:T(8,128)} %bitcast.16, f32[8,8,128]{2,1,0:T(8,128)} %potential.1), custom_call_target="tpu_custom_call" | custom-call | tf_op jit(solution)/shard_map/pallas_call | solution.py:434
  1.9 29.2 %all_to_all.15 = f32[16,2,10,8,128]{4,3,2,1,0:T(8,128)S(1)} all-to-all(f32[16,2,10,8,128]{4,3,2,1,0:T(8,128)S(1)} %shard_map.41), channel_id=1, replica_groups=mesh['s'=8,'z'=4,'gy'=4] {'z','gy'}, dimensions={0} | all-to-all | bytes 2621440 | tf_op jit(solution)/shard_map/all_to_all | solution.py:443
  31.1 1.4 %shard_map.42 = (f32[21,8,8,128]{3,2,1,0:T(8,128)}, f32[21,8,8,128]{3,2,1,0:T(8,128)S(1)}, f32[8,8,8,128]{3,2,1,0:T(8,128)}) custom-call(f32[2560,128]{1,0:T(8,128)S(1)} %bitcast.11), custom_call_target="tpu_custom_call" | custom-call | tf_op jit(solution)/shard_map/pallas_call | solution.py:445
  32.5 1.2 %collective-permute-start = (f32[21,8,8,128]{3,2,1,0:T(8,128)}, f32[21,8,8,128]{3,2,1,0:T(8,128)S(1)}, u32[]{:S(2)}, u32[]{:S(2)}) collective-permute-start(f32[21,8,8,128]{3,2,1,0:T(8,128)} %get-tuple-element.24), channel_id=1, source_target_pairs={{0,16},{16,32},{32,48},{48,64},{64,80},{80,96},{96,112},{112,0},{1... | collective-permute-start | bytes 2064392 | tf_op jit(solution)/shard_map/ppermute | solution.py:451
  33.7 2.4 %collective-permute-start.1 = (f32[21,8,8,128]{3,2,1,0:T(8,128)S(1)}, f32[21,8,8,128]{3,2,1,0:T(8,128)S(1)}, u32[]{:S(2)}, u32[]{:S(2)}) collective-permute-start(f32[21,8,8,128]{3,2,1,0:T(8,128)S(1)} %get-tuple-element.25), channel_id=1, source_target_pairs={{16,0},{32,16},{48,32},{64,48},{80,64},{96,80},{112,96},{0,112},{1... | collective-permute-start | bytes 2064392 | tf_op jit(solution)/shard_map/ppermute | solution.py:452
  36.0 1.5 %collective-permute-start.2 = (f32[8,8,8,128]{3,2,1,0:T(8,128)}, f32[8,8,8,128]{3,2,1,0:T(8,128)}, u32[]{:S(2)}, u32[]{:S(2)}) collective-permute-start(f32[8,8,8,128]{3,2,1,0:T(8,128)} %get-tuple-element.26.mid_pot), channel_id=1, source_target_pairs={{0,1},{1,0},{2,3},{3,2},{4,5},{5,4},{6,7},{7,6},{8,9},{9,8},{10,11... | collective-permute-start | bytes 786440 | tf_op jit(solution)/shard_map/ppermute | solution.py:453
  37.6 1.5 %collective-permute-done.2.far_mid = f32[8,8,8,128]{3,2,1,0:T(8,128)} collective-permute-done((f32[8,8,8,128]{3,2,1,0:T(8,128)}, f32[8,8,8,128]{3,2,1,0:T(8,128)}, u32[]{:S(2)}, u32[]{:S(2)}) %collective-permute-start.2) | collective-permute-done | bytes 262176 | tf_op jit(solution)/shard_map/ppermute | solution.py:453
  39.1 3.6 %shard_map.43 = (f32[68,8,16,128]{3,2,1,0:T(8,128)S(1)}, f32[56,8,16,128]{3,2,1,0:T(8,128)S(1)}, f32[44,8,16,128]{3,2,1,0:T(8,128)S(1)}, f32[56,8,8,128]{3,2,1,0:T(8,128)S(1)}, f32[12,8,8,128]{3,2,1,0:T(8,128)S(1)}) custom-call(s32[1]{0:T(128)} %bitcast.core, f32[2560,128]{1,0:T(8,128)S(1)} %bitcast.12, f32[8,8,8,128]{3,2,1,0:T(8,128)} %get-tuple-element.26.mid_pot, ...), custom_call_target="tpu_custom_call" | custom-call | flops 4294967296 | tf_op jit(solution)/shard_map/pallas_call | solution.py:458
  42.6 8.1 %collective-permute-done.low = f32[21,8,8,128]{3,2,1,0:T(8,128)S(1)} collective-permute-done((f32[21,8,8,128]{3,2,1,0:T(8,128)}, f32[21,8,8,128]{3,2,1,0:T(8,128)S(1)}, u32[]{:S(2)}, u32[]{:S(2)}) %collective-permute-start) | collective-permute-done | bytes 688160 | tf_op jit(solution)/shard_map/ppermute | solution.py:451
  50.7 0.0 collective-permute-done.1.high
  50.8 2.0 %collective-permute-start.3 = (f32[3,8,8,128]{3,2,1,0:T(8,128)S(1)}, f32[3,8,8,128]{3,2,1,0:T(8,128)S(1)}, u32[]{:S(2)}, u32[]{:S(2)}) collective-permute-start(f32[3,8,8,128]{3,2,1,0:T(8,128)S(1)} %get-tuple-element.34.low_pot), channel_id=1, source_target_pairs={{0,1},{1,0},{2,3},{3,2},{4,5},{5,4},{6,7},{7,6},{8,9},{9,8},{10,11... | collective-permute-start | bytes 294920 | tf_op jit(solution)/shard_map/ppermute | solution.py:463
  52.7 0.1 collective-permute-start.4
  52.8 0.6 shard_map.45
  53.5 0.2 collective-permute-done.3.far_low
  53.7 0.4 collective-permute-done.4.far_high
  54.0 5.7 %shard_map.46 = (f32[2048,128]{1,0:T(8,128)S(1)}, f32[56,8,16,128]{3,2,1,0:T(8,128)S(1)}, f32[44,8,16,128]{3,2,1,0:T(8,128)S(1)}, f32[56,8,8,128]{3,2,1,0:T(8,128)S(1)}, f32[56,8,8,128]{3,2,1,0:T(8,128)S(1)}) custom-call(s32[1]{0:T(128)} %bitcast.core, ...), custom_call_target="tpu_custom_call", output_to_operand_aliasing={{1}: (7, {}), {2}: (8, {}), {3}: (9, {}), {4}: (10, {})} | custom-call | tf_op jit(solution)/shard_map/pallas_call | solution.py:469
  59.7 19.9 %all_to_all.16 = f32[16,2,8,8,128]{4,3,2,1,0:T(8,128)S(1)} all-to-all(f32[16,2,8,8,128]{4,3,2,1,0:T(8,128)S(1)} %bitcast.15), channel_id=1, replica_groups=mesh['s'=8,'z'=4,'gy'=4] {'z','gy'}, dimensions={0} | all-to-all | bytes 2097152 | tf_op jit(solution)/shard_map/all_to_all | solution.py:478
  79.6 1.5 %shard_map.47 = f32[640,128]{1,0:T(8,128)S(1)} custom-call(f32[32,8,8,128]{3,2,1,0:T(8,128)S(1)} %bitcast.9), custom_call_target="tpu_custom_call" | custom-call | tf_op jit(solution)/shard_map/pallas_call | solution.py:481
  81.1 17.6 %all_to_all.17 = f32[128,1,640]{2,1,0:T(1,128)S(1)} all-to-all(f32[128,1,640]{2,1,0:T(1,128)S(1)} %bitcast.14), channel_id=1, replica_groups=mesh['s'=8,'z'=4,'gy'=4] {'gy','z','s'}, dimensions={0} | all-to-all | bytes 655360 | tf_op jit(solution)/shard_map/all_to_all | solution.py:484
  98.7 3.1 %shard_map.48 = (f32[2048,128]{1,0:T(8,128)}, f32[32,32]{1,0:T(8,128)}) custom-call(f32[640,128]{1,0:T(8,128)S(1)} %bitcast.13, f32[2048,128]{1,0:T(8,128)S(1)} %bitcast.10), custom_call_target="tpu_custom_call" | custom-call | tf_op jit(solution)/shard_map/pallas_call | solution.py:487
  (1 shorter events, 0.0 us)
Async XLA Ops:
  32.5 18.3 %collective-permute-start = (f32[21,8,8,128]{3,2,1,0:T(8,128)}, f32[21,8,8,128]{3,2,1,0:T(8,128)S(1)}, u32[]{:S(2)}, u32[]{:S(2)}) collective-permute-start(f32[21,8,8,128]{3,2,1,0:T(8,128)} %get-tuple-element.24), channel_id=1, source_target_pairs={{0,16},{16,32},{32,48},{48,64},{64,80},{80,96},{96,112},{112,0},{1... | collective-permute-start | bytes 2064392 | tf_op jit(solution)/shard_map/ppermute | solution.py:451
  33.7 17.1 %collective-permute-start.1 = (f32[21,8,8,128]{3,2,1,0:T(8,128)S(1)}, f32[21,8,8,128]{3,2,1,0:T(8,128)S(1)}, u32[]{:S(2)}, u32[]{:S(2)}) collective-permute-start(f32[21,8,8,128]{3,2,1,0:T(8,128)S(1)} %get-tuple-element.25), channel_id=1, source_target_pairs={{16,0},{32,16},{48,32},{64,48},{80,64},{96,80},{112,96},{0,112},{1... | collective-permute-start | bytes 2064392 | tf_op jit(solution)/shard_map/ppermute | solution.py:452
  36.0 3.0 %collective-permute-start.2 = (f32[8,8,8,128]{3,2,1,0:T(8,128)}, f32[8,8,8,128]{3,2,1,0:T(8,128)}, u32[]{:S(2)}, u32[]{:S(2)}) collective-permute-start(f32[8,8,8,128]{3,2,1,0:T(8,128)} %get-tuple-element.26.mid_pot), channel_id=1, source_target_pairs={{0,1},{1,0},{2,3},{3,2},{4,5},{5,4},{6,7},{7,6},{8,9},{9,8},{10,11... | collective-permute-start | bytes 786440 | tf_op jit(solution)/shard_map/ppermute | solution.py:453
  50.8 2.9 %collective-permute-start.3 = (f32[3,8,8,128]{3,2,1,0:T(8,128)S(1)}, f32[3,8,8,128]{3,2,1,0:T(8,128)S(1)}, u32[]{:S(2)}, u32[]{:S(2)}) collective-permute-start(f32[3,8,8,128]{3,2,1,0:T(8,128)S(1)} %get-tuple-element.34.low_pot), channel_id=1, source_target_pairs={{0,1},{1,0},{2,3},{3,2},{4,5},{5,4},{6,7},{7,6},{8,9},{9,8},{10,11... | collective-permute-start | bytes 294920 | tf_op jit(solution)/shard_map/ppermute | solution.py:463
  52.7 1.3 %collective-permute-start.4 = (f32[3,8,8,128]{3,2,1,0:T(8,128)S(1)}, f32[3,8,8,128]{3,2,1,0:T(8,128)S(1)}, u32[]{:S(2)}, u32[]{:S(2)}) collective-permute-start(f32[3,8,8,128]{3,2,1,0:T(8,128)S(1)} %get-tuple-element.35.high_pot), channel_id=1, source_target_pairs={{0,1},{1,0},{2,3},{3,2},{4,5},{5,4},{6,7},{7,6},{8,9},{9,8},{10,11... | collective-permute-start | bytes 294920 | tf_op jit(solution)/shard_map/ppermute | solution.py:464

commit v10 on v9

--- a/solution.py
+++ b/solution.py
@@ -168,10 +168,14 @@
 WHOLE = tuple((8 * z + 2 * k, 8 * z + 2 * k + 4) for z in range(4) for k in range(2))
 
 
-def put_pots(pot, mine, sources, slots, row):
+LOW_SLOTS = ((0, 2), (4, 8), (6, 10))
+HIGH_SLOTS = ((0, 4), (2, 6), (8, 10))
+
+
+def put_pots(pot, sources, slots, row):
     odd = iota((8, 128), 0) % 2 == 1
     for slot, (even_row, odd_row) in enumerate(slots):
-        for source, parity in zip(sources, (mine, 1 - mine)):
+        for source, parity in sources:
             for yi in range(BX):
                 tile = diagonal + source[slot, yi] * (1.0 / half_width)
                 pot[row + even_row + parity, yi] = jnp.where(odd, pltpu.roll(tile, 1, 0), tile)
@@ -199,7 +203,7 @@
             return carry
 
         lax.fori_loop(0, BX, fill, 0)
-    put_pots(pot, core[0], (mid_pot, far_mid), WHOLE, FLAT)
+    put_pots(pot, ((mid_pot, core[0]), (far_mid, 1 - core[0])), WHOLE, FLAT)
     first, second = steps(field0, field1, field2, pot, far_z)
     sweep(field0, far_z, bands, *IN1, IN1[1] - IN1[0], first)
     sweep(field1, far_z, bands, *IN2, IN2[1] - IN2[0], second)
@@ -218,7 +222,7 @@
     high_pot[...] = high[DEEP:]
 
 
-def edge_kernel(low, high, _, field0, far_z):
+def edge_kernel(core, low, high, _0, _1, field0, pot, far_z):
     bands = band_parts()
 
     def edge(i, carry):
@@ -227,18 +231,19 @@
         return carry
 
     lax.fori_loop(0, DEEP, edge, 0)
+    put_pots(pot, ((low.at[DEEP:], core[0]),), LOW_SLOTS, 0)
+    put_pots(pot, ((high.at[DEEP:], core[0]),), HIGH_SLOTS, FLAT + SLAB)
     along_z(field0, far_z, bands, REACH, 0, FLAT)
     along_z(field0, far_z, bands, REACH + FLAT + SLAB, FLAT + SLAB, FLAT)
 
 
 def outer_kernel(
-    core, low_pot, high_pot, far_low, far_high, field0, begun, _1, _2, _3, _4,
+    core, far_low, far_high, field0, begun, _1, _2, _3, _4,
     out, field1, field2, pot, far_z,
 ):
     bands = band_parts()
-    mine = core[0]
-    put_pots(pot, mine, (low_pot, far_low), ((0, 2), (4, 8), (6, 10)), 0)
-    put_pots(pot, mine, (high_pot, far_high), ((0, 4), (2, 6), (8, 10)), FLAT + SLAB)
+    put_pots(pot, ((far_low, 1 - core[0]),), LOW_SLOTS, 0)
+    put_pots(pot, ((far_high, 1 - core[0]),), HIGH_SLOTS, FLAT + SLAB)
     first, second = steps(field0, field1, field2, pot, far_z)
 
     def third(i):
@@ -463,17 +468,23 @@
     far_low = lax.ppermute(low_pot, "gy", twin)
     far_high = lax.ppermute(high_pot, "gy", twin)
     field0, field1, field2, pot, begun = inner
-    field0, products = call(
-        edge_kernel, (fields[0], fields[3]), [VMEM] * 3, (), 10, flops=1 << 30, aliases={2: 0}
-    )(low, high, field0)
+    field0, pot, products = call(
+        edge_kernel,
+        (fields[0], fields[3], fields[3]),
+        [SMEM] + [VMEM] * 4,
+        (),
+        10,
+        flops=1 << 30,
+        aliases={3: 0, 4: 1},
+    )(*own, low, high, field0, pot)
     filtered = call(
         outer_kernel,
         (f32(group * PAIR * BX * BX, 128),) + fields[1:] + (fields[3],),
-        [SMEM] + [VMEM] * 10,
+        [SMEM] + [VMEM] * 8,
         (),
         10,
-        aliases={7 + k: 1 + k for k in range(4)},
-    )(*own, low_pot, high_pot, far_low, far_high, field0, begun, field1, field2, pot, products)[0]
+        aliases={5 + k: 1 + k for k in range(4)},
+    )(*own, far_low, far_high, field0, begun, field1, field2, pot, products)[0]
     filtered = filtered.reshape(group, PAIR, BX, BX, 128)
     back = lax.all_to_all(filtered, ("z", "gy"), 0, 0, tiled=True).reshape(n, BX, BX, 128)
     devices = slabs * group

time: 102 us -> 102 us (level)
  no operation moved by 1% of the time
where the time goes in v10:
time: 102 us; the launch traced here: 101 us
  blocking collectives  66.7 us (65%)
  Pallas kernels  16.7 us (16%)
  waiting for transfers between devices  10.2 us (10%)
  starting transfers between devices  7.18 us (7%)
    all_to_all x1, blocking collectives, per_device(): got = lax.all_to_all(sent, ('z', 'gy'), 0, 0, tiled=True)  29.2 us
    all_to_all x1, blocking collectives, per_device(): lax.all_to_all(filtered, ('z', 'gy'), 0, 0, tiled=True)  19.9 us
    all_to_all x1, blocking collectives, per_device(): lax.all_to_all(parts.reshape(devices, 1, 5 * 128), ('gy', 'z', 's'), 0, 0...  17.6 us
    ppermute x1, waiting for transfers between devices, per_device(): low = lax.ppermute(up, 's', ring)  8.12 us
    pallas_call x1, Pallas kernels, per_device(): call(outer_kernel, (f32(group * PAIR * BX * BX, 128),) + fields[1:] + (fi...  5.31 us
    pallas_call x1, Pallas kernels, per_device(): call(inner_kernel, fields + (f32(2 * REACH, BX, 8, 128),), [SMEM] + [VMEM...  3.53 us
    pallas_call x1, Pallas kernels, per_device(): call(finish_kernel, (f32(n * BX * BX, 128), f32(n, n)), [VMEM, VMEM])  3.09 us
    ppermute x1, starting transfers between devices, per_device(): high = lax.ppermute(down, 's', back_ring)  2.36 us
  transfers between devices with their start and end apart: 5, of which 4 were waited for; matrix products, arithmetic and copies ran while one was open for 0% of the time, Pallas kernels for 4%

profile of v10, /device:TPU:1, one launch (start us, length us, event | category | flops | bytes accessed | tf_op | source)
XLA Modules:
  0.0 101.4 jit_solution(13512248224094077670)
XLA Ops:
  0.6 1.2 %shard_map.41 = f32[16,2,10,8,128]{4,3,2,1,0:T(8,128)S(1)} custom-call(f32[16,2,8,8,128]{4,3,2,1,0:T(8,128)} %bitcast.16, f32[8,8,128]{2,1,0:T(8,128)} %potential.1), custom_call_target="tpu_custom_call" | custom-call | tf_op jit(solution)/shard_map/pallas_call | solution.py:439
  1.9 29.2 %all_to_all.15 = f32[16,2,10,8,128]{4,3,2,1,0:T(8,128)S(1)} all-to-all(f32[16,2,10,8,128]{4,3,2,1,0:T(8,128)S(1)} %shard_map.41), channel_id=1, replica_groups=mesh['s'=8,'z'=4,'gy'=4] {'z','gy'}, dimensions={0} | all-to-all | bytes 2621440 | tf_op jit(solution)/shard_map/all_to_all | solution.py:448
  31.1 1.4 %shard_map.42 = (f32[21,8,8,128]{3,2,1,0:T(8,128)}, f32[21,8,8,128]{3,2,1,0:T(8,128)S(1)}, f32[8,8,8,128]{3,2,1,0:T(8,128)}) custom-call(f32[2560,128]{1,0:T(8,128)S(1)} %bitcast.11), custom_call_target="tpu_custom_call" | custom-call | tf_op jit(solution)/shard_map/pallas_call | solution.py:450
  32.5 1.2 %collective-permute-start = (f32[21,8,8,128]{3,2,1,0:T(8,128)}, f32[21,8,8,128]{3,2,1,0:T(8,128)S(1)}, u32[]{:S(2)}, u32[]{:S(2)}) collective-permute-start(f32[21,8,8,128]{3,2,1,0:T(8,128)} %get-tuple-element.25), channel_id=1, source_target_pairs={{0,16},{16,32},{32,48},{48,64},{64,80},{80,96},{96,112},{112,0},{1... | collective-permute-start | bytes 2064392 | tf_op jit(solution)/shard_map/ppermute | solution.py:456
  33.7 2.4 %collective-permute-start.1 = (f32[21,8,8,128]{3,2,1,0:T(8,128)S(1)}, f32[21,8,8,128]{3,2,1,0:T(8,128)S(1)}, u32[]{:S(2)}, u32[]{:S(2)}) collective-permute-start(f32[21,8,8,128]{3,2,1,0:T(8,128)S(1)} %get-tuple-element.26), channel_id=1, source_target_pairs={{16,0},{32,16},{48,32},{64,48},{80,64},{96,80},{112,96},{0,112},{1... | collective-permute-start | bytes 2064392 | tf_op jit(solution)/shard_map/ppermute | solution.py:457
  36.0 1.5 %collective-permute-start.2 = (f32[8,8,8,128]{3,2,1,0:T(8,128)}, f32[8,8,8,128]{3,2,1,0:T(8,128)}, u32[]{:S(2)}, u32[]{:S(2)}) collective-permute-start(f32[8,8,8,128]{3,2,1,0:T(8,128)} %get-tuple-element.27.mid_pot), channel_id=1, source_target_pairs={{0,1},{1,0},{2,3},{3,2},{4,5},{5,4},{6,7},{7,6},{8,9},{9,8},{10,11... | collective-permute-start | bytes 786440 | tf_op jit(solution)/shard_map/ppermute | solution.py:458
  37.6 1.5 %collective-permute-done.2.far_mid = f32[8,8,8,128]{3,2,1,0:T(8,128)} collective-permute-done((f32[8,8,8,128]{3,2,1,0:T(8,128)}, f32[8,8,8,128]{3,2,1,0:T(8,128)}, u32[]{:S(2)}, u32[]{:S(2)}) %collective-permute-start.2) | collective-permute-done | bytes 262176 | tf_op jit(solution)/shard_map/ppermute | solution.py:458
  39.1 3.5 %shard_map.43 = (f32[68,8,16,128]{3,2,1,0:T(8,128)S(1)}, f32[56,8,16,128]{3,2,1,0:T(8,128)S(1)}, f32[44,8,16,128]{3,2,1,0:T(8,128)S(1)}, f32[56,8,8,128]{3,2,1,0:T(8,128)S(1)}, f32[12,8,8,128]{3,2,1,0:T(8,128)S(1)}) custom-call(s32[1]{0:T(128)} %bitcast.core, f32[2560,128]{1,0:T(8,128)S(1)} %bitcast.12, f32[8,8,8,128]{3,2,1,0:T(8,128)} %get-tuple-element.27.mid_pot, ...), custom_call_target="tpu_custom_call" | custom-call | flops 4294967296 | tf_op jit(solution)/shard_map/pallas_call | solution.py:463
  42.6 8.1 %collective-permute-done.low = f32[21,8,8,128]{3,2,1,0:T(8,128)S(1)} collective-permute-done((f32[21,8,8,128]{3,2,1,0:T(8,128)}, f32[21,8,8,128]{3,2,1,0:T(8,128)S(1)}, u32[]{:S(2)}, u32[]{:S(2)}) %collective-permute-start) | collective-permute-done | bytes 688160 | tf_op jit(solution)/shard_map/ppermute | solution.py:456
  50.7 0.0 collective-permute-done.1.high
  50.8 2.0 %collective-permute-start.3 = (f32[3,8,8,128]{3,2,1,0:T(8,128)S(1)}, f32[3,8,8,128]{3,2,1,0:T(8,128)S(1)}, u32[]{:S(2)}, u32[]{:S(2)}) collective-permute-start(f32[3,8,8,128]{3,2,1,0:T(8,128)S(1)} %get-tuple-element.35), channel_id=1, source_target_pairs={{0,1},{1,0},{2,3},{3,2},{4,5},{5,4},{6,7},{7,6},{8,9},{9,8},{10,11... | collective-permute-start | bytes 294920 | tf_op jit(solution)/shard_map/ppermute | solution.py:468
  52.7 0.1 collective-permute-start.4
  52.8 0.7 shard_map.45
  53.5 0.2 collective-permute-done.3.far_low
  53.7 0.4 collective-permute-done.4.far_high
  54.0 5.3 %shard_map.46 = (f32[2048,128]{1,0:T(8,128)S(1)}, f32[56,8,16,128]{3,2,1,0:T(8,128)S(1)}, f32[44,8,16,128]{3,2,1,0:T(8,128)S(1)}, f32[56,8,8,128]{3,2,1,0:T(8,128)S(1)}, f32[56,8,8,128]{3,2,1,0:T(8,128)S(1)}) custom-call(s32[1]{0:T(128)} %bitcast.core, ...), custom_call_target="tpu_custom_call", output_to_operand_aliasing={{1}: (5, {}), {2}: (6, {}), {3}: (7, {}), {4}: (8, {})} | custom-call | tf_op jit(solution)/shard_map/pallas_call | solution.py:480
  59.3 19.9 %all_to_all.16 = f32[16,2,8,8,128]{4,3,2,1,0:T(8,128)S(1)} all-to-all(f32[16,2,8,8,128]{4,3,2,1,0:T(8,128)S(1)} %bitcast.15), channel_id=1, replica_groups=mesh['s'=8,'z'=4,'gy'=4] {'z','gy'}, dimensions={0} | all-to-all | bytes 2097152 | tf_op jit(solution)/shard_map/all_to_all | solution.py:489
  79.3 1.5 %shard_map.47 = f32[640,128]{1,0:T(8,128)S(1)} custom-call(f32[32,8,8,128]{3,2,1,0:T(8,128)S(1)} %bitcast.9), custom_call_target="tpu_custom_call" | custom-call | tf_op jit(solution)/shard_map/pallas_call | solution.py:492
  80.8 17.6 %all_to_all.17 = f32[128,1,640]{2,1,0:T(1,128)S(1)} all-to-all(f32[128,1,640]{2,1,0:T(1,128)S(1)} %bitcast.14), channel_id=1, replica_groups=mesh['s'=8,'z'=4,'gy'=4] {'gy','z','s'}, dimensions={0} | all-to-all | bytes 655360 | tf_op jit(solution)/shard_map/all_to_all | solution.py:495
  98.4 3.1 %shard_map.48 = (f32[2048,128]{1,0:T(8,128)}, f32[32,32]{1,0:T(8,128)}) custom-call(f32[640,128]{1,0:T(8,128)S(1)} %bitcast.13, f32[2048,128]{1,0:T(8,128)S(1)} %bitcast.10), custom_call_target="tpu_custom_call" | custom-call | tf_op jit(solution)/shard_map/pallas_call | solution.py:498
  (1 shorter events, 0.0 us)
Async XLA Ops:
  32.5 18.3 %collective-permute-start = (f32[21,8,8,128]{3,2,1,0:T(8,128)}, f32[21,8,8,128]{3,2,1,0:T(8,128)S(1)}, u32[]{:S(2)}, u32[]{:S(2)}) collective-permute-start(f32[21,8,8,128]{3,2,1,0:T(8,128)} %get-tuple-element.25), channel_id=1, source_target_pairs={{0,16},{16,32},{32,48},{48,64},{64,80},{80,96},{96,112},{112,0},{1... | collective-permute-start | bytes 2064392 | tf_op jit(solution)/shard_map/ppermute | solution.py:456
  33.7 17.1 %collective-permute-start.1 = (f32[21,8,8,128]{3,2,1,0:T(8,128)S(1)}, f32[21,8,8,128]{3,2,1,0:T(8,128)S(1)}, u32[]{:S(2)}, u32[]{:S(2)}) collective-permute-start(f32[21,8,8,128]{3,2,1,0:T(8,128)S(1)} %get-tuple-element.26), channel_id=1, source_target_pairs={{16,0},{32,16},{48,32},{64,48},{80,64},{96,80},{112,96},{0,112},{1... | collective-permute-start | bytes 2064392 | tf_op jit(solution)/shard_map/ppermute | solution.py:457
  36.0 3.0 %collective-permute-start.2 = (f32[8,8,8,128]{3,2,1,0:T(8,128)}, f32[8,8,8,128]{3,2,1,0:T(8,128)}, u32[]{:S(2)}, u32[]{:S(2)}) collective-permute-start(f32[8,8,8,128]{3,2,1,0:T(8,128)} %get-tuple-element.27.mid_pot), channel_id=1, source_target_pairs={{0,1},{1,0},{2,3},{3,2},{4,5},{5,4},{6,7},{7,6},{8,9},{9,8},{10,11... | collective-permute-start | bytes 786440 | tf_op jit(solution)/shard_map/ppermute | solution.py:458
  50.8 2.9 %collective-permute-start.3 = (f32[3,8,8,128]{3,2,1,0:T(8,128)S(1)}, f32[3,8,8,128]{3,2,1,0:T(8,128)S(1)}, u32[]{:S(2)}, u32[]{:S(2)}) collective-permute-start(f32[3,8,8,128]{3,2,1,0:T(8,128)S(1)} %get-tuple-element.35), channel_id=1, source_target_pairs={{0,1},{1,0},{2,3},{3,2},{4,5},{5,4},{6,7},{7,6},{8,9},{9,8},{10,11... | collective-permute-start | bytes 294920 | tf_op jit(solution)/shard_map/ppermute | solution.py:468
  52.7 1.3 %collective-permute-start.4 = (f32[3,8,8,128]{3,2,1,0:T(8,128)S(1)}, f32[3,8,8,128]{3,2,1,0:T(8,128)S(1)}, u32[]{:S(2)}, u32[]{:S(2)}) collective-permute-start(f32[3,8,8,128]{3,2,1,0:T(8,128)S(1)} %get-tuple-element.36), channel_id=1, source_target_pairs={{0,1},{1,0},{2,3},{3,2},{4,5},{5,4},{6,7},{7,6},{8,9},{9,8},{10,11... | collective-permute-start | bytes 294920 | tf_op jit(solution)/shard_map/ppermute | solution.py:469

commit v11 on v10

--- a/solution.py
+++ b/solution.py
@@ -323,7 +323,12 @@
         total = part if total is None else total + part
     total = jnp.where(same_y(n), total, 0.0) * scale
     ones = spread(n)
-    gram = dot(dot(ones, total, ((0,), (0,))), ones)
+    exact = ones.astype(jnp.bfloat16)
+    down = (((0,), (0,)), ((), ()))
+    tall = sum(
+        lax.dot_general(exact, p, down, preferred_element_type=jnp.float32) for p in parts_of(total)
+    )
+    gram = sum(jnp.dot(p, exact, preferred_element_type=jnp.float32) for p in parts_of(tall))
     gram = gram + gram.T
     half = n // 2
     upper = iota((half, half), 0) <= iota((half, half), 1)

time: 102 us -> 102 us (level)
  no operation moved by 1% of the time
where the time goes in v11:
time: 102 us; the launch traced here: 101 us
  blocking collectives  66.7 us (65%)
  Pallas kernels  16.6 us (16%)
  waiting for transfers between devices  10.2 us (10%)
  starting transfers between devices  7.18 us (7%)
    all_to_all x1, blocking collectives, per_device(): got = lax.all_to_all(sent, ('z', 'gy'), 0, 0, tiled=True)  29.2 us
    all_to_all x1, blocking collectives, per_device(): lax.all_to_all(filtered, ('z', 'gy'), 0, 0, tiled=True)  19.9 us
    all_to_all x1, blocking collectives, per_device(): lax.all_to_all(parts.reshape(devices, 1, 5 * 128), ('gy', 'z', 's'), 0, 0...  17.6 us
    ppermute x1, waiting for transfers between devices, per_device(): low = lax.ppermute(up, 's', ring)  8.12 us
    pallas_call x1, Pallas kernels, per_device(): call(outer_kernel, (f32(group * PAIR * BX * BX, 128),) + fields[1:] + (fi...  5.31 us
    pallas_call x1, Pallas kernels, per_device(): call(inner_kernel, fields + (f32(2 * REACH, BX, 8, 128),), [SMEM] + [VMEM...  3.53 us
    pallas_call x1, Pallas kernels, per_device(): call(finish_kernel, (f32(n * BX * BX, 128), f32(n, n)), [VMEM, VMEM])  3.09 us
    ppermute x1, starting transfers between devices, per_device(): high = lax.ppermute(down, 's', back_ring)  2.36 us
  transfers between devices with their start and end apart: 5, of which 4 were waited for; matrix products, arithmetic and copies ran while one was open for 0% of the time, Pallas kernels for 4%

profile of v11, /device:TPU:1, one launch (start us, length us, event | category | flops | bytes accessed | tf_op | source)
XLA Modules:
  0.0 101.3 jit_solution(12862557566140926919)
XLA Ops:
  0.6 1.2 %shard_map.41 = f32[16,2,10,8,128]{4,3,2,1,0:T(8,128)S(1)} custom-call(f32[16,2,8,8,128]{4,3,2,1,0:T(8,128)} %bitcast.16, f32[8,8,128]{2,1,0:T(8,128)} %potential.1), custom_call_target="tpu_custom_call" | custom-call | tf_op jit(solution)/shard_map/pallas_call | solution.py:444
  1.9 29.2 %all_to_all.15 = f32[16,2,10,8,128]{4,3,2,1,0:T(8,128)S(1)} all-to-all(f32[16,2,10,8,128]{4,3,2,1,0:T(8,128)S(1)} %shard_map.41), channel_id=1, replica_groups=mesh['s'=8,'z'=4,'gy'=4] {'z','gy'}, dimensions={0} | all-to-all | bytes 2621440 | tf_op jit(solution)/shard_map/all_to_all | solution.py:453
  31.1 1.4 %shard_map.42 = (f32[21,8,8,128]{3,2,1,0:T(8,128)}, f32[21,8,8,128]{3,2,1,0:T(8,128)S(1)}, f32[8,8,8,128]{3,2,1,0:T(8,128)}) custom-call(f32[2560,128]{1,0:T(8,128)S(1)} %bitcast.11), custom_call_target="tpu_custom_call" | custom-call | tf_op jit(solution)/shard_map/pallas_call | solution.py:455
  32.5 1.2 %collective-permute-start = (f32[21,8,8,128]{3,2,1,0:T(8,128)}, f32[21,8,8,128]{3,2,1,0:T(8,128)S(1)}, u32[]{:S(2)}, u32[]{:S(2)}) collective-permute-start(f32[21,8,8,128]{3,2,1,0:T(8,128)} %get-tuple-element.25), channel_id=1, source_target_pairs={{0,16},{16,32},{32,48},{48,64},{64,80},{80,96},{96,112},{112,0},{1... | collective-permute-start | bytes 2064392 | tf_op jit(solution)/shard_map/ppermute | solution.py:461
  33.7 2.4 %collective-permute-start.1 = (f32[21,8,8,128]{3,2,1,0:T(8,128)S(1)}, f32[21,8,8,128]{3,2,1,0:T(8,128)S(1)}, u32[]{:S(2)}, u32[]{:S(2)}) collective-permute-start(f32[21,8,8,128]{3,2,1,0:T(8,128)S(1)} %get-tuple-element.26), channel_id=1, source_target_pairs={{16,0},{32,16},{48,32},{64,48},{80,64},{96,80},{112,96},{0,112},{1... | collective-permute-start | bytes 2064392 | tf_op jit(solution)/shard_map/ppermute | solution.py:462
  36.0 1.5 %collective-permute-start.2 = (f32[8,8,8,128]{3,2,1,0:T(8,128)}, f32[8,8,8,128]{3,2,1,0:T(8,128)}, u32[]{:S(2)}, u32[]{:S(2)}) collective-permute-start(f32[8,8,8,128]{3,2,1,0:T(8,128)} %get-tuple-element.27.mid_pot), channel_id=1, source_target_pairs={{0,1},{1,0},{2,3},{3,2},{4,5},{5,4},{6,7},{7,6},{8,9},{9,8},{10,11... | collective-permute-start | bytes 786440 | tf_op jit(solution)/shard_map/ppermute | solution.py:463
  37.6 1.5 %collective-permute-done.2.far_mid = f32[8,8,8,128]{3,2,1,0:T(8,128)} collective-permute-done((f32[8,8,8,128]{3,2,1,0:T(8,128)}, f32[8,8,8,128]{3,2,1,0:T(8,128)}, u32[]{:S(2)}, u32[]{:S(2)}) %collective-permute-start.2) | collective-permute-done | bytes 262176 | tf_op jit(solution)/shard_map/ppermute | solution.py:463
  39.1 3.5 %shard_map.43 = (f32[68,8,16,128]{3,2,1,0:T(8,128)S(1)}, f32[56,8,16,128]{3,2,1,0:T(8,128)S(1)}, f32[44,8,16,128]{3,2,1,0:T(8,128)S(1)}, f32[56,8,8,128]{3,2,1,0:T(8,128)S(1)}, f32[12,8,8,128]{3,2,1,0:T(8,128)S(1)}) custom-call(s32[1]{0:T(128)} %bitcast.core, f32[2560,128]{1,0:T(8,128)S(1)} %bitcast.12, f32[8,8,8,128]{3,2,1,0:T(8,128)} %get-tuple-element.27.mid_pot, ...), custom_call_target="tpu_custom_call" | custom-call | flops 4294967296 | tf_op jit(solution)/shard_map/pallas_call | solution.py:468
  42.6 8.1 %collective-permute-done.low = f32[21,8,8,128]{3,2,1,0:T(8,128)S(1)} collective-permute-done((f32[21,8,8,128]{3,2,1,0:T(8,128)}, f32[21,8,8,128]{3,2,1,0:T(8,128)S(1)}, u32[]{:S(2)}, u32[]{:S(2)}) %collective-permute-start) | collective-permute-done | bytes 688160 | tf_op jit(solution)/shard_map/ppermute | solution.py:461
  50.7 0.0 collective-permute-done.1.high
  50.8 2.0 %collective-permute-start.3 = (f32[3,8,8,128]{3,2,1,0:T(8,128)S(1)}, f32[3,8,8,128]{3,2,1,0:T(8,128)S(1)}, u32[]{:S(2)}, u32[]{:S(2)}) collective-permute-start(f32[3,8,8,128]{3,2,1,0:T(8,128)S(1)} %get-tuple-element.35), channel_id=1, source_target_pairs={{0,1},{1,0},{2,3},{3,2},{4,5},{5,4},{6,7},{7,6},{8,9},{9,8},{10,11... | collective-permute-start | bytes 294920 | tf_op jit(solution)/shard_map/ppermute | solution.py:473
  52.7 0.1 collective-permute-start.4
  52.8 0.7 shard_map.45
  53.5 0.2 collective-permute-done.3.far_low
  53.7 0.4 collective-permute-done.4.far_high
  54.0 5.3 %shard_map.46 = (f32[2048,128]{1,0:T(8,128)S(1)}, f32[56,8,16,128]{3,2,1,0:T(8,128)S(1)}, f32[44,8,16,128]{3,2,1,0:T(8,128)S(1)}, f32[56,8,8,128]{3,2,1,0:T(8,128)S(1)}, f32[56,8,8,128]{3,2,1,0:T(8,128)S(1)}) custom-call(s32[1]{0:T(128)} %bitcast.core, ...), custom_call_target="tpu_custom_call", output_to_operand_aliasing={{1}: (5, {}), {2}: (6, {}), {3}: (7, {}), {4}: (8, {})} | custom-call | tf_op jit(solution)/shard_map/pallas_call | solution.py:485
  59.3 19.9 %all_to_all.16 = f32[16,2,8,8,128]{4,3,2,1,0:T(8,128)S(1)} all-to-all(f32[16,2,8,8,128]{4,3,2,1,0:T(8,128)S(1)} %bitcast.15), channel_id=1, replica_groups=mesh['s'=8,'z'=4,'gy'=4] {'z','gy'}, dimensions={0} | all-to-all | bytes 2097152 | tf_op jit(solution)/shard_map/all_to_all | solution.py:494
  79.3 1.3 %shard_map.47 = f32[640,128]{1,0:T(8,128)S(1)} custom-call(f32[32,8,8,128]{3,2,1,0:T(8,128)S(1)} %bitcast.9), custom_call_target="tpu_custom_call" | custom-call | tf_op jit(solution)/shard_map/pallas_call | solution.py:497
  80.6 17.6 %all_to_all.17 = f32[128,1,640]{2,1,0:T(1,128)S(1)} all-to-all(f32[128,1,640]{2,1,0:T(1,128)S(1)} %bitcast.14), channel_id=1, replica_groups=mesh['s'=8,'z'=4,'gy'=4] {'gy','z','s'}, dimensions={0} | all-to-all | bytes 655360 | tf_op jit(solution)/shard_map/all_to_all | solution.py:500
  98.2 3.1 %shard_map.48 = (f32[2048,128]{1,0:T(8,128)}, f32[32,32]{1,0:T(8,128)}) custom-call(f32[640,128]{1,0:T(8,128)S(1)} %bitcast.13, f32[2048,128]{1,0:T(8,128)S(1)} %bitcast.10), custom_call_target="tpu_custom_call" | custom-call | tf_op jit(solution)/shard_map/pallas_call | solution.py:503
  (1 shorter events, 0.0 us)
Async XLA Ops:
  32.5 18.3 %collective-permute-start = (f32[21,8,8,128]{3,2,1,0:T(8,128)}, f32[21,8,8,128]{3,2,1,0:T(8,128)S(1)}, u32[]{:S(2)}, u32[]{:S(2)}) collective-permute-start(f32[21,8,8,128]{3,2,1,0:T(8,128)} %get-tuple-element.25), channel_id=1, source_target_pairs={{0,16},{16,32},{32,48},{48,64},{64,80},{80,96},{96,112},{112,0},{1... | collective-permute-start | bytes 2064392 | tf_op jit(solution)/shard_map/ppermute | solution.py:461
  33.7 17.1 %collective-permute-start.1 = (f32[21,8,8,128]{3,2,1,0:T(8,128)S(1)}, f32[21,8,8,128]{3,2,1,0:T(8,128)S(1)}, u32[]{:S(2)}, u32[]{:S(2)}) collective-permute-start(f32[21,8,8,128]{3,2,1,0:T(8,128)S(1)} %get-tuple-element.26), channel_id=1, source_target_pairs={{16,0},{32,16},{48,32},{64,48},{80,64},{96,80},{112,96},{0,112},{1... | collective-permute-start | bytes 2064392 | tf_op jit(solution)/shard_map/ppermute | solution.py:462
  36.0 3.0 %collective-permute-start.2 = (f32[8,8,8,128]{3,2,1,0:T(8,128)}, f32[8,8,8,128]{3,2,1,0:T(8,128)}, u32[]{:S(2)}, u32[]{:S(2)}) collective-permute-start(f32[8,8,8,128]{3,2,1,0:T(8,128)} %get-tuple-element.27.mid_pot), channel_id=1, source_target_pairs={{0,1},{1,0},{2,3},{3,2},{4,5},{5,4},{6,7},{7,6},{8,9},{9,8},{10,11... | collective-permute-start | bytes 786440 | tf_op jit(solution)/shard_map/ppermute | solution.py:463
  50.8 2.9 %collective-permute-start.3 = (f32[3,8,8,128]{3,2,1,0:T(8,128)S(1)}, f32[3,8,8,128]{3,2,1,0:T(8,128)S(1)}, u32[]{:S(2)}, u32[]{:S(2)}) collective-permute-start(f32[3,8,8,128]{3,2,1,0:T(8,128)S(1)} %get-tuple-element.35), channel_id=1, source_target_pairs={{0,1},{1,0},{2,3},{3,2},{4,5},{5,4},{6,7},{7,6},{8,9},{9,8},{10,11... | collective-permute-start | bytes 294920 | tf_op jit(solution)/shard_map/ppermute | solution.py:473
  52.7 1.3 %collective-permute-start.4 = (f32[3,8,8,128]{3,2,1,0:T(8,128)S(1)}, f32[3,8,8,128]{3,2,1,0:T(8,128)S(1)}, u32[]{:S(2)}, u32[]{:S(2)}) collective-permute-start(f32[3,8,8,128]{3,2,1,0:T(8,128)S(1)} %get-tuple-element.36), channel_id=1, source_target_pairs={{0,1},{1,0},{2,3},{3,2},{4,5},{5,4},{6,7},{7,6},{8,9},{9,8},{10,11... | collective-permute-start | bytes 294920 | tf_op jit(solution)/shard_map/ppermute | solution.py:474
